TPU v7x, 512 devices: a whole 4x4x16 slice. The times are simulated.
512 devices in a mesh: pipe: 16 (over z_hi, y), expert: 32 (over z_lo, x, core).
Axes of the slice: x: 4, y: 4, z: 16 (z_hi: 4, z_lo: 4; z = z_hi * 4 + z_lo), core: 2. Of those that a mesh axis runs over, the one named last changes fastest.
Arguments:
- tokens: bfloat16 [16, 4096, 3584], P('pipe', 'expert'), may hold values from -6 to 6
- cotangent: bfloat16 [16, 4096, 3584], P('pipe', 'expert'), may hold values from -6 to 6
- routed: int32 [16, 4096, 2], P('pipe', 'expert'), may hold values from 0 to 1, as said below
- gate: float32 [16, 4096, 2], P('pipe', 'expert'), may hold values from 0.05 to 0.5
- up_weight: bfloat16 [3584, 4096], P(None, 'expert'), may hold values from -0.09375 to 0.09375
- down_weight: bfloat16 [4096, 3584], P('expert'), may hold values from -0.125 to 0.125
Outputs:
- up_grad: bfloat16 [16, 1792, 4096], P('pipe', None, 'expert')
- down_grad: bfloat16 [16, 4096, 1792], P('pipe', 'expert')
Inputs may be any that keep to these rules, and one draw needn't show every extreme that they name: In each micro-batch and token block of 128 tokens, at most 16 tokens are routed to each expert in flight; in each micro-batch one expert, drawn from the seed, gets exactly 16 tokens from every block, and every expert gets exactly 16 from at least one block. A token may be routed to several experts in flight or to none.
All inputs are finite; a program needn't handle non-finite values.
Results may differ from a plain program's by a relative error of at most 0.02.
Values may be sent and summed in bfloat16 or wider, within the bound.
No kernel may reach another device: no remote copies, remote signals or barrier semaphores. Data moves between devices by JAX's collectives and lax.ppermute only.
A program may use at most 64 MiB of HBM per device.

v0:
```python
import jax
import jax.numpy as jnp
from jax import lax
from jax.sharding import PartitionSpec as P

CAP = 16


def swapped(value, axis, stride):
    mask = 2**stride
    pairs = [(source, source ^ mask) for source in range(lax.axis_size(axis))]
    return lax.ppermute(value, axis, pairs)


def shards(tokens, cotangent, routed, gate, up_weight, down_weight):
    token_block = tokens[0]
    grad_block = cotangent[0]
    routing = routed[0]
    gating = gate[0]
    experts_count = routing.shape[1]
    width_full = token_block.shape[1]
    group_size = lax.axis_size("expert") // experts_count
    slot_index = jnp.cumsum(routing, axis=0) - 1
    slot_ids = jnp.arange(CAP, dtype=jnp.int32)
    chosen = (routing.T[:, None, :] == 1) & (slot_index.T[:, None, :] == slot_ids[None, :, None])
    picker_bf = jnp.where(chosen, 1.0, 0.0).astype(jnp.bfloat16)
    picker_fl = jnp.where(chosen, 1.0, 0.0).astype(jnp.float32)
    token_rows = jnp.einsum(
        "ect,td->ecd", picker_bf, token_block, preferred_element_type=jnp.float32
    ).astype(jnp.bfloat16)
    plain_rows = jnp.einsum(
        "ect,td->ecd", picker_bf, grad_block, preferred_element_type=jnp.float32
    )
    slot_gate = jnp.einsum("ect,te->ec", picker_fl, gating)
    grad_rows = (slot_gate[..., None] * plain_rows).astype(jnp.bfloat16)
    send_tokens = jnp.repeat(token_rows, group_size, axis=0)
    send_grads = jnp.repeat(grad_rows, group_size, axis=0)
    recv_tokens, recv_grads = (
        lax.all_to_all(send_tokens, "expert", split_axis=0, concat_axis=0, tiled=True),
        lax.all_to_all(send_grads, "expert", split_axis=0, concat_axis=0, tiled=True),
    )
    recv_tokens = recv_tokens.reshape(-1, width_full)
    recv_grads = recv_grads.reshape(-1, width_full)
    upper = jnp.dot(recv_tokens, up_weight, preferred_element_type=jnp.float32)
    hidden = jax.nn.silu(upper).astype(jnp.bfloat16)
    section_down = lax.dot_general(
        hidden, recv_grads, (((0,), (0,)), ((), ())), preferred_element_type=jnp.float32
    ).astype(jnp.bfloat16)
    hidden_grad = lax.dot_general(
        recv_grads, down_weight, (((1,), (1,)), ((), ())), preferred_element_type=jnp.float32
    )
    sigma = jax.nn.sigmoid(upper)
    act_grad = (hidden_grad * sigma * (1.0 + upper * (1.0 - sigma))).astype(jnp.bfloat16)
    section_up = lax.dot_general(
        recv_tokens, act_grad, (((0,), (0,)), ((), ())), preferred_element_type=jnp.float32
    ).astype(jnp.bfloat16)
    section_count = lax.axis_size("pipe")
    top_bit = section_count.bit_length() - 2
    upper_half = (lax.axis_index("pipe") >= section_count // 2).astype(jnp.int32)
    half_width = width_full // 2
    own_start = upper_half * half_width
    partner_up, partner_down = swapped((section_up, section_down), "pipe", top_bit)
    summed_up = section_up.astype(jnp.float32) + partner_up.astype(jnp.float32)
    summed_down = section_down.astype(jnp.float32) + partner_down.astype(jnp.float32)
    kept_up = lax.dynamic_slice_in_dim(summed_up, own_start, half_width, 0)
    kept_down = lax.dynamic_slice_in_dim(summed_down, own_start, half_width, 1)
    return (kept_up.astype(jnp.bfloat16)[None], kept_down.astype(jnp.bfloat16)[None])


def solution(mesh):
    in_specs = (
        P("pipe", "expert", None),
        P("pipe", "expert", None),
        P("pipe", "expert", None),
        P("pipe", "expert", None),
        P(None, "expert"),
        P("expert", None),
    )
    out_specs = (P("pipe", None, "expert"), P("pipe", "expert", None))
    return jax.shard_map(shards, mesh=mesh, in_specs=in_specs, out_specs=out_specs, check_vma=False)
```

profile of v0, /device:TPU:161, one launch (start us, length us, event | category | flops | bytes accessed | tf_op | source)
XLA Modules:
  0.0 367.5 jit_solution(17808655780842806257)
XLA Ops:
  0.6 0.0 copy-start
  0.6 0.8 compare_bitcast_fusion
  1.4 0.8 copy.8
  2.2 0.2 reduce_window_sum.11
  2.4 0.1 copy.9
  2.4 1.4 convolution_convert_fusion.2
  3.9 2.3 broadcast_in_dim.28
  6.1 0.0 copy-start.3
  6.1 0.0 copy-start.2
  6.1 9.1 %all-to-all-start = ((bf16[32,16,3584]{2,1,0:T(8,128)(2,1)}), bf16[32,16,3584]{2,1,0:T(8,128)(2,1)}, u32[]{:S(2)}, u32[]{:S(2)}) async-start(bf16[32,16,3584]{2,1,0:T(8,128)(2,1)} %bitcast.35), calls=%async_computation | async-start | bytes 7340032 | tf_op jit(solution)/shard_map/all_to_all | solution.py:39
  15.3 0.0 copy-done.3
  15.3 0.1 fusion.12
  15.4 0.0 copy-done.2
  15.4 0.3 fusion
  15.7 81.0 %all-to-all-done = bf16[32,16,3584]{2,1,0:T(8,128)(2,1)} async-done(((bf16[32,16,3584]{2,1,0:T(8,128)(2,1)}), bf16[32,16,3584]{2,1,0:T(8,128)(2,1)}, u32[]{:S(2)}, u32[]{:S(2)}) %all-to-all-start) | async-done | bytes 3670048 | tf_op jit(solution)/shard_map/all_to_all | solution.py:39
  96.6 2.3 broadcast_in_dim.29
  99.0 0.0 copy-start.1
  99.0 7.3 %all-to-all-start.1 = ((bf16[32,16,3584]{2,1,0:T(8,128)(2,1)}), bf16[32,16,3584]{2,1,0:T(8,128)(2,1)}, u32[]{:S(2)}, u32[]{:S(2)}) async-start(bf16[32,16,3584]{2,1,0:T(8,128)(2,1)} %bitcast.36), calls=%async_computation.1 | async-start | bytes 7340032 | tf_op jit(solution)/shard_map/all_to_all | solution.py:40
  106.3 0.0 copy-done.1
  106.3 3.1 fusion.36
  109.4 78.2 %all-to-all-done.1 = bf16[32,16,3584]{2,1,0:T(8,128)(2,1)} async-done(((bf16[32,16,3584]{2,1,0:T(8,128)(2,1)}), bf16[32,16,3584]{2,1,0:T(8,128)(2,1)}, u32[]{:S(2)}, u32[]{:S(2)}) %all-to-all-start.1) | async-done | bytes 3670048 | tf_op jit(solution)/shard_map/all_to_all | solution.py:40
  187.7 0.0 copy-done
  187.7 7.1 %convolution_convert_fusion.1 = bf16[3584,128]{1,0:T(8,128)(2,1)S(1)} fusion(bf16[512,3584]{1,0:T(8,128)(2,1)} %bitcast.6, bf16[512,3584]{1,0:T(8,128)(2,1)} %bitcast.15, bf16[128,3584]{1,0:T(8,128)(2,1)S(1)} %copy-done, f32[512,128]{1,0:T(8,128)S(1)} %fusion.36), kind=kOutput, calls=%fused_computation.1 | convolution fusion | flops 940572672 | bytes 9437184 | tf_op jit(solution)/shard_map/dot_general | solution.py:54
  194.8 7.9 %collective-permute-start = (bf16[3584,128]{1,0:T(8,128)(2,1)S(1)}, bf16[3584,128]{1,0:T(8,128)(2,1)}, u32[]{:S(2)}, u32[]{:S(2)}) collective-permute-start(bf16[3584,128]{1,0:T(8,128)(2,1)S(1)} %convolution_convert_fusion.1), channel_id=1, source_target_pairs={{0,256},{32,288},{64,320},{96,352},{128,384},{160,416},{192,448},{... | collective-permute-start | bytes 2752520 | tf_op jit(solution)/shard_map/ppermute | solution.py:12
  202.8 2.7 convolution_convert_fusion
  205.5 6.0 %collective-permute-start.1 = (bf16[128,3584]{1,0:T(8,128)(2,1)S(1)}, bf16[128,3584]{1,0:T(8,128)(2,1)}, u32[]{:S(2)}, u32[]{:S(2)}) collective-permute-start(bf16[128,3584]{1,0:T(8,128)(2,1)S(1)} %convolution_convert_fusion), channel_id=1, source_target_pairs={{0,256},{32,288},{64,320},{96,352},{128,384},{160,416},{192,448},{... | collective-permute-start | bytes 2752520 | tf_op jit(solution)/shard_map/ppermute | solution.py:12
  211.6 92.9 %collective-permute-done = bf16[3584,128]{1,0:T(8,128)(2,1)} collective-permute-done((bf16[3584,128]{1,0:T(8,128)(2,1)S(1)}, bf16[3584,128]{1,0:T(8,128)(2,1)}, u32[]{:S(2)}, u32[]{:S(2)}) %collective-permute-start) | collective-permute-done | bytes 917536 | tf_op jit(solution)/shard_map/ppermute | solution.py:12
  304.4 1.9 fusion.5
  306.3 59.2 %collective-permute-done.1 = bf16[128,3584]{1,0:T(8,128)(2,1)} collective-permute-done((bf16[128,3584]{1,0:T(8,128)(2,1)S(1)}, bf16[128,3584]{1,0:T(8,128)(2,1)}, u32[]{:S(2)}, u32[]{:S(2)}) %collective-permute-start.1) | collective-permute-done | bytes 917536 | tf_op jit(solution)/shard_map/ppermute | solution.py:12
  365.6 1.9 fusion.6
  (1 shorter events, 0.0 us)
Async XLA Ops:
  0.6 187.0 %copy-start = (bf16[128,3584]{1,0:T(8,128)(2,1)S(1)}, bf16[128,3584]{1,0:T(8,128)(2,1)}, u32[]{:S(2)}) copy-start(bf16[128,3584]{1,0:T(8,128)(2,1)} %param.11) | copy-start | bytes 2752516
  6.1 9.1 %copy-start.3 = (f32[1,128,2]{1,2,0:T(2,128)S(1)}, f32[1,128,2]{1,2,0:T(2,128)}, u32[]{:S(2)}) copy-start(f32[1,128,2]{1,2,0:T(2,128)} %param.9) | copy-start | bytes 3076
  6.1 9.3 %copy-start.2 = (bf16[1,128,3584]{2,1,0:T(8,128)(2,1)S(1)}, bf16[1,128,3584]{2,1,0:T(8,128)(2,1)}, u32[]{:S(2)}) copy-start(bf16[1,128,3584]{2,1,0:T(8,128)(2,1)} %param.7) | copy-start | bytes 2752516
  6.1 90.5 %all-to-all-start = ((bf16[32,16,3584]{2,1,0:T(8,128)(2,1)}), bf16[32,16,3584]{2,1,0:T(8,128)(2,1)}, u32[]{:S(2)}, u32[]{:S(2)}) async-start(bf16[32,16,3584]{2,1,0:T(8,128)(2,1)} %bitcast.35), calls=%async_computation | async-start | bytes 7340032 | tf_op jit(solution)/shard_map/all_to_all | solution.py:39
  99.0 7.3 %copy-start.1 = (bf16[3584,128]{1,0:T(8,128)(2,1)S(1)}, bf16[3584,128]{1,0:T(8,128)(2,1)}, u32[]{:S(2)}) copy-start(bf16[3584,128]{1,0:T(8,128)(2,1)} %param.10) | copy-start | bytes 2752516
  99.0 88.7 %all-to-all-start.1 = ((bf16[32,16,3584]{2,1,0:T(8,128)(2,1)}), bf16[32,16,3584]{2,1,0:T(8,128)(2,1)}, u32[]{:S(2)}, u32[]{:S(2)}) async-start(bf16[32,16,3584]{2,1,0:T(8,128)(2,1)} %bitcast.36), calls=%async_computation.1 | async-start | bytes 7340032 | tf_op jit(solution)/shard_map/all_to_all | solution.py:40
  194.8 109.6 %collective-permute-start = (bf16[3584,128]{1,0:T(8,128)(2,1)S(1)}, bf16[3584,128]{1,0:T(8,128)(2,1)}, u32[]{:S(2)}, u32[]{:S(2)}) collective-permute-start(bf16[3584,128]{1,0:T(8,128)(2,1)S(1)} %convolution_convert_fusion.1), channel_id=1, source_target_pairs={{0,256},{32,288},{64,320},{96,352},{128,384},{160,416},{192,448},{... | collective-permute-start | bytes 2752520 | tf_op jit(solution)/shard_map/ppermute | solution.py:12
  205.5 160.1 %collective-permute-start.1 = (bf16[128,3584]{1,0:T(8,128)(2,1)S(1)}, bf16[128,3584]{1,0:T(8,128)(2,1)}, u32[]{:S(2)}, u32[]{:S(2)}) collective-permute-start(bf16[128,3584]{1,0:T(8,128)(2,1)S(1)} %convolution_convert_fusion), channel_id=1, source_target_pairs={{0,256},{32,288},{64,320},{96,352},{128,384},{160,416},{192,448},{... | collective-permute-start | bytes 2752520 | tf_op jit(solution)/shard_map/ppermute | solution.py:12
where the time goes:
time: 368 us; the launch traced here: 367 us
  waiting for transfers between devices  311 us (85%)
  starting transfers between devices  30.4 us (8%)
  matrix products  14.9 us (4%)
  local copies, waits for them, and re-layouts  5.45 us (1%)
  other arithmetic  4.74 us (1%)
    ppermute x2, waiting for transfers between devices, swapped(): return lax.ppermute(value, axis, pairs)  152 us
    all_to_all x1, waiting for transfers between devices, shards(): lax.all_to_all(send_tokens, 'expert', split_axis=0, concat_axis=0, tiled=...  81 us
    all_to_all x1, waiting for transfers between devices, shards(): lax.all_to_all(send_grads, 'expert', split_axis=0, concat_axis=0, tiled=T...  78.2 us
    ppermute x2, starting transfers between devices, swapped(): return lax.ppermute(value, axis, pairs)  14 us
    all_to_all x1, starting transfers between devices, shards(): lax.all_to_all(send_tokens, 'expert', split_axis=0, concat_axis=0, tiled=...  9.12 us
  transfers between devices with their start and end apart: 4, of which 4 were waited for; matrix products, arithmetic and copies ran while one was open for 2% of the time, Pallas kernels for 0%

commit v1 on v0

v1 whole, which is shorter than its diff:
```python
import jax
import jax.numpy as jnp
from jax import lax
from jax.experimental import pallas as pl
from jax.experimental.pallas import tpu as pltpu
from jax.sharding import PartitionSpec as P

CAP = 16
BF = jnp.bfloat16
FL = jnp.float32


def pick_rows(side_ref, tok_ref, cot_ref, routed_ref, gate_ref, own_t, other_t, own_g, other_g):
    side = side_ref[0]
    tokens = tok_ref.shape[0]
    routed = routed_ref[...]
    row_id = lax.broadcasted_iota(jnp.int32, (tokens, tokens), 0)
    col_id = lax.broadcasted_iota(jnp.int32, (tokens, tokens), 1)
    upper = jnp.where(row_id <= col_id, 1.0, 0.0).astype(BF)
    count = jnp.dot(routed.astype(FL).astype(BF), upper, preferred_element_type=FL)
    slot = count.astype(jnp.int32) - 1
    slot_ids = lax.broadcasted_iota(jnp.int32, (CAP, tokens), 0)

    def chosen(e):
        return (routed[e : e + 1] == 1) & (slot[e : e + 1] == slot_ids)

    first, second = chosen(0), chosen(1)
    gates = gate_ref[...]
    lean = jnp.full((CAP, tokens), side, jnp.int32) == 0
    one = jnp.where(first, 1.0, 0.0)
    two = jnp.where(second, 1.0, 0.0)
    mine = jnp.where(lean, one, two)
    rest = jnp.where(lean, two, one)
    gate_one = jnp.where(first, gates[0:1], 0.0)
    gate_two = jnp.where(second, gates[1:2], 0.0)
    gate_mine = jnp.sum(jnp.where(lean, gate_one, gate_two), axis=1, keepdims=True)
    gate_rest = jnp.sum(jnp.where(lean, gate_two, gate_one), axis=1, keepdims=True)
    picker = jnp.concatenate([mine, rest], axis=0).astype(BF)
    scale = jnp.concatenate([gate_mine, gate_rest], axis=0)
    rows = jnp.dot(picker, tok_ref[...], preferred_element_type=FL).astype(BF)
    own_t[...] = rows[:CAP]
    other_t[...] = rows[CAP:]
    grads = (jnp.dot(picker, cot_ref[...], preferred_element_type=FL) * scale).astype(BF)
    own_g[...] = grads[:CAP]
    other_g[...] = grads[CAP:]


def picked(side, tokens, cotangent, routed, gate):
    vmem = pl.BlockSpec(memory_space=pltpu.VMEM)
    out = jax.ShapeDtypeStruct((CAP, tokens.shape[1]), BF)
    return pl.pallas_call(
        pick_rows,
        in_specs=[pl.BlockSpec(memory_space=pltpu.SMEM), vmem, vmem, vmem, vmem],
        out_specs=(vmem,) * 4,
        out_shape=(out,) * 4,
    )(side[None], tokens, cotangent, routed, gate)


def shards(tokens, cotangent, routed, gate, up_weight, down_weight):
    members = lax.axis_size("expert")
    sections = lax.axis_size("pipe")
    width = tokens.shape[2]
    half = width // 2
    hid = up_weight.shape[1]

    def across(value, z_mask=0, x_mask=0, core_mask=0):
        flip = z_mask * 8 + x_mask * 2 + core_mask
        return lax.ppermute(value, "expert", [(s, s ^ flip) for s in range(members)])

    def mirrored(value):
        return lax.ppermute(value, "pipe", [(q, q ^ (sections // 2)) for q in range(sections)])

    member = lax.axis_index("expert")
    side = (member >= members // 2).astype(jnp.int32)
    upper = (lax.axis_index("pipe") >= sections // 2).astype(jnp.int32)
    own_start = upper * half
    sent_start = (1 - upper) * half

    def columns(value, start):
        return lax.dynamic_slice_in_dim(value, start, half, 1)

    own_t, other_t, own_g, other_g = picked(side, tokens[0], cotangent[0], routed[0].T, gate[0].T)

    far_t = across(other_t, z_mask=2)
    far_g = across(other_g, z_mask=2)
    near_t = jnp.concatenate([own_t, far_t], axis=0)
    near_g = jnp.concatenate([own_g, far_g], axis=0)
    pair_t = across(near_t, z_mask=1)
    pair_g = across(near_g, z_mask=1)

    other_up = across(up_weight, core_mask=1)
    other_down = across(down_weight, core_mask=1)
    wide_up = jnp.concatenate([up_weight, other_up], axis=1)
    wide_down = jnp.concatenate([down_weight, other_down], axis=0)

    def around(block):
        n = block.shape[0] // 2
        one = across(block, x_mask=1)
        three = across(block, x_mask=3)
        two_a = across(one[:n], x_mask=3)
        two_b = across(three[n:], x_mask=1)
        return one, three, two_a, two_b

    block_t = jnp.concatenate([near_t, pair_t], axis=0)
    block_g = jnp.concatenate([near_g, pair_g], axis=0)
    rows_t = jnp.concatenate([block_t, *around(block_t)], axis=0)
    rows_g = jnp.concatenate([block_g, *around(block_g)], axis=0)

    sent = jnp.concatenate([columns(near_t, sent_start), columns(near_g, sent_start)], axis=0)
    mirror_near = mirrored(sent)
    mirror_pair = across(mirror_near, z_mask=1)
    mirror_block = jnp.concatenate([mirror_near, mirror_pair], axis=0)
    m_one, m_three, m_two_a, m_two_b = around(mirror_block)
    n = CAP * 2
    m_t = jnp.concatenate(
        [part[k : k + n] for part in (mirror_block, m_one, m_three) for k in (0, 2 * n)] + [m_two_a[:n], m_two_b[:n]],
        axis=0,
    )
    m_g = jnp.concatenate(
        [part[k : k + n] for part in (mirror_block, m_one, m_three) for k in (n, 3 * n)] + [m_two_a[n:], m_two_b[n:]],
        axis=0,
    )

    up = jnp.dot(rows_t, wide_up, preferred_element_type=FL)
    sigma = jax.nn.sigmoid(up)
    hidden = (up * sigma).astype(BF)
    m_hidden = mirrored(hidden)
    hidden_grad = lax.dot_general(rows_g, wide_down, (((1,), (1,)), ((), ())), preferred_element_type=FL)
    act_grad = (hidden_grad * sigma * (1.0 + up * (1.0 - sigma))).astype(BF)
    m_act = mirrored(act_grad)

    all_hidden = jnp.concatenate([hidden, m_hidden], axis=0)
    all_act = jnp.concatenate([act_grad, m_act], axis=0)
    all_t = jnp.concatenate([columns(rows_t, own_start), m_t], axis=0)
    all_g = jnp.concatenate([columns(rows_g, own_start), m_g], axis=0)
    down = lax.dot_general(all_hidden, all_g, (((0,), (0,)), ((), ())), preferred_element_type=FL)
    down_in = across(down[hid:].astype(BF), core_mask=1)
    raise_ = lax.dot_general(all_t, all_act, (((0,), (0,)), ((), ())), preferred_element_type=FL)
    up_in = across(raise_[:, hid:].astype(BF), core_mask=1)
    down_out = (down[:hid] + down_in.astype(FL)).astype(BF)
    up_out = (raise_[:, :hid] + up_in.astype(FL)).astype(BF)
    return up_out[None], down_out[None]


def solution(mesh):
    in_specs = (
        P("pipe", "expert", None),
        P("pipe", "expert", None),
        P("pipe", "expert", None),
        P("pipe", "expert", None),
        P(None, "expert"),
        P("expert", None),
    )
    out_specs = (P("pipe", None, "expert"), P("pipe", "expert", None))
    return jax.shard_map(shards, mesh=mesh, in_specs=in_specs, out_specs=out_specs, check_vma=False)
```

time: 368 us -> 171 us (0.46)
  the two profiles are of different devices: /device:TPU:161 before, /device:TPU:1 now
where the time goes in v1:
time: 171 us; the launch traced here: 169 us
  starting transfers between devices  98.5 us (58%)
  waiting for transfers between devices  55.1 us (32%)
  matrix products  5.61 us (3%)
  local copies, waits for them, and re-layouts  3.84 us (2%)
  Pallas kernels  2.64 us (2%)
  other arithmetic  1.73 us (1%)
    ppermute x21, starting transfers between devices, across(): lax.ppermute(value, 'expert', [(s, s ^ flip) for s in range(members)])  76.6 us
    ppermute x3, waiting for transfers between devices, mirrored(): lax.ppermute(value, 'pipe', [(q, q ^ sections // 2) for q in range(sectio...  30 us
    ppermute x21, waiting for transfers between devices, across(): lax.ppermute(value, 'expert', [(s, s ^ flip) for s in range(members)])  25.1 us
    ppermute x3, starting transfers between devices, mirrored(): lax.ppermute(value, 'pipe', [(q, q ^ sections // 2) for q in range(sectio...  21.9 us
  transfers between devices with their start and end apart: 24, of which 8 were waited for; matrix products, arithmetic and copies ran while one was open for 6% of the time, Pallas kernels for 0%

profile of v1, /device:TPU:1, one launch (start us, length us, event | category | flops | bytes accessed | tf_op | source)
XLA Modules:
  0.0 168.7 jit_solution(15260319644481233023)
XLA Ops:
  0.6 2.6 %shard_map.77 = (bf16[16,3584]{1,0:T(8,128)(2,1)}, bf16[16,3584]{1,0:T(8,128)(2,1)}, bf16[16,3584]{1,0:T(8,128)(2,1)}, bf16[16,3584]{1,0:T(8,128)(2,1)}) custom-call(s32[1]{0:T(128)} %bitcast.side_ref, bf16[128,3584]{1,0:T(8,128)(2,1)} %bitcast.17, bf16[128,3584]{1,0:T(8,128)(2,1)} %bitcast.18, s32[2,128]{1,0:T(2,128)} %bitcast.19, f32[2,128]{1,0:T(2,128)} %bitcast.20), custom_call_target="tpu_custom_call" | custom-call | tf_op jit(solution)/shard_map/pallas_call | solution.py:51
  3.3 5.7 %collective-permute-start = (bf16[16,3584]{1,0:T(8,128)(2,1)}, bf16[16,3584]{1,0:T(8,128)(2,1)S(1)}, u32[]{:S(2)}, u32[]{:S(2)}) collective-permute-start(bf16[16,3584]{1,0:T(8,128)(2,1)} %get-tuple-element.7), channel_id=1, source_target_pairs={{0,16},{1,17},{2,18},{3,19},{4,20},{5,21},{6,22},{7,23},{8,24},{9,... | collective-permute-start | bytes 344072 | tf_op jit(solution)/shard_map/ppermute | solution.py:68
  9.0 1.9 %collective-permute-start.6 = (bf16[16,3584]{1,0:T(8,128)(2,1)}, bf16[16,3584]{1,0:T(8,128)(2,1)S(1)}, u32[]{:S(2)}, u32[]{:S(2)}) collective-permute-start(bf16[16,3584]{1,0:T(8,128)(2,1)} %get-tuple-element.9), channel_id=1, source_target_pairs={{0,16},{1,17},{2,18},{3,19},{4,20},{5,21},{6,22},{7,23},{8,24},{9,... | collective-permute-start | bytes 344072 | tf_op jit(solution)/shard_map/ppermute | solution.py:68
  10.9 7.9 %collective-permute-start.19 = (bf16[3584,128]{1,0:T(8,128)(2,1)}, bf16[3584,128]{1,0:T(8,128)(2,1)}, u32[]{:S(2)}, u32[]{:S(2)}) collective-permute-start(bf16[3584,128]{1,0:T(8,128)(2,1)} %param.10), channel_id=1, source_target_pairs={{0,1},{1,0},{2,3},{3,2},{4,5},{5,4},{6,7},{7,6},{8,9},{9,8},{10,11... | collective-permute-start | bytes 2752520 | tf_op jit(solution)/shard_map/ppermute | solution.py:68
  18.8 1.9 %collective-permute-start.18 = (bf16[128,3584]{1,0:T(8,128)(2,1)}, bf16[128,3584]{1,0:T(8,128)(2,1)}, u32[]{:S(2)}, u32[]{:S(2)}) collective-permute-start(bf16[128,3584]{1,0:T(8,128)(2,1)} %param.11), channel_id=1, source_target_pairs={{0,1},{1,0},{2,3},{3,2},{4,5},{5,4},{6,7},{7,6},{8,9},{9,8},{10,11... | collective-permute-start | bytes 2752520 | tf_op jit(solution)/shard_map/ppermute | solution.py:68
  25.1 3.4 %collective-permute-start.13 = (bf16[32,3584]{1,0:T(8,128)(2,1)S(1)}, bf16[32,3584]{1,0:T(8,128)(2,1)S(1)}, u32[]{:S(2)}, u32[]{:S(2)}) collective-permute-start(bf16[32,3584]{1,0:T(8,128)(2,1)S(1)} %get-tuple-element.32), channel_id=1, source_target_pairs={{0,8},{1,9},{2,10},{3,11},{4,12},{5,13},{6,14},{7,15},{8,0},{9,1},... | collective-permute-start | bytes 688136 | tf_op jit(solution)/shard_map/ppermute | solution.py:68
  28.5 10.1 %collective-permute-start.7 = (bf16[64,1792]{1,0:T(8,128)(2,1)S(1)}, bf16[64,1792]{1,0:T(8,128)(2,1)S(1)}, u32[]{:S(2)}, u32[]{:S(2)}) collective-permute-start(bf16[64,1792]{1,0:T(8,128)(2,1)S(1)} %pad_maximum_fusion), channel_id=1, source_target_pairs={{0,256},{32,288},{64,320},{96,352},{128,384},{160,416},{192,448},{... | collective-permute-start | bytes 688136 | tf_op jit(solution)/shard_map/ppermute | solution.py:71
  39.3 4.5 %collective-permute-start.3 = (bf16[64,3584]{1,0:T(8,128)(2,1)S(1)}, bf16[64,3584]{1,0:T(8,128)(2,1)S(1)}, u32[]{:S(2)}, u32[]{:S(2)}) collective-permute-start(bf16[64,3584]{1,0:T(8,128)(2,1)S(1)} %get-tuple-element.28), channel_id=1, source_target_pairs={{0,6},{1,7},{2,4},{3,5},{4,2},{5,3},{6,0},{7,1},{8,14},{9,15},{10,... | collective-permute-start | bytes 1376264 | tf_op jit(solution)/shard_map/ppermute | solution.py:68
  43.8 17.1 %collective-permute-done.7 = bf16[64,1792]{1,0:T(8,128)(2,1)S(1)} collective-permute-done((bf16[64,1792]{1,0:T(8,128)(2,1)S(1)}, bf16[64,1792]{1,0:T(8,128)(2,1)S(1)}, u32[]{:S(2)}, u32[]{:S(2)}) %collective-permute-start.7) | collective-permute-done | bytes 229408 | tf_op jit(solution)/shard_map/ppermute | solution.py:71
  60.9 3.1 %collective-permute-start.2 = (bf16[64,3584]{1,0:T(8,128)(2,1)S(1)}, bf16[64,3584]{1,0:T(8,128)(2,1)S(1)}, u32[]{:S(2)}, u32[]{:S(2)}) collective-permute-start(bf16[64,3584]{1,0:T(8,128)(2,1)S(1)} %get-tuple-element.28), channel_id=1, source_target_pairs={{0,2},{1,3},{2,0},{3,1},{4,6},{5,7},{6,4},{7,5},{8,10},{9,11},{10,... | collective-permute-start | bytes 1376264 | tf_op jit(solution)/shard_map/ppermute | solution.py:68
  64.0 1.9 %collective-permute-start.8 = (bf16[64,1792]{1,0:T(8,128)(2,1)S(1)}, bf16[64,1792]{1,0:T(8,128)(2,1)S(1)}, u32[]{:S(2)}, u32[]{:S(2)}) collective-permute-start(bf16[64,1792]{1,0:T(8,128)(2,1)S(1)} %collective-permute-done.7), channel_id=1, source_target_pairs={{0,8},{1,9},{2,10},{3,11},{4,12},{5,13},{6,14},{7,15},{8,0},{9,1},... | collective-permute-start | bytes 688136 | tf_op jit(solution)/shard_map/ppermute | solution.py:68
  66.0 5.1 %collective-permute-done.8 = bf16[64,1792]{1,0:T(8,128)(2,1)S(1)} collective-permute-done((bf16[64,1792]{1,0:T(8,128)(2,1)S(1)}, bf16[64,1792]{1,0:T(8,128)(2,1)S(1)}, u32[]{:S(2)}, u32[]{:S(2)}) %collective-permute-start.8) | collective-permute-done | bytes 229408 | tf_op jit(solution)/shard_map/ppermute | solution.py:68
  71.1 3.7 %collective-permute-start.15 = (bf16[64,3584]{1,0:T(8,128)(2,1)S(1)}, bf16[64,3584]{1,0:T(8,128)(2,1)S(1)}, u32[]{:S(2)}, u32[]{:S(2)}) collective-permute-start(bf16[64,3584]{1,0:T(8,128)(2,1)S(1)} %get-tuple-element.26), channel_id=1, source_target_pairs={{0,6},{1,7},{2,4},{3,5},{4,2},{5,3},{6,0},{7,1},{8,14},{9,15},{10,... | collective-permute-start | bytes 1376264 | tf_op jit(solution)/shard_map/ppermute | solution.py:68
  74.8 2.2 %collective-permute-start.14 = (bf16[64,3584]{1,0:T(8,128)(2,1)S(1)}, bf16[64,3584]{1,0:T(8,128)(2,1)S(1)}, u32[]{:S(2)}, u32[]{:S(2)}) collective-permute-start(bf16[64,3584]{1,0:T(8,128)(2,1)S(1)} %get-tuple-element.26), channel_id=1, source_target_pairs={{0,2},{1,3},{2,0},{3,1},{4,6},{5,7},{6,4},{7,5},{8,10},{9,11},{10,... | collective-permute-start | bytes 1376264 | tf_op jit(solution)/shard_map/ppermute | solution.py:68
  77.2 3.2 %collective-permute-start.10 = (bf16[128,1792]{1,0:T(8,128)(2,1)S(1)}, bf16[128,1792]{1,0:T(8,128)(2,1)S(1)}, u32[]{:S(2)}, u32[]{:S(2)}) collective-permute-start(bf16[128,1792]{1,0:T(8,128)(2,1)S(1)} %constant_dynamic-update-slice_fusion.14), channel_id=1, source_target_pairs={{0,6},{1,7},{2,4},{3,5},{4,2},{5,3},{6,0},{7,1},{8,14},{9,15},{10,... | collective-permute-start | bytes 1376264 | tf_op jit(solution)/shard_map/ppermute | solution.py:68
  80.4 4.0 %collective-permute-done.14 = bf16[64,3584]{1,0:T(8,128)(2,1)S(1)} collective-permute-done((bf16[64,3584]{1,0:T(8,128)(2,1)S(1)}, bf16[64,3584]{1,0:T(8,128)(2,1)S(1)}, u32[]{:S(2)}, u32[]{:S(2)}) %collective-permute-start.14) | collective-permute-done | bytes 458784 | tf_op jit(solution)/shard_map/ppermute | solution.py:68
  84.4 2.2 %collective-permute-start.9 = (bf16[128,1792]{1,0:T(8,128)(2,1)S(1)}, bf16[128,1792]{1,0:T(8,128)(2,1)S(1)}, u32[]{:S(2)}, u32[]{:S(2)}) collective-permute-start(bf16[128,1792]{1,0:T(8,128)(2,1)S(1)} %constant_dynamic-update-slice_fusion.14), channel_id=1, source_target_pairs={{0,2},{1,3},{2,0},{3,1},{4,6},{5,7},{6,4},{7,5},{8,10},{9,11},{10,... | collective-permute-start | bytes 1376264 | tf_op jit(solution)/shard_map/ppermute | solution.py:68
  86.6 4.0 %collective-permute-start.4 = (bf16[32,3584]{1,0:T(8,128)(2,1)S(1)}, bf16[32,3584]{1,0:T(8,128)(2,1)S(1)}, u32[]{:S(2)}, u32[]{:S(2)}) collective-permute-start(bf16[32,3584]{1,0:T(8,128)(2,1)S(1)} %slice.106), channel_id=1, source_target_pairs={{0,6},{1,7},{2,4},{3,5},{4,2},{5,3},{6,0},{7,1},{8,14},{9,15},{10,... | collective-permute-start | bytes 688136 | tf_op jit(solution)/shard_map/ppermute | solution.py:68
  90.8 7.0 %collective-permute-done.4 = bf16[32,3584]{1,0:T(8,128)(2,1)S(1)} collective-permute-done((bf16[32,3584]{1,0:T(8,128)(2,1)S(1)}, bf16[32,3584]{1,0:T(8,128)(2,1)S(1)}, u32[]{:S(2)}, u32[]{:S(2)}) %collective-permute-start.4) | collective-permute-done | bytes 229408 | tf_op jit(solution)/shard_map/ppermute | solution.py:68
  97.8 1.9 %collective-permute-start.5 = (bf16[32,3584]{1,0:T(8,128)(2,1)S(1)}, bf16[32,3584]{1,0:T(8,128)(2,1)S(1)}, u32[]{:S(2)}, u32[]{:S(2)}) collective-permute-start(bf16[32,3584]{1,0:T(8,128)(2,1)S(1)} %slice.107), channel_id=1, source_target_pairs={{0,2},{1,3},{2,0},{3,1},{4,6},{5,7},{6,4},{7,5},{8,10},{9,11},{10,... | collective-permute-start | bytes 688136 | tf_op jit(solution)/shard_map/ppermute | solution.py:68
  99.7 4.8 %collective-permute-done.5 = bf16[32,3584]{1,0:T(8,128)(2,1)S(1)} collective-permute-done((bf16[32,3584]{1,0:T(8,128)(2,1)S(1)}, bf16[32,3584]{1,0:T(8,128)(2,1)S(1)}, u32[]{:S(2)}, u32[]{:S(2)}) %collective-permute-start.5) | collective-permute-done | bytes 229408 | tf_op jit(solution)/shard_map/ppermute | solution.py:68
  106.5 3.7 %collective-permute-start.16 = (bf16[32,3584]{1,0:T(8,128)(2,1)S(1)}, bf16[32,3584]{1,0:T(8,128)(2,1)S(1)}, u32[]{:S(2)}, u32[]{:S(2)}) collective-permute-start(bf16[32,3584]{1,0:T(8,128)(2,1)S(1)} %slice.118), channel_id=1, source_target_pairs={{0,6},{1,7},{2,4},{3,5},{4,2},{5,3},{6,0},{7,1},{8,14},{9,15},{10,... | collective-permute-start | bytes 688136 | tf_op jit(solution)/shard_map/ppermute | solution.py:68
  110.2 2.1 %multiply_convert_fusion = (bf16[256,256]{1,0:T(8,128)(2,1)S(1)}, f32[256,256]{1,0:T(8,128)S(1)}) fusion(bf16[256,3584]{1,0:T(8,128)(2,1)S(1)} %constant_dynamic-update-slice_fusion.5, bf16[3584,128]{1,0:T(8,128)(2,1)} %collective-permute-done.19, bf16[3584,128]{1,0:T(8,128)(2,1)} %param.10), kind=kOutput, calls=%fused_computation.29 | convolution fusion | flops 473759744 | bytes 4063232 | tf_op jit(solution)/shard_map/dot_general | solution.py:124
  112.3 5.4 %collective-permute-start.22 = (bf16[256,256]{1,0:T(8,128)(2,1)S(1)}, bf16[256,256]{1,0:T(8,128)(2,1)S(1)}, u32[]{:S(2)}, u32[]{:S(2)}) collective-permute-start(bf16[256,256]{1,0:T(8,128)(2,1)S(1)} %get-tuple-element.42), channel_id=1, source_target_pairs={{0,256},{32,288},{64,320},{96,352},{128,384},{160,416},{192,448},{... | collective-permute-start | bytes 393224 | tf_op jit(solution)/shard_map/ppermute | solution.py:71
  117.8 2.6 %collective-permute-start.12 = (bf16[64,1792]{1,0:T(8,128)(2,1)S(1)}, bf16[64,1792]{1,0:T(8,128)(2,1)S(1)}, u32[]{:S(2)}, u32[]{:S(2)}) collective-permute-start(bf16[64,1792]{1,0:T(8,128)(2,1)S(1)} %slice.116), channel_id=1, source_target_pairs={{0,2},{1,3},{2,0},{3,1},{4,6},{5,7},{6,4},{7,5},{8,10},{9,11},{10,... | collective-permute-start | bytes 688136 | tf_op jit(solution)/shard_map/ppermute | solution.py:68
  120.4 4.0 %collective-permute-start.11 = (bf16[64,1792]{1,0:T(8,128)(2,1)S(1)}, bf16[64,1792]{1,0:T(8,128)(2,1)S(1)}, u32[]{:S(2)}, u32[]{:S(2)}) collective-permute-start(bf16[64,1792]{1,0:T(8,128)(2,1)S(1)} %slice.114), channel_id=1, source_target_pairs={{0,6},{1,7},{2,4},{3,5},{4,2},{5,3},{6,0},{7,1},{8,14},{9,15},{10,... | collective-permute-start | bytes 688136 | tf_op jit(solution)/shard_map/ppermute | solution.py:68
  124.7 3.6 %collective-permute-done.11 = bf16[64,1792]{1,0:T(8,128)(2,1)S(1)} collective-permute-done((bf16[64,1792]{1,0:T(8,128)(2,1)S(1)}, bf16[64,1792]{1,0:T(8,128)(2,1)S(1)}, u32[]{:S(2)}, u32[]{:S(2)}) %collective-permute-start.11) | collective-permute-done | bytes 229408 | tf_op jit(solution)/shard_map/ppermute | solution.py:68
  129.2 12.6 %collective-permute-start.23 = (bf16[128,1792]{1,0:T(8,128)(2,1)S(1)}, bf16[128,1792]{1,0:T(8,128)(2,1)S(1)}, u32[]{:S(2)}, u32[]{:S(2)}) collective-permute-start(bf16[128,1792]{1,0:T(8,128)(2,1)S(1)} %slice.160), channel_id=1, source_target_pairs={{0,1},{1,0},{2,3},{3,2},{4,5},{5,4},{6,7},{7,6},{8,9},{9,8},{10,11... | collective-permute-start | bytes 1376264 | tf_op jit(solution)/shard_map/ppermute | solution.py:68
  141.7 2.1 %fusion.14 = bf16[256,256]{1,0:T(8,128)(2,1)S(1)} fusion(bf16[256,3584]{1,0:T(8,128)(2,1)S(1)} %constant_dynamic-update-slice_fusion.19, bf16[128,3584]{1,0:T(8,128)(2,1)} %collective-permute-done.18, bf16[128,3584]{1,0:T(8,128)(2,1)} %param.11, f32[256,256]{1,0:T(8,128)S(1)} %get-tuple-element.43), kind=kOutput, calls=%fused_computation.10 | convolution fusion | flops 474021888 | bytes 4063232 | tf_op jit(solution)/shard_map/dot_general | solution.py:128
  143.9 6.4 %collective-permute-start.20 = (bf16[256,256]{1,0:T(8,128)(2,1)S(1)}, bf16[256,256]{1,0:T(8,128)(2,1)S(1)}, u32[]{:S(2)}, u32[]{:S(2)}) collective-permute-start(bf16[256,256]{1,0:T(8,128)(2,1)S(1)} %fusion.14), channel_id=1, source_target_pairs={{0,256},{32,288},{64,320},{96,352},{128,384},{160,416},{192,448},{... | collective-permute-start | bytes 393224 | tf_op jit(solution)/shard_map/ppermute | solution.py:71
  150.3 12.9 %collective-permute-done.20 = bf16[256,256]{1,0:T(8,128)(2,1)S(1)} collective-permute-done((bf16[256,256]{1,0:T(8,128)(2,1)S(1)}, bf16[256,256]{1,0:T(8,128)(2,1)S(1)}, u32[]{:S(2)}, u32[]{:S(2)}) %collective-permute-start.20) | collective-permute-done | bytes 131104 | tf_op jit(solution)/shard_map/ppermute | solution.py:71
  164.0 2.4 %collective-permute-start.21 = (bf16[1792,128]{1,0:T(8,128)(2,1)S(1)}, bf16[1792,128]{1,0:T(8,128)(2,1)S(1)}, u32[]{:S(2)}, u32[]{:S(2)}) collective-permute-start(bf16[1792,128]{1,0:T(8,128)(2,1)S(1)} %slice.161), channel_id=1, source_target_pairs={{0,1},{1,0},{2,3},{3,2},{4,5},{5,4},{6,7},{7,6},{8,9},{9,8},{10,11... | collective-permute-start | bytes 1376264 | tf_op jit(solution)/shard_map/ppermute | solution.py:68
  (61 shorter events, 11.3 us)
Async XLA Ops:
  3.3 19.1 %collective-permute-start = (bf16[16,3584]{1,0:T(8,128)(2,1)}, bf16[16,3584]{1,0:T(8,128)(2,1)S(1)}, u32[]{:S(2)}, u32[]{:S(2)}) collective-permute-start(bf16[16,3584]{1,0:T(8,128)(2,1)} %get-tuple-element.7), channel_id=1, source_target_pairs={{0,16},{1,17},{2,18},{3,19},{4,20},{5,21},{6,22},{7,23},{8,24},{9,... | collective-permute-start | bytes 344072 | tf_op jit(solution)/shard_map/ppermute | solution.py:68
  9.0 16.0 %collective-permute-start.6 = (bf16[16,3584]{1,0:T(8,128)(2,1)}, bf16[16,3584]{1,0:T(8,128)(2,1)S(1)}, u32[]{:S(2)}, u32[]{:S(2)}) collective-permute-start(bf16[16,3584]{1,0:T(8,128)(2,1)} %get-tuple-element.9), channel_id=1, source_target_pairs={{0,16},{1,17},{2,18},{3,19},{4,20},{5,21},{6,22},{7,23},{8,24},{9,... | collective-permute-start | bytes 344072 | tf_op jit(solution)/shard_map/ppermute | solution.py:68
  10.9 95.6 %collective-permute-start.19 = (bf16[3584,128]{1,0:T(8,128)(2,1)}, bf16[3584,128]{1,0:T(8,128)(2,1)}, u32[]{:S(2)}, u32[]{:S(2)}) collective-permute-start(bf16[3584,128]{1,0:T(8,128)(2,1)} %param.10), channel_id=1, source_target_pairs={{0,1},{1,0},{2,3},{3,2},{4,5},{5,4},{6,7},{7,6},{8,9},{9,8},{10,11... | collective-permute-start | bytes 2752520 | tf_op jit(solution)/shard_map/ppermute | solution.py:68
  18.8 122.9 %collective-permute-start.18 = (bf16[128,3584]{1,0:T(8,128)(2,1)}, bf16[128,3584]{1,0:T(8,128)(2,1)}, u32[]{:S(2)}, u32[]{:S(2)}) collective-permute-start(bf16[128,3584]{1,0:T(8,128)(2,1)} %param.11), channel_id=1, source_target_pairs={{0,1},{1,0},{2,3},{3,2},{4,5},{5,4},{6,7},{7,6},{8,9},{9,8},{10,11... | collective-permute-start | bytes 2752520 | tf_op jit(solution)/shard_map/ppermute | solution.py:68
  23.0 15.5 %collective-permute-start.1 = (bf16[32,3584]{1,0:T(8,128)(2,1)S(1)}, bf16[32,3584]{1,0:T(8,128)(2,1)S(1)}, u32[]{:S(2)}, u32[]{:S(2)}) collective-permute-start(bf16[32,3584]{1,0:T(8,128)(2,1)S(1)} %get-tuple-element.38), channel_id=1, source_target_pairs={{0,8},{1,9},{2,10},{3,11},{4,12},{5,13},{6,14},{7,15},{8,0},{9,1},... | collective-permute-start | bytes 688136 | tf_op jit(solution)/shard_map/ppermute | solution.py:68
  25.1 39.0 %collective-permute-start.13 = (bf16[32,3584]{1,0:T(8,128)(2,1)S(1)}, bf16[32,3584]{1,0:T(8,128)(2,1)S(1)}, u32[]{:S(2)}, u32[]{:S(2)}) collective-permute-start(bf16[32,3584]{1,0:T(8,128)(2,1)S(1)} %get-tuple-element.32), channel_id=1, source_target_pairs={{0,8},{1,9},{2,10},{3,11},{4,12},{5,13},{6,14},{7,15},{8,0},{9,1},... | collective-permute-start | bytes 688136 | tf_op jit(solution)/shard_map/ppermute | solution.py:68
  28.5 32.5 %collective-permute-start.7 = (bf16[64,1792]{1,0:T(8,128)(2,1)S(1)}, bf16[64,1792]{1,0:T(8,128)(2,1)S(1)}, u32[]{:S(2)}, u32[]{:S(2)}) collective-permute-start(bf16[64,1792]{1,0:T(8,128)(2,1)S(1)} %pad_maximum_fusion), channel_id=1, source_target_pairs={{0,256},{32,288},{64,320},{96,352},{128,384},{160,416},{192,448},{... | collective-permute-start | bytes 688136 | tf_op jit(solution)/shard_map/ppermute | solution.py:71
  39.3 37.9 %copy-start = (bf16[256,3584]{1,0:T(8,128)(2,1)S(1)}, bf16[256,3584]{1,0:T(8,128)(2,1)}, u32[]{:S(2)}) copy-start(bf16[256,3584]{1,0:T(8,128)(2,1)} %get-tuple-element.29) | copy-start | bytes 5505028
  39.3 37.9 %collective-permute-start.3 = (bf16[64,3584]{1,0:T(8,128)(2,1)S(1)}, bf16[64,3584]{1,0:T(8,128)(2,1)S(1)}, u32[]{:S(2)}, u32[]{:S(2)}) collective-permute-start(bf16[64,3584]{1,0:T(8,128)(2,1)S(1)} %get-tuple-element.28), channel_id=1, source_target_pairs={{0,6},{1,7},{2,4},{3,5},{4,2},{5,3},{6,0},{7,1},{8,14},{9,15},{10,... | collective-permute-start | bytes 1376264 | tf_op jit(solution)/shard_map/ppermute | solution.py:68
  60.9 13.9 %collective-permute-start.2 = (bf16[64,3584]{1,0:T(8,128)(2,1)S(1)}, bf16[64,3584]{1,0:T(8,128)(2,1)S(1)}, u32[]{:S(2)}, u32[]{:S(2)}) collective-permute-start(bf16[64,3584]{1,0:T(8,128)(2,1)S(1)} %get-tuple-element.28), channel_id=1, source_target_pairs={{0,2},{1,3},{2,0},{3,1},{4,6},{5,7},{6,4},{7,5},{8,10},{9,11},{10,... | collective-permute-start | bytes 1376264 | tf_op jit(solution)/shard_map/ppermute | solution.py:68
  64.0 7.1 %collective-permute-start.8 = (bf16[64,1792]{1,0:T(8,128)(2,1)S(1)}, bf16[64,1792]{1,0:T(8,128)(2,1)S(1)}, u32[]{:S(2)}, u32[]{:S(2)}) collective-permute-start(bf16[64,1792]{1,0:T(8,128)(2,1)S(1)} %collective-permute-done.7), channel_id=1, source_target_pairs={{0,8},{1,9},{2,10},{3,11},{4,12},{5,13},{6,14},{7,15},{8,0},{9,1},... | collective-permute-start | bytes 688136 | tf_op jit(solution)/shard_map/ppermute | solution.py:68
  71.1 15.6 %collective-permute-start.15 = (bf16[64,3584]{1,0:T(8,128)(2,1)S(1)}, bf16[64,3584]{1,0:T(8,128)(2,1)S(1)}, u32[]{:S(2)}, u32[]{:S(2)}) collective-permute-start(bf16[64,3584]{1,0:T(8,128)(2,1)S(1)} %get-tuple-element.26), channel_id=1, source_target_pairs={{0,6},{1,7},{2,4},{3,5},{4,2},{5,3},{6,0},{7,1},{8,14},{9,15},{10,... | collective-permute-start | bytes 1376264 | tf_op jit(solution)/shard_map/ppermute | solution.py:68
  74.8 9.5 %collective-permute-start.14 = (bf16[64,3584]{1,0:T(8,128)(2,1)S(1)}, bf16[64,3584]{1,0:T(8,128)(2,1)S(1)}, u32[]{:S(2)}, u32[]{:S(2)}) collective-permute-start(bf16[64,3584]{1,0:T(8,128)(2,1)S(1)} %get-tuple-element.26), channel_id=1, source_target_pairs={{0,2},{1,3},{2,0},{3,1},{4,6},{5,7},{6,4},{7,5},{8,10},{9,11},{10,... | collective-permute-start | bytes 1376264 | tf_op jit(solution)/shard_map/ppermute | solution.py:68
  77.2 35.2 %collective-permute-start.10 = (bf16[128,1792]{1,0:T(8,128)(2,1)S(1)}, bf16[128,1792]{1,0:T(8,128)(2,1)S(1)}, u32[]{:S(2)}, u32[]{:S(2)}) collective-permute-start(bf16[128,1792]{1,0:T(8,128)(2,1)S(1)} %constant_dynamic-update-slice_fusion.14), channel_id=1, source_target_pairs={{0,6},{1,7},{2,4},{3,5},{4,2},{5,3},{6,0},{7,1},{8,14},{9,15},{10,... | collective-permute-start | bytes 1376264 | tf_op jit(solution)/shard_map/ppermute | solution.py:68
  84.4 33.4 %collective-permute-start.9 = (bf16[128,1792]{1,0:T(8,128)(2,1)S(1)}, bf16[128,1792]{1,0:T(8,128)(2,1)S(1)}, u32[]{:S(2)}, u32[]{:S(2)}) collective-permute-start(bf16[128,1792]{1,0:T(8,128)(2,1)S(1)} %constant_dynamic-update-slice_fusion.14), channel_id=1, source_target_pairs={{0,2},{1,3},{2,0},{3,1},{4,6},{5,7},{6,4},{7,5},{8,10},{9,11},{10,... | collective-permute-start | bytes 1376264 | tf_op jit(solution)/shard_map/ppermute | solution.py:68
  86.6 11.1 %collective-permute-start.4 = (bf16[32,3584]{1,0:T(8,128)(2,1)S(1)}, bf16[32,3584]{1,0:T(8,128)(2,1)S(1)}, u32[]{:S(2)}, u32[]{:S(2)}) collective-permute-start(bf16[32,3584]{1,0:T(8,128)(2,1)S(1)} %slice.106), channel_id=1, source_target_pairs={{0,6},{1,7},{2,4},{3,5},{4,2},{5,3},{6,0},{7,1},{8,14},{9,15},{10,... | collective-permute-start | bytes 688136 | tf_op jit(solution)/shard_map/ppermute | solution.py:68
  97.8 6.8 %collective-permute-start.5 = (bf16[32,3584]{1,0:T(8,128)(2,1)S(1)}, bf16[32,3584]{1,0:T(8,128)(2,1)S(1)}, u32[]{:S(2)}, u32[]{:S(2)}) collective-permute-start(bf16[32,3584]{1,0:T(8,128)(2,1)S(1)} %slice.107), channel_id=1, source_target_pairs={{0,2},{1,3},{2,0},{3,1},{4,6},{5,7},{6,4},{7,5},{8,10},{9,11},{10,... | collective-permute-start | bytes 688136 | tf_op jit(solution)/shard_map/ppermute | solution.py:68
  104.5 19.9 %collective-permute-start.17 = (bf16[32,3584]{1,0:T(8,128)(2,1)S(1)}, bf16[32,3584]{1,0:T(8,128)(2,1)S(1)}, u32[]{:S(2)}, u32[]{:S(2)}) collective-permute-start(bf16[32,3584]{1,0:T(8,128)(2,1)S(1)} %slice.119), channel_id=1, source_target_pairs={{0,2},{1,3},{2,0},{3,1},{4,6},{5,7},{6,4},{7,5},{8,10},{9,11},{10,... | collective-permute-start | bytes 688136 | tf_op jit(solution)/shard_map/ppermute | solution.py:68
  106.5 13.9 %collective-permute-start.16 = (bf16[32,3584]{1,0:T(8,128)(2,1)S(1)}, bf16[32,3584]{1,0:T(8,128)(2,1)S(1)}, u32[]{:S(2)}, u32[]{:S(2)}) collective-permute-start(bf16[32,3584]{1,0:T(8,128)(2,1)S(1)} %slice.118), channel_id=1, source_target_pairs={{0,6},{1,7},{2,4},{3,5},{4,2},{5,3},{6,0},{7,1},{8,14},{9,15},{10,... | collective-permute-start | bytes 688136 | tf_op jit(solution)/shard_map/ppermute | solution.py:68
  112.3 16.1 %collective-permute-start.22 = (bf16[256,256]{1,0:T(8,128)(2,1)S(1)}, bf16[256,256]{1,0:T(8,128)(2,1)S(1)}, u32[]{:S(2)}, u32[]{:S(2)}) collective-permute-start(bf16[256,256]{1,0:T(8,128)(2,1)S(1)} %get-tuple-element.42), channel_id=1, source_target_pairs={{0,256},{32,288},{64,320},{96,352},{128,384},{160,416},{192,448},{... | collective-permute-start | bytes 393224 | tf_op jit(solution)/shard_map/ppermute | solution.py:71
  117.8 10.6 %collective-permute-start.12 = (bf16[64,1792]{1,0:T(8,128)(2,1)S(1)}, bf16[64,1792]{1,0:T(8,128)(2,1)S(1)}, u32[]{:S(2)}, u32[]{:S(2)}) collective-permute-start(bf16[64,1792]{1,0:T(8,128)(2,1)S(1)} %slice.116), channel_id=1, source_target_pairs={{0,2},{1,3},{2,0},{3,1},{4,6},{5,7},{6,4},{7,5},{8,10},{9,11},{10,... | collective-permute-start | bytes 688136 | tf_op jit(solution)/shard_map/ppermute | solution.py:68
  120.4 8.0 %collective-permute-start.11 = (bf16[64,1792]{1,0:T(8,128)(2,1)S(1)}, bf16[64,1792]{1,0:T(8,128)(2,1)S(1)}, u32[]{:S(2)}, u32[]{:S(2)}) collective-permute-start(bf16[64,1792]{1,0:T(8,128)(2,1)S(1)} %slice.114), channel_id=1, source_target_pairs={{0,6},{1,7},{2,4},{3,5},{4,2},{5,3},{6,0},{7,1},{8,14},{9,15},{10,... | collective-permute-start | bytes 688136 | tf_op jit(solution)/shard_map/ppermute | solution.py:68
  129.2 37.2 %collective-permute-start.23 = (bf16[128,1792]{1,0:T(8,128)(2,1)S(1)}, bf16[128,1792]{1,0:T(8,128)(2,1)S(1)}, u32[]{:S(2)}, u32[]{:S(2)}) collective-permute-start(bf16[128,1792]{1,0:T(8,128)(2,1)S(1)} %slice.160), channel_id=1, source_target_pairs={{0,1},{1,0},{2,3},{3,2},{4,5},{5,4},{6,7},{7,6},{8,9},{9,8},{10,11... | collective-permute-start | bytes 1376264 | tf_op jit(solution)/shard_map/ppermute | solution.py:68
  143.9 19.3 %collective-permute-start.20 = (bf16[256,256]{1,0:T(8,128)(2,1)S(1)}, bf16[256,256]{1,0:T(8,128)(2,1)S(1)}, u32[]{:S(2)}, u32[]{:S(2)}) collective-permute-start(bf16[256,256]{1,0:T(8,128)(2,1)S(1)} %fusion.14), channel_id=1, source_target_pairs={{0,256},{32,288},{64,320},{96,352},{128,384},{160,416},{192,448},{... | collective-permute-start | bytes 393224 | tf_op jit(solution)/shard_map/ppermute | solution.py:71
  164.0 3.8 %collective-permute-start.21 = (bf16[1792,128]{1,0:T(8,128)(2,1)S(1)}, bf16[1792,128]{1,0:T(8,128)(2,1)S(1)}, u32[]{:S(2)}, u32[]{:S(2)}) collective-permute-start(bf16[1792,128]{1,0:T(8,128)(2,1)S(1)} %slice.161), channel_id=1, source_target_pairs={{0,1},{1,0},{2,3},{3,2},{4,5},{5,4},{6,7},{7,6},{8,9},{9,8},{10,11... | collective-permute-start | bytes 1376264 | tf_op jit(solution)/shard_map/ppermute | solution.py:68

commit v2 on v1

v2 whole, which is shorter than its diff:
```python
import jax
import jax.numpy as jnp
from jax import lax
from jax.experimental import pallas as pl
from jax.experimental.pallas import tpu as pltpu
from jax.sharding import PartitionSpec as P

CAP = 16
BF = jnp.bfloat16
FL = jnp.float32


def pick_rows(side_ref, tok_hbm, cot_hbm, routed_ref, gate_ref, own_ref, other_ref, tok_ref, cot_ref, sems):
    tok_copy = pltpu.make_async_copy(tok_hbm, tok_ref, sems.at[0])
    cot_copy = pltpu.make_async_copy(cot_hbm, cot_ref, sems.at[1])
    tok_copy.start()
    cot_copy.start()
    side = side_ref[0]
    tokens = tok_ref.shape[0]
    routed = routed_ref[...]
    row_id = lax.broadcasted_iota(jnp.int32, (tokens, tokens), 0)
    col_id = lax.broadcasted_iota(jnp.int32, (tokens, tokens), 1)
    upper = jnp.where(row_id <= col_id, 1.0, 0.0).astype(BF)
    count = jnp.dot(routed.astype(FL).astype(BF), upper, preferred_element_type=FL)
    slot = count.astype(jnp.int32) - 1
    slot_ids = lax.broadcasted_iota(jnp.int32, (CAP, tokens), 0)

    def chosen(e):
        return (routed[e : e + 1] == 1) & (slot[e : e + 1] == slot_ids)

    first, second = chosen(0), chosen(1)
    gates = gate_ref[...]
    lean = jnp.full((CAP, tokens), side, jnp.int32) == 0
    one = jnp.where(first, 1.0, 0.0)
    two = jnp.where(second, 1.0, 0.0)
    mine = jnp.where(lean, one, two)
    rest = jnp.where(lean, two, one)
    gate_one = jnp.where(first, gates[0:1], 0.0)
    gate_two = jnp.where(second, gates[1:2], 0.0)
    gate_mine = jnp.sum(jnp.where(lean, gate_one, gate_two), axis=1, keepdims=True)
    gate_rest = jnp.sum(jnp.where(lean, gate_two, gate_one), axis=1, keepdims=True)
    picker = jnp.concatenate([mine, rest], axis=0).astype(BF)
    scale = jnp.concatenate([gate_mine, gate_rest], axis=0)
    tok_copy.wait()
    rows = jnp.dot(picker, tok_ref[...], preferred_element_type=FL).astype(BF)
    own_ref[:CAP] = rows[:CAP]
    other_ref[:CAP] = rows[CAP:]
    cot_copy.wait()
    grads = (jnp.dot(picker, cot_ref[...], preferred_element_type=FL) * scale).astype(BF)
    own_ref[CAP:] = grads[:CAP]
    other_ref[CAP:] = grads[CAP:]


def picked(side, tokens, cotangent, routed, gate):
    vmem = pl.BlockSpec(memory_space=pltpu.VMEM)
    hbm = pl.BlockSpec(memory_space=pltpu.HBM)
    block = pltpu.VMEM(tokens.shape, BF)
    out = jax.ShapeDtypeStruct((2 * CAP, tokens.shape[1]), BF)
    return pl.pallas_call(
        pick_rows,
        in_specs=[pl.BlockSpec(memory_space=pltpu.SMEM), hbm, hbm, vmem, vmem],
        out_specs=(vmem,) * 2,
        out_shape=(out,) * 2,
        scratch_shapes=[block, block, pltpu.SemaphoreType.DMA((2,))],
        name="pick",
        compiler_params=pltpu.CompilerParams(vmem_limit_bytes=60 * 2**20),
    )(side[None], tokens, cotangent, routed, gate)


FREE = pl.CostEstimate(flops=0, transcendentals=0, bytes_accessed=0)
COPY = pl.CostEstimate(flops=0, transcendentals=0, bytes_accessed=10 * 2**20)
STEP = 512


def rows_to_units(rows, up_mine, up_other, down_mine, down_other, units):
    parts, tall, width = rows.shape
    starts = [(k, at) for k in range(parts) for at in range(0, tall, 2 * CAP)]
    up = grad = None
    for at in range(0, width, STEP):
        span = slice(at, at + STEP)
        wide_up = jnp.concatenate([up_mine[span], up_other[span]], axis=1)
        wide_down = jnp.concatenate([down_mine[:, span], down_other[:, span]], axis=0)
        rows_t = jnp.concatenate([rows[k, r : r + CAP, span] for k, r in starts], axis=0)
        rows_g = jnp.concatenate([rows[k, r + CAP : r + 2 * CAP, span] for k, r in starts], axis=0)
        more_up = jnp.dot(rows_t, wide_up, preferred_element_type=FL)
        more_grad = lax.dot_general(rows_g, wide_down, (((1,), (1,)), ((), ())), preferred_element_type=FL)
        up = more_up if up is None else up + more_up
        grad = more_grad if grad is None else grad + more_grad
    sigma = 1.0 / (1.0 + jnp.exp(-up))
    slots = up.shape[0]
    units[:slots] = (up * sigma).astype(BF)
    units[slots:] = (grad * sigma * (1.0 + up * (1.0 - sigma))).astype(BF)


def in_vmem(kernel, name, shape, *operands):
    vmem = pl.BlockSpec(memory_space=pltpu.VMEM)
    return pl.pallas_call(
        kernel,
        in_specs=[vmem] * len(operands),
        out_specs=vmem,
        out_shape=jax.ShapeDtypeStruct(shape, BF),
        name=name,
        cost_estimate=FREE,
        compiler_params=pltpu.CompilerParams(vmem_limit_bytes=20 * 2**20),
    )(*operands)


def repeat_block(first, second, out):
    n = first.shape[0]
    out[0, :n] = first[...]
    out[0, n:] = second[...]


def repeated(name, first, second):
    n, width = first.shape
    whole = pl.BlockSpec((n, width), lambda k: (0, 0))
    return pl.pallas_call(
        repeat_block,
        grid=(4,),
        in_specs=[whole, whole],
        out_specs=pl.BlockSpec((1, 2 * n, width), lambda k: (k, 0, 0)),
        out_shape=jax.ShapeDtypeStruct((4, 2 * n, width), BF),
        name=name,
        cost_estimate=COPY,
        compiler_params=pltpu.CompilerParams(vmem_limit_bytes=8 * 2**20),
    )(first, second)


def shards(tokens, cotangent, routed, gate, up_weight, down_weight):
    members = lax.axis_size("expert")
    sections = lax.axis_size("pipe")
    width = tokens.shape[2]
    half = width // 2
    hid = up_weight.shape[1]

    def across(name, value, z_mask=0, x_mask=0, core_mask=0):
        flip = z_mask * 8 + x_mask * 2 + core_mask
        with jax.named_scope(name):
            return lax.ppermute(value, "expert", [(s, s ^ flip) for s in range(members)])

    def mirrored(name, value):
        with jax.named_scope(name):
            return lax.ppermute(value, "pipe", [(q, q ^ (sections // 2)) for q in range(sections)])

    def after(value, other):
        return lax.optimization_barrier((value, other))

    member = lax.axis_index("expert")
    side = (member >= members // 2).astype(jnp.int32)
    upper = (lax.axis_index("pipe") >= sections // 2).astype(jnp.int32)
    own_start = upper * half
    sent_start = (1 - upper) * half

    def columns(value, start):
        return lax.dynamic_slice_in_dim(value, start, half, 1)

    own, other = picked(side, tokens[0], cotangent[0], routed[0].T, gate[0].T)

    circles = [[z + 2 * x for x in range(4)] for z in [8 * (k // 2) + k % 2 for k in range(members // 4)]]

    def ring(tag, first, second):
        with jax.named_scope(tag):
            copies = repeated(tag + "_copies", first, second)
            return lax.all_to_all(copies, "expert", 0, 0, axis_index_groups=circles, tiled=True)

    other_up = across("weight_up", up_weight, core_mask=1)
    other_down = across("weight_down", down_weight, core_mask=1)
    far = across("far", other, z_mask=2)
    beside = across("beside", own, z_mask=1)
    far, beside = after(far, beside)
    far_beside = across("far_beside", far, z_mask=1)

    sent = jnp.concatenate([columns(own, sent_start), columns(far, sent_start)], axis=0)
    far_beside, other_up, other_down = lax.optimization_barrier((far_beside, other_up, other_down))
    sent, far_beside = after(sent, far_beside)
    near_ring = ring("near_ring", own, far)
    pair_ring = ring("pair_ring", beside, far_beside)

    slots = 8 * CAP

    def through(name, rows, *weights):
        return in_vmem(rows_to_units, name, (2 * slots, 2 * hid), rows, *weights)

    near_units = through("near_units", near_ring, up_weight, other_up, down_weight, other_down)
    near_sent = mirrored("units_near", near_units)
    other_down, near_units = after(other_down, near_units)
    pair_units = through("pair_units", pair_ring, up_weight, other_up, down_weight, other_down)
    pair_sent = mirrored("units_pair", pair_units)

    mirror_near = mirrored("rows_mirror", sent)
    mirror_near, near_units = after(mirror_near, near_units)
    mirror_pair = across("pair_m", mirror_near, z_mask=1)
    mirror_ring = ring("mirror_ring", mirror_near, mirror_pair)
    near_ring, near_units = after(near_ring, near_units)
    pair_ring, near_sent, pair_units = lax.optimization_barrier((pair_ring, near_sent, pair_units))
    pair_sent, mirror_ring = after(pair_sent, mirror_ring)

    def gathered(kind):
        own_parts = [
            lax.dynamic_slice_in_dim(part.reshape(4, 2, 2, CAP, width)[:, :, kind], own_start, half, 3)
            for part in (near_ring, pair_ring)
        ]
        sent_rows = mirror_ring.reshape(4, 4, 2, CAP, half)[:, :, kind]
        parts = own_parts + [sent_rows[:, :2], sent_rows[:, 2:]]
        return jnp.concatenate([part.reshape(slots, half) for part in parts], axis=0)

    all_t = gathered(0)
    all_g = gathered(1)
    units = (near_units, pair_units, near_sent, pair_sent)
    all_hidden = jnp.concatenate([part[:slots] for part in units], axis=0)
    all_act = jnp.concatenate([part[slots:] for part in units], axis=0)
    down = lax.dot_general(all_hidden, all_g, (((0,), (0,)), ((), ())), preferred_element_type=FL)
    down_in = across("down_swap", down[hid:].astype(BF), core_mask=1)
    raise_ = lax.dot_general(all_t, all_act, (((0,), (0,)), ((), ())), preferred_element_type=FL)
    up_in = across("up_swap", raise_[:, hid:].astype(BF), core_mask=1)
    down_out = (down[:hid] + down_in.astype(FL)).astype(BF)
    up_out = (raise_[:, :hid] + up_in.astype(FL)).astype(BF)
    return up_out[None], down_out[None]


def solution(mesh):
    in_specs = (
        P("pipe", "expert", None),
        P("pipe", "expert", None),
        P("pipe", "expert", None),
        P("pipe", "expert", None),
        P(None, "expert"),
        P("expert", None),
    )
    out_specs = (P("pipe", None, "expert"), P("pipe", "expert", None))
    return jax.shard_map(shards, mesh=mesh, in_specs=in_specs, out_specs=out_specs, check_vma=False)
```

time: 171 us -> 138 us (0.81); the launches traced: 169 us -> 137 us
  starting transfers between devices: 98.5 us -> 69.1 us
  waiting for transfers between devices: 55.1 us -> 42.9 us
  Pallas kernels: 2.64 us -> 10.7 us
  local copies, waits for them, and re-layouts: 3.84 us -> 10 us
  matrix products: 5.61 us -> 1.34 us
    ppermute x21 -> x8, starting transfers between devices: 76.6 us -> 29.8 us  [across(): lax.ppermute(value, 'expert', [(s, s ^ flip) for s in range(members)])]
    ppermute x3, waiting for transfers between devices: 30 us -> 9.01 us  [mirrored(): lax.ppermute(value, 'pipe', [(q, q ^ sections // 2) for q in range(sectio...]
    all_to_all x0 -> x3, starting transfers between devices: none -> 15.8 us  [ring(): lax.all_to_all(copies, 'expert', 0, 0, axis_index_groups=circles, tiled=T...]
    pallas_call x0 -> x5, Pallas kernels: none -> 7.55 us  [the longest x2 5.39 us: in_vmem(): pl.pallas_call(kernel, in_specs=[vmem] * len(operands), out_specs=vmem, o...]
    ppermute x21 -> x8, waiting for transfers between devices: 25.1 us -> 29.8 us  [across(): lax.ppermute(value, 'expert', [(s, s ^ flip) for s in range(members)])]
    dot_general x2 -> x0, matrix products: 4.27 us -> none  [the longest x1 2.15 us: shards(): up = jnp.dot(rows_t, wide_up, preferred_element_type=FL)]
    all_to_all x0 -> x3, waiting for transfers between devices: none -> 4.04 us  [ring(): lax.all_to_all(copies, 'expert', 0, 0, axis_index_groups=circles, tiled=T...]
    unnamed x21 -> x16, local copies, waits for them, and re-layouts: 2.77 us -> 5.49 us
  transfers between devices with their start and end apart: 24 -> 14, of which waited for: 8 -> 6; matrix products, arithmetic and copies ran while one was open for 6% -> 4% of each run, Pallas kernels for 0% -> 5%
where the time goes in v2:
time: 138 us; the launch traced here: 137 us
  starting transfers between devices  69.1 us (50%)
  waiting for transfers between devices  42.9 us (31%)
  Pallas kernels  10.7 us (8%)
  local copies, waits for them, and re-layouts  10 us (7%)
  other arithmetic  2.41 us (2%)
    ppermute x8, waiting for transfers between devices, across(): lax.ppermute(value, 'expert', [(s, s ^ flip) for s in range(members)])  29.8 us
    ppermute x8, starting transfers between devices, across(): lax.ppermute(value, 'expert', [(s, s ^ flip) for s in range(members)])  29.8 us
    ppermute x3, starting transfers between devices, mirrored(): lax.ppermute(value, 'pipe', [(q, q ^ sections // 2) for q in range(sectio...  23.6 us
    all_to_all x3, starting transfers between devices, ring(): lax.all_to_all(copies, 'expert', 0, 0, axis_index_groups=circles, tiled=T...  15.8 us
    ppermute x3, waiting for transfers between devices, mirrored(): lax.ppermute(value, 'pipe', [(q, q ^ sections // 2) for q in range(sectio...  9.01 us
    unnamed x16, local copies, waits for them, and re-layouts  5.49 us
    pallas_call x2, Pallas kernels, in_vmem(): pl.pallas_call(kernel, in_specs=[vmem] * len(operands), out_specs=vmem, o...  5.39 us
    all_to_all x3, waiting for transfers between devices, ring(): lax.all_to_all(copies, 'expert', 0, 0, axis_index_groups=circles, tiled=T...  4.04 us
  transfers between devices with their start and end apart: 14, of which 6 were waited for; matrix products, arithmetic and copies ran while one was open for 4% of the time, Pallas kernels for 5%

profile of v2, /device:TPU:1, one launch (start us, length us, event | category | flops | bytes accessed | tf_op | source)
XLA Modules:
  0.0 137.4 jit_solution(10532294312867311795)
XLA Ops:
  0.6 3.2 %pick.1 = (bf16[32,3584]{1,0:T(8,128)(2,1)}, bf16[32,3584]{1,0:T(8,128)(2,1)}) custom-call(s32[1]{0:T(128)} %bitcast.side_ref, bf16[128,3584]{1,0:T(8,128)(2,1)} %bitcast.29, bf16[128,3584]{1,0:T(8,128)(2,1)} %bitcast.30, s32[2,128]{1,0:T(2,128)} %bitcast.39, f32[2,128]{1,0:T(2,128)} %bitcast.40), custom_call_target="tpu_custom_call" | custom-call | tf_op jit(solution)/shard_map/pick/pallas_call | solution.py:59
  3.8 5.7 %collective-permute-start = (bf16[32,3584]{1,0:T(8,128)(2,1)}, bf16[32,3584]{1,0:T(8,128)(2,1)S(1)}, u32[]{:S(2)}, u32[]{:S(2)}) collective-permute-start(bf16[32,3584]{1,0:T(8,128)(2,1)} %get-tuple-element.23), channel_id=1, source_target_pairs={{0,16},{1,17},{2,18},{3,19},{4,20},{5,21},{6,22},{7,23},{8,24},{9,... | collective-permute-start | bytes 688136 | tf_op jit(solution)/shard_map/far/ppermute | solution.py:139
  9.6 3.5 %collective-permute-start.1 = (bf16[32,3584]{1,0:T(8,128)(2,1)}, bf16[32,3584]{1,0:T(8,128)(2,1)S(1)}, u32[]{:S(2)}, u32[]{:S(2)}) collective-permute-start(bf16[32,3584]{1,0:T(8,128)(2,1)} %get-tuple-element.22.first), channel_id=1, source_target_pairs={{0,8},{1,9},{2,10},{3,11},{4,12},{5,13},{6,14},{7,15},{8,0},{9,1},... | collective-permute-start | bytes 688136 | tf_op jit(solution)/shard_map/beside/ppermute | solution.py:139
  13.1 6.1 %collective-permute-done.second = bf16[32,3584]{1,0:T(8,128)(2,1)S(1)} collective-permute-done((bf16[32,3584]{1,0:T(8,128)(2,1)}, bf16[32,3584]{1,0:T(8,128)(2,1)S(1)}, u32[]{:S(2)}, u32[]{:S(2)}) %collective-permute-start) | collective-permute-done | bytes 229408 | tf_op jit(solution)/shard_map/far/ppermute | solution.py:139
  19.2 0.9 copy-done.5
  20.4 1.3 copy-done
  21.6 6.6 %all-to-all-start = ((bf16[4,64,3584]{2,1,0:T(8,128)(2,1)}), bf16[4,64,3584]{2,1,0:T(8,128)(2,1)S(1)}, u32[]{:S(2)}, u32[]{:S(2)}) async-start(bf16[4,64,3584]{2,1,0:T(8,128)(2,1)} %copy-done), calls=%async_computation | async-start | bytes 3670016 | tf_op jit(solution)/shard_map/near_ring/all_to_all | solution.py:164
  28.2 3.8 %collective-permute-start.3 = (bf16[3584,128]{1,0:T(8,128)(2,1)S(1)}, bf16[3584,128]{1,0:T(8,128)(2,1)}, u32[]{:S(2)}, u32[]{:S(2)}) collective-permute-start(bf16[3584,128]{1,0:T(8,128)(2,1)S(1)} %copy-done.2), channel_id=1, source_target_pairs={{0,1},{1,0},{2,3},{3,2},{4,5},{5,4},{6,7},{7,6},{8,9},{9,8},{10,11... | collective-permute-start | bytes 2752520 | tf_op jit(solution)/shard_map/weight_up/ppermute | solution.py:139
  32.1 1.9 %collective-permute-start.4 = (bf16[128,3584]{1,0:T(8,128)(2,1)}, bf16[128,3584]{1,0:T(8,128)(2,1)}, u32[]{:S(2)}, u32[]{:S(2)}) collective-permute-start(bf16[128,3584]{1,0:T(8,128)(2,1)} %down_mine.3), channel_id=1, source_target_pairs={{0,1},{1,0},{2,3},{3,2},{4,5},{5,4},{6,7},{7,6},{8,9},{9,8},{10,11... | collective-permute-start | bytes 2752520 | tf_op jit(solution)/shard_map/weight_down/ppermute | solution.py:139
  34.0 1.9 %collective-permute-start.2 = (bf16[32,3584]{1,0:T(8,128)(2,1)S(1)}, bf16[32,3584]{1,0:T(8,128)(2,1)S(1)}, u32[]{:S(2)}, u32[]{:S(2)}) collective-permute-start(bf16[32,3584]{1,0:T(8,128)(2,1)S(1)} %collective-permute-done.second), channel_id=1, source_target_pairs={{0,8},{1,9},{2,10},{3,11},{4,12},{5,13},{6,14},{7,15},{8,0},{9,1},... | collective-permute-start | bytes 688136 | tf_op jit(solution)/shard_map/far_beside/ppermute | solution.py:139
  36.7 5.9 %collective-permute-done.2.second = bf16[32,3584]{1,0:T(8,128)(2,1)S(1)} collective-permute-done((bf16[32,3584]{1,0:T(8,128)(2,1)S(1)}, bf16[32,3584]{1,0:T(8,128)(2,1)S(1)}, u32[]{:S(2)}, u32[]{:S(2)}) %collective-permute-start.2) | collective-permute-done | bytes 229408 | tf_op jit(solution)/shard_map/far_beside/ppermute | solution.py:139
  42.6 14.4 %collective-permute-start.5 = (bf16[64,1792]{1,0:T(8,128)(2,1)}, bf16[64,1792]{1,0:T(8,128)(2,1)S(1)}, u32[]{:S(2)}, u32[]{:S(2)}) collective-permute-start(bf16[64,1792]{1,0:T(8,128)(2,1)} %pad_maximum_fusion), channel_id=1, source_target_pairs={{0,256},{32,288},{64,320},{96,352},{128,384},{160,416},{192,448},{... | collective-permute-start | bytes 688136 | tf_op jit(solution)/shard_map/rows_mirror/ppermute | solution.py:143
  57.2 1.3 copy-done.1
  58.5 4.5 %all-to-all-start.1 = ((bf16[4,64,3584]{2,1,0:T(8,128)(2,1)}), bf16[4,64,3584]{2,1,0:T(8,128)(2,1)}, u32[]{:S(2)}, u32[]{:S(2)}) async-start(bf16[4,64,3584]{2,1,0:T(8,128)(2,1)} %copy-done.1), calls=%async_computation.1 | async-start | bytes 3670016 | tf_op jit(solution)/shard_map/pair_ring/all_to_all | solution.py:164
  63.0 1.2 copy-done.3
  64.1 2.4 %near_units.1 = bf16[256,256]{1,0:T(8,128)(2,1)S(1)} custom-call(bf16[4,64,3584]{2,1,0:T(8,128)(2,1)S(1)} %all-to-all-done.rows, bf16[3584,128]{1,0:T(8,128)(2,1)S(1)} %copy-done.2, bf16[3584,128]{1,0:T(8,128)(2,1)} %collective-permute-done.3.up_other, bf16[128,3584]{1,0:T(8,128)(2,1)S(1)} %copy-done.3, bf16[128,3584]{1,0:T(8,128)(2,1)} %collective-permute-done.4.down_other), custom_call_target="tpu_custom_call" | custom-call | tf_op jit(solution)/shard_map/near_units/pallas_call | solution.py:97
  66.6 5.2 %collective-permute-start.6 = (bf16[256,256]{1,0:T(8,128)(2,1)S(1)}, bf16[256,256]{1,0:T(8,128)(2,1)S(1)}, u32[]{:S(2)}, u32[]{:S(2)}) collective-permute-start(bf16[256,256]{1,0:T(8,128)(2,1)S(1)} %near_units.1), channel_id=1, source_target_pairs={{0,256},{32,288},{64,320},{96,352},{128,384},{160,416},{192,448},{... | collective-permute-start | bytes 393224 | tf_op jit(solution)/shard_map/units_near/ppermute | solution.py:143
  71.8 3.4 %collective-permute-start.8 = (bf16[64,1792]{1,0:T(8,128)(2,1)S(1)}, bf16[64,1792]{1,0:T(8,128)(2,1)S(1)}, u32[]{:S(2)}, u32[]{:S(2)}) collective-permute-start(bf16[64,1792]{1,0:T(8,128)(2,1)S(1)} %collective-permute-done.5.first), channel_id=1, source_target_pairs={{0,8},{1,9},{2,10},{3,11},{4,12},{5,13},{6,14},{7,15},{8,0},{9,1},... | collective-permute-start | bytes 688136 | tf_op jit(solution)/shard_map/pair_m/ppermute | solution.py:139
  75.3 0.8 constant_dynamic-slice_fusion.1
  76.2 16.9 %collective-permute-done.8.second = bf16[64,1792]{1,0:T(8,128)(2,1)S(1)} collective-permute-done((bf16[64,1792]{1,0:T(8,128)(2,1)S(1)}, bf16[64,1792]{1,0:T(8,128)(2,1)S(1)}, u32[]{:S(2)}, u32[]{:S(2)}) %collective-permute-start.8) | collective-permute-done | bytes 229408 | tf_op jit(solution)/shard_map/pair_m/ppermute | solution.py:139
  93.1 1.8 %mirror_ring_copies.1 = bf16[4,128,1792]{2,1,0:T(8,128)(2,1)} custom-call(bf16[64,1792]{1,0:T(8,128)(2,1)S(1)} %collective-permute-done.5.first, bf16[64,1792]{1,0:T(8,128)(2,1)S(1)} %collective-permute-done.8.second), custom_call_target="tpu_custom_call" | custom-call | bytes 10485760 | tf_op jit(solution)/shard_map/mirror_ring/mirror_ring_copies/pallas_call | solution.py:117
  94.9 4.6 %all-to-all-start.2 = ((bf16[4,128,1792]{2,1,0:T(8,128)(2,1)}), bf16[4,128,1792]{2,1,0:T(8,128)(2,1)}, u32[]{:S(2)}, u32[]{:S(2)}) async-start(bf16[4,128,1792]{2,1,0:T(8,128)(2,1)} %mirror_ring_copies.1), calls=%async_computation.2 | async-start | bytes 3670016 | tf_op jit(solution)/shard_map/mirror_ring/all_to_all | solution.py:164
  99.5 3.0 %pair_units.1 = bf16[256,256]{1,0:T(8,128)(2,1)S(1)} custom-call(bf16[4,64,3584]{2,1,0:T(8,128)(2,1)} %all-to-all-done.1.rows, bf16[3584,128]{1,0:T(8,128)(2,1)S(1)} %copy-done.2, bf16[3584,128]{1,0:T(8,128)(2,1)} %collective-permute-done.3.up_other, bf16[128,3584]{1,0:T(8,128)(2,1)S(1)} %copy-done.4, bf16[128,3584]{1,0:T(8,128)(2,1)} %collective-permute-done.4.down_other), custom_call_target="tpu_custom_call" | custom-call | tf_op jit(solution)/shard_map/pair_units/pallas_call | solution.py:97
  102.5 4.0 %collective-permute-start.7 = (bf16[256,256]{1,0:T(8,128)(2,1)S(1)}, bf16[256,256]{1,0:T(8,128)(2,1)S(1)}, u32[]{:S(2)}, u32[]{:S(2)}) collective-permute-start(bf16[256,256]{1,0:T(8,128)(2,1)S(1)} %pair_units.1), channel_id=1, source_target_pairs={{0,256},{32,288},{64,320},{96,352},{128,384},{160,416},{192,448},{... | collective-permute-start | bytes 393224 | tf_op jit(solution)/shard_map/units_pair/ppermute | solution.py:143
  106.5 1.6 %fusion.37 = (bf16[4,2,1,16,3584]{4,3,2,1,0:T(8,128)(2,1)S(1)}, bf16[4,2,1,16,3584]{4,3,2,1,0:T(8,128)(2,1)S(1)}) fusion(bf16[4,2,2,16,3584]{4,3,2,1,0:T(8,128)(2,1)} %bitcast.9), kind=kLoop, calls=%fused_computation.50 | loop fusion | bytes 3670016 | tf_op jit(solution)/shard_map/slice | solution.py:200
  108.2 9.0 %collective-permute-done.7 = bf16[256,256]{1,0:T(8,128)(2,1)S(1)} collective-permute-done((bf16[256,256]{1,0:T(8,128)(2,1)S(1)}, bf16[256,256]{1,0:T(8,128)(2,1)S(1)}, u32[]{:S(2)}, u32[]{:S(2)}) %collective-permute-start.7) | collective-permute-done | bytes 131104 | tf_op jit(solution)/shard_map/units_pair/ppermute | solution.py:143
  117.2 4.0 %all-to-all-done.2 = bf16[4,128,1792]{2,1,0:T(8,128)(2,1)} async-done(((bf16[4,128,1792]{2,1,0:T(8,128)(2,1)}), bf16[4,128,1792]{2,1,0:T(8,128)(2,1)}, u32[]{:S(2)}, u32[]{:S(2)}) %all-to-all-start.2) | async-done | bytes 1835040 | tf_op jit(solution)/shard_map/mirror_ring/all_to_all | solution.py:164
  121.3 1.6 %slice_bitcast_fusion = (bf16[4,4,16,1792]{3,2,1,0:T(8,128)(2,1)S(1)}, bf16[4,4,16,1792]{3,2,1,0:T(8,128)(2,1)S(1)}) fusion(bf16[4,4,2,16,1792]{4,3,2,1,0:T(8,128)(2,1)} %bitcast.11), kind=kLoop, calls=%fused_computation.19 | loop fusion | bytes 3670016 | tf_op jit(solution)/shard_map/squeeze | solution.py:203
  124.6 7.5 %collective-permute-start.9 = (bf16[1792,128]{1,0:T(8,128)(2,1)S(1)}, bf16[1792,128]{1,0:T(8,128)(2,1)S(1)}, u32[]{:S(2)}, u32[]{:S(2)}) collective-permute-start(bf16[1792,128]{1,0:T(8,128)(2,1)S(1)} %slice.119), channel_id=1, source_target_pairs={{0,1},{1,0},{2,3},{3,2},{4,5},{5,4},{6,7},{7,6},{8,9},{9,8},{10,11... | collective-permute-start | bytes 1376264 | tf_op jit(solution)/shard_map/up_swap/ppermute | solution.py:139
  132.9 1.9 %collective-permute-start.10 = (bf16[128,1792]{1,0:T(8,128)(2,1)S(1)}, bf16[128,1792]{1,0:T(8,128)(2,1)S(1)}, u32[]{:S(2)}, u32[]{:S(2)}) collective-permute-start(bf16[128,1792]{1,0:T(8,128)(2,1)S(1)} %slice.118), channel_id=1, source_target_pairs={{0,1},{1,0},{2,3},{3,2},{4,5},{5,4},{6,7},{7,6},{8,9},{9,8},{10,11... | collective-permute-start | bytes 1376264 | tf_op jit(solution)/shard_map/down_swap/ppermute | solution.py:139
  134.8 0.9 fusion.18
  135.7 0.9 collective-permute-done.10
  (35 shorter events, 4.7 us)
Async XLA Ops:
  3.8 15.4 %collective-permute-start = (bf16[32,3584]{1,0:T(8,128)(2,1)}, bf16[32,3584]{1,0:T(8,128)(2,1)S(1)}, u32[]{:S(2)}, u32[]{:S(2)}) collective-permute-start(bf16[32,3584]{1,0:T(8,128)(2,1)} %get-tuple-element.23), channel_id=1, source_target_pairs={{0,16},{1,17},{2,18},{3,19},{4,20},{5,21},{6,22},{7,23},{8,24},{9,... | collective-permute-start | bytes 688136 | tf_op jit(solution)/shard_map/far/ppermute | solution.py:139
  9.6 9.7 %collective-permute-start.1 = (bf16[32,3584]{1,0:T(8,128)(2,1)}, bf16[32,3584]{1,0:T(8,128)(2,1)S(1)}, u32[]{:S(2)}, u32[]{:S(2)}) collective-permute-start(bf16[32,3584]{1,0:T(8,128)(2,1)} %get-tuple-element.22.first), channel_id=1, source_target_pairs={{0,8},{1,9},{2,10},{3,11},{4,12},{5,13},{6,14},{7,15},{8,0},{9,1},... | collective-permute-start | bytes 688136 | tf_op jit(solution)/shard_map/beside/ppermute | solution.py:139
  19.2 0.9 copy-start.5
  20.3 1.3 copy-start
  21.6 6.6 %copy-start.2 = (bf16[3584,128]{1,0:T(8,128)(2,1)S(1)}, bf16[3584,128]{1,0:T(8,128)(2,1)}, u32[]{:S(2)}) copy-start(bf16[3584,128]{1,0:T(8,128)(2,1)} %up_mine.3) | copy-start | bytes 2752516
  21.6 12.4 %copy-start.6 = (bf16[32,3584]{1,0:T(8,128)(2,1)S(1)}, bf16[32,3584]{1,0:T(8,128)(2,1)}, u32[]{:S(2)}) copy-start(bf16[32,3584]{1,0:T(8,128)(2,1)} %get-tuple-element.22.first) | copy-start | bytes 688132
  21.6 36.8 %all-to-all-start = ((bf16[4,64,3584]{2,1,0:T(8,128)(2,1)}), bf16[4,64,3584]{2,1,0:T(8,128)(2,1)S(1)}, u32[]{:S(2)}, u32[]{:S(2)}) async-start(bf16[4,64,3584]{2,1,0:T(8,128)(2,1)} %copy-done), calls=%async_computation | async-start | bytes 3670016 | tf_op jit(solution)/shard_map/near_ring/all_to_all | solution.py:164
  28.2 14.4 %collective-permute-start.3 = (bf16[3584,128]{1,0:T(8,128)(2,1)S(1)}, bf16[3584,128]{1,0:T(8,128)(2,1)}, u32[]{:S(2)}, u32[]{:S(2)}) collective-permute-start(bf16[3584,128]{1,0:T(8,128)(2,1)S(1)} %copy-done.2), channel_id=1, source_target_pairs={{0,1},{1,0},{2,3},{3,2},{4,5},{5,4},{6,7},{7,6},{8,9},{9,8},{10,11... | collective-permute-start | bytes 2752520 | tf_op jit(solution)/shard_map/weight_up/ppermute | solution.py:139
  32.1 10.5 %collective-permute-start.4 = (bf16[128,3584]{1,0:T(8,128)(2,1)}, bf16[128,3584]{1,0:T(8,128)(2,1)}, u32[]{:S(2)}, u32[]{:S(2)}) collective-permute-start(bf16[128,3584]{1,0:T(8,128)(2,1)} %down_mine.3), channel_id=1, source_target_pairs={{0,1},{1,0},{2,3},{3,2},{4,5},{5,4},{6,7},{7,6},{8,9},{9,8},{10,11... | collective-permute-start | bytes 2752520 | tf_op jit(solution)/shard_map/weight_down/ppermute | solution.py:139
  34.0 8.6 %collective-permute-start.2 = (bf16[32,3584]{1,0:T(8,128)(2,1)S(1)}, bf16[32,3584]{1,0:T(8,128)(2,1)S(1)}, u32[]{:S(2)}, u32[]{:S(2)}) collective-permute-start(bf16[32,3584]{1,0:T(8,128)(2,1)S(1)} %collective-permute-done.second), channel_id=1, source_target_pairs={{0,8},{1,9},{2,10},{3,11},{4,12},{5,13},{6,14},{7,15},{8,0},{9,1},... | collective-permute-start | bytes 688136 | tf_op jit(solution)/shard_map/far_beside/ppermute | solution.py:139
  42.6 29.2 %collective-permute-start.5 = (bf16[64,1792]{1,0:T(8,128)(2,1)}, bf16[64,1792]{1,0:T(8,128)(2,1)S(1)}, u32[]{:S(2)}, u32[]{:S(2)}) collective-permute-start(bf16[64,1792]{1,0:T(8,128)(2,1)} %pad_maximum_fusion), channel_id=1, source_target_pairs={{0,256},{32,288},{64,320},{96,352},{128,384},{160,416},{192,448},{... | collective-permute-start | bytes 688136 | tf_op jit(solution)/shard_map/rows_mirror/ppermute | solution.py:143
  57.2 1.3 copy-start.1
  58.5 36.4 %all-to-all-start.1 = ((bf16[4,64,3584]{2,1,0:T(8,128)(2,1)}), bf16[4,64,3584]{2,1,0:T(8,128)(2,1)}, u32[]{:S(2)}, u32[]{:S(2)}) async-start(bf16[4,64,3584]{2,1,0:T(8,128)(2,1)} %copy-done.1), calls=%async_computation.1 | async-start | bytes 3670016 | tf_op jit(solution)/shard_map/pair_ring/all_to_all | solution.py:164
  63.0 1.2 copy-start.3
  66.6 39.9 %collective-permute-start.6 = (bf16[256,256]{1,0:T(8,128)(2,1)S(1)}, bf16[256,256]{1,0:T(8,128)(2,1)S(1)}, u32[]{:S(2)}, u32[]{:S(2)}) collective-permute-start(bf16[256,256]{1,0:T(8,128)(2,1)S(1)} %near_units.1), channel_id=1, source_target_pairs={{0,256},{32,288},{64,320},{96,352},{128,384},{160,416},{192,448},{... | collective-permute-start | bytes 393224 | tf_op jit(solution)/shard_map/units_near/ppermute | solution.py:143
  71.8 21.3 %collective-permute-start.8 = (bf16[64,1792]{1,0:T(8,128)(2,1)S(1)}, bf16[64,1792]{1,0:T(8,128)(2,1)S(1)}, u32[]{:S(2)}, u32[]{:S(2)}) collective-permute-start(bf16[64,1792]{1,0:T(8,128)(2,1)S(1)} %collective-permute-done.5.first), channel_id=1, source_target_pairs={{0,8},{1,9},{2,10},{3,11},{4,12},{5,13},{6,14},{7,15},{8,0},{9,1},... | collective-permute-start | bytes 688136 | tf_op jit(solution)/shard_map/pair_m/ppermute | solution.py:139
  94.9 4.7 %copy-start.4 = (bf16[128,3584]{1,0:T(8,128)(2,1)S(1)}, bf16[128,3584]{1,0:T(8,128)(2,1)}, u32[]{:S(2)}) copy-start(bf16[128,3584]{1,0:T(8,128)(2,1)} %down_mine.3) | copy-start | bytes 2752516
  94.9 26.4 %all-to-all-start.2 = ((bf16[4,128,1792]{2,1,0:T(8,128)(2,1)}), bf16[4,128,1792]{2,1,0:T(8,128)(2,1)}, u32[]{:S(2)}, u32[]{:S(2)}) async-start(bf16[4,128,1792]{2,1,0:T(8,128)(2,1)} %mirror_ring_copies.1), calls=%async_computation.2 | async-start | bytes 3670016 | tf_op jit(solution)/shard_map/mirror_ring/all_to_all | solution.py:164
  102.5 14.7 %collective-permute-start.7 = (bf16[256,256]{1,0:T(8,128)(2,1)S(1)}, bf16[256,256]{1,0:T(8,128)(2,1)S(1)}, u32[]{:S(2)}, u32[]{:S(2)}) collective-permute-start(bf16[256,256]{1,0:T(8,128)(2,1)S(1)} %pair_units.1), channel_id=1, source_target_pairs={{0,256},{32,288},{64,320},{96,352},{128,384},{160,416},{192,448},{... | collective-permute-start | bytes 393224 | tf_op jit(solution)/shard_map/units_pair/ppermute | solution.py:143
  122.8 1.0 copy-start.7
  124.6 10.2 %collective-permute-start.9 = (bf16[1792,128]{1,0:T(8,128)(2,1)S(1)}, bf16[1792,128]{1,0:T(8,128)(2,1)S(1)}, u32[]{:S(2)}, u32[]{:S(2)}) collective-permute-start(bf16[1792,128]{1,0:T(8,128)(2,1)S(1)} %slice.119), channel_id=1, source_target_pairs={{0,1},{1,0},{2,3},{3,2},{4,5},{5,4},{6,7},{7,6},{8,9},{9,8},{10,11... | collective-permute-start | bytes 1376264 | tf_op jit(solution)/shard_map/up_swap/ppermute | solution.py:139
  132.9 3.7 %collective-permute-start.10 = (bf16[128,1792]{1,0:T(8,128)(2,1)S(1)}, bf16[128,1792]{1,0:T(8,128)(2,1)S(1)}, u32[]{:S(2)}, u32[]{:S(2)}) collective-permute-start(bf16[128,1792]{1,0:T(8,128)(2,1)S(1)} %slice.118), channel_id=1, source_target_pairs={{0,1},{1,0},{2,3},{3,2},{4,5},{5,4},{6,7},{7,6},{8,9},{9,8},{10,11... | collective-permute-start | bytes 1376264 | tf_op jit(solution)/shard_map/down_swap/ppermute | solution.py:139

commit v3 on v2

--- a/solution.py
+++ b/solution.py
@@ -10,11 +10,7 @@
 FL = jnp.float32
 
 
-def pick_rows(side_ref, tok_hbm, cot_hbm, routed_ref, gate_ref, own_ref, other_ref, tok_ref, cot_ref, sems):
-    tok_copy = pltpu.make_async_copy(tok_hbm, tok_ref, sems.at[0])
-    cot_copy = pltpu.make_async_copy(cot_hbm, cot_ref, sems.at[1])
-    tok_copy.start()
-    cot_copy.start()
+def pick_rows(side_ref, tok_ref, cot_ref, routed_ref, gate_ref, own_ref, other_ref):
     side = side_ref[0]
     tokens = tok_ref.shape[0]
     routed = routed_ref[...]
@@ -41,11 +37,9 @@
     gate_rest = jnp.sum(jnp.where(lean, gate_two, gate_one), axis=1, keepdims=True)
     picker = jnp.concatenate([mine, rest], axis=0).astype(BF)
     scale = jnp.concatenate([gate_mine, gate_rest], axis=0)
-    tok_copy.wait()
     rows = jnp.dot(picker, tok_ref[...], preferred_element_type=FL).astype(BF)
     own_ref[:CAP] = rows[:CAP]
     other_ref[:CAP] = rows[CAP:]
-    cot_copy.wait()
     grads = (jnp.dot(picker, cot_ref[...], preferred_element_type=FL) * scale).astype(BF)
     own_ref[CAP:] = grads[:CAP]
     other_ref[CAP:] = grads[CAP:]
@@ -53,35 +47,31 @@
 
 def picked(side, tokens, cotangent, routed, gate):
     vmem = pl.BlockSpec(memory_space=pltpu.VMEM)
-    hbm = pl.BlockSpec(memory_space=pltpu.HBM)
-    block = pltpu.VMEM(tokens.shape, BF)
     out = jax.ShapeDtypeStruct((2 * CAP, tokens.shape[1]), BF)
     return pl.pallas_call(
         pick_rows,
-        in_specs=[pl.BlockSpec(memory_space=pltpu.SMEM), hbm, hbm, vmem, vmem],
+        in_specs=[pl.BlockSpec(memory_space=pltpu.SMEM), vmem, vmem, vmem, vmem],
         out_specs=(vmem,) * 2,
         out_shape=(out,) * 2,
-        scratch_shapes=[block, block, pltpu.SemaphoreType.DMA((2,))],
         name="pick",
         compiler_params=pltpu.CompilerParams(vmem_limit_bytes=60 * 2**20),
     )(side[None], tokens, cotangent, routed, gate)
 
 
 FREE = pl.CostEstimate(flops=0, transcendentals=0, bytes_accessed=0)
-COPY = pl.CostEstimate(flops=0, transcendentals=0, bytes_accessed=10 * 2**20)
 STEP = 512
 
 
 def rows_to_units(rows, up_mine, up_other, down_mine, down_other, units):
     parts, tall, width = rows.shape
-    starts = [(k, at) for k in range(parts) for at in range(0, tall, 2 * CAP)]
+    n = tall // 2
     up = grad = None
     for at in range(0, width, STEP):
         span = slice(at, at + STEP)
         wide_up = jnp.concatenate([up_mine[span], up_other[span]], axis=1)
         wide_down = jnp.concatenate([down_mine[:, span], down_other[:, span]], axis=0)
-        rows_t = jnp.concatenate([rows[k, r : r + CAP, span] for k, r in starts], axis=0)
-        rows_g = jnp.concatenate([rows[k, r + CAP : r + 2 * CAP, span] for k, r in starts], axis=0)
+        rows_t = jnp.concatenate([rows[k, :n, span] for k in range(parts)], axis=0)
+        rows_g = jnp.concatenate([rows[k, n:, span] for k in range(parts)], axis=0)
         more_up = jnp.dot(rows_t, wide_up, preferred_element_type=FL)
         more_grad = lax.dot_general(rows_g, wide_down, (((1,), (1,)), ((), ())), preferred_element_type=FL)
         up = more_up if up is None else up + more_up
@@ -103,27 +93,6 @@
         cost_estimate=FREE,
         compiler_params=pltpu.CompilerParams(vmem_limit_bytes=20 * 2**20),
     )(*operands)
-
-
-def repeat_block(first, second, out):
-    n = first.shape[0]
-    out[0, :n] = first[...]
-    out[0, n:] = second[...]
-
-
-def repeated(name, first, second):
-    n, width = first.shape
-    whole = pl.BlockSpec((n, width), lambda k: (0, 0))
-    return pl.pallas_call(
-        repeat_block,
-        grid=(4,),
-        in_specs=[whole, whole],
-        out_specs=pl.BlockSpec((1, 2 * n, width), lambda k: (k, 0, 0)),
-        out_shape=jax.ShapeDtypeStruct((4, 2 * n, width), BF),
-        name=name,
-        cost_estimate=COPY,
-        compiler_params=pltpu.CompilerParams(vmem_limit_bytes=8 * 2**20),
-    )(first, second)
 
 
 def shards(tokens, cotangent, routed, gate, up_weight, down_weight):
@@ -158,24 +127,27 @@
 
     circles = [[z + 2 * x for x in range(4)] for z in [8 * (k // 2) + k % 2 for k in range(members // 4)]]
 
-    def ring(tag, first, second):
+    def ring(tag, block):
         with jax.named_scope(tag):
-            copies = repeated(tag + "_copies", first, second)
+            copies = jnp.broadcast_to(block[None], (4, *block.shape))
             return lax.all_to_all(copies, "expert", 0, 0, axis_index_groups=circles, tiled=True)
 
     other_up = across("weight_up", up_weight, core_mask=1)
     other_down = across("weight_down", down_weight, core_mask=1)
     far = across("far", other, z_mask=2)
     beside = across("beside", own, z_mask=1)
-    far, beside = after(far, beside)
     far_beside = across("far_beside", far, z_mask=1)
+    far_beside, other_up, other_down = lax.optimization_barrier((far_beside, other_up, other_down))
 
-    sent = jnp.concatenate([columns(own, sent_start), columns(far, sent_start)], axis=0)
-    far_beside, other_up, other_down = lax.optimization_barrier((far_beside, other_up, other_down))
-    sent, far_beside = after(sent, far_beside)
-    near_ring = ring("near_ring", own, far)
-    pair_ring = ring("pair_ring", beside, far_beside)
+    def joined(first, second):
+        return jnp.concatenate([first[:CAP], second[:CAP], first[CAP:], second[CAP:]], axis=0)
 
+    near = joined(own, far)
+    sent, far_beside = after(columns(near, sent_start), far_beside)
+    pair = joined(beside, far_beside)
+    near_ring = ring("near_ring", near)
+    pair_ring = ring("pair_ring", pair)
+    n = 2 * CAP
     slots = 8 * CAP
 
     def through(name, rows, *weights):
@@ -190,22 +162,18 @@
     mirror_near = mirrored("rows_mirror", sent)
     mirror_near, near_units = after(mirror_near, near_units)
     mirror_pair = across("pair_m", mirror_near, z_mask=1)
-    mirror_ring = ring("mirror_ring", mirror_near, mirror_pair)
+    mirror_ring = ring("mirror_ring", jnp.concatenate([mirror_near, mirror_pair], axis=0))
     near_ring, near_units = after(near_ring, near_units)
     pair_ring, near_sent, pair_units = lax.optimization_barrier((pair_ring, near_sent, pair_units))
     pair_sent, mirror_ring = after(pair_sent, mirror_ring)
 
-    def gathered(kind):
-        own_parts = [
-            lax.dynamic_slice_in_dim(part.reshape(4, 2, 2, CAP, width)[:, :, kind], own_start, half, 3)
-            for part in (near_ring, pair_ring)
-        ]
-        sent_rows = mirror_ring.reshape(4, 4, 2, CAP, half)[:, :, kind]
-        parts = own_parts + [sent_rows[:, :2], sent_rows[:, 2:]]
-        return jnp.concatenate([part.reshape(slots, half) for part in parts], axis=0)
+    def gathered(at):
+        own = [lax.dynamic_slice_in_dim(part[:, at : at + n], own_start, half, 2) for part in (near_ring, pair_ring)]
+        sent = [mirror_ring[:, at + k : at + k + n] for k in (0, 2 * n)]
+        return jnp.concatenate([part.reshape(slots, half) for part in own + sent], axis=0)
 
     all_t = gathered(0)
-    all_g = gathered(1)
+    all_g = gathered(n)
     units = (near_units, pair_units, near_sent, pair_sent)
     all_hidden = jnp.concatenate([part[:slots] for part in units], axis=0)
     all_act = jnp.concatenate([part[slots:] for part in units], axis=0)

time: 138 us -> 133 us (0.964)
  waiting for transfers between devices: 42.9 us -> 29.7 us
  starting transfers between devices: 69.1 us -> 75.1 us
  local copies, waits for them, and re-layouts: 10 us -> 12.2 us
  Pallas kernels: 10.7 us -> 8.75 us
    ppermute x8, waiting for transfers between devices: 29.8 us -> 17.7 us  [across(): lax.ppermute(value, 'expert', [(s, s ^ flip) for s in range(members)])]
    ppermute x3, starting transfers between devices: 23.6 us -> 33.2 us  [mirrored(): lax.ppermute(value, 'pipe', [(q, q ^ sections // 2) for q in range(sectio...]
    unnamed x16 -> x12, local copies, waits for them, and re-layouts: 5.49 us -> 0.03 us
    broadcast_in_dim x0 -> x3, local copies, waits for them, and re-layouts: none -> 4.11 us  [ring(): copies = jnp.broadcast_to(block[None], (4, *block.shape))]
    all_to_all x3, starting transfers between devices: 15.8 us -> 12.6 us  [ring(): lax.all_to_all(copies, 'expert', 0, 0, axis_index_groups=circles, tiled=T...]
    all_to_all x3, waiting for transfers between devices: 4.04 us -> 1.37 us  [ring(): lax.all_to_all(copies, 'expert', 0, 0, axis_index_groups=circles, tiled=T...]
    pallas_call x3 -> x0, Pallas kernels: 2.16 us -> none  [repeated(): pl.pallas_call(repeat_block, grid=(4,), in_specs=[whole, whole], out_spec...]
    slice x3 -> x7, local copies, waits for them, and re-layouts: 1.84 us -> 3.81 us  [the longest x2 1.94 us: joined(): first[:CAP]]
  transfers between devices with their start and end apart: 14 -> 14, of which waited for: 6 -> 5; matrix products, arithmetic and copies ran while one was open for 4% -> 10% of each run, Pallas kernels for 5% -> 5%
where the time goes in v3:
time: 133 us; the launch traced here: 132 us
  starting transfers between devices  75.1 us (56%)
  waiting for transfers between devices  29.7 us (22%)
  local copies, waits for them, and re-layouts  12.2 us (9%)
  Pallas kernels  8.75 us (7%)
  other arithmetic  2.76 us (2%)
  matrix products  2.56 us (2%)
    ppermute x3, starting transfers between devices, mirrored(): lax.ppermute(value, 'pipe', [(q, q ^ sections // 2) for q in range(sectio...  33.2 us
    ppermute x8, starting transfers between devices, across(): lax.ppermute(value, 'expert', [(s, s ^ flip) for s in range(members)])  29.3 us
    ppermute x8, waiting for transfers between devices, across(): lax.ppermute(value, 'expert', [(s, s ^ flip) for s in range(members)])  17.7 us
    all_to_all x3, starting transfers between devices, ring(): lax.all_to_all(copies, 'expert', 0, 0, axis_index_groups=circles, tiled=T...  12.6 us
    ppermute x3, waiting for transfers between devices, mirrored(): lax.ppermute(value, 'pipe', [(q, q ^ sections // 2) for q in range(sectio...  10.7 us
    pallas_call x2, Pallas kernels, in_vmem(): pl.pallas_call(kernel, in_specs=[vmem] * len(operands), out_specs=vmem, o...  5.95 us
    broadcast_in_dim x3, local copies, waits for them, and re-layouts, ring(): copies = jnp.broadcast_to(block[None], (4, *block.shape))  4.11 us
    pallas_call x1, Pallas kernels, picked(): pl.pallas_call(pick_rows, in_specs=[pl.BlockSpec(memory_space=pltpu.SMEM)...  2.8 us
  transfers between devices with their start and end apart: 14, of which 5 were waited for; matrix products, arithmetic and copies ran while one was open for 10% of the time, Pallas kernels for 5%

profile of v3, /device:TPU:1, one launch (start us, length us, event | category | flops | bytes accessed | tf_op | source)
XLA Modules:
  0.0 132.1 jit_solution(6537434779945684823)
XLA Ops:
  0.6 2.8 %pick.1 = (bf16[32,3584]{1,0:T(8,128)(2,1)}, bf16[32,3584]{1,0:T(8,128)(2,1)}) custom-call(s32[1]{0:T(128)} %bitcast.side_ref, bf16[128,3584]{1,0:T(8,128)(2,1)} %bitcast.21, bf16[128,3584]{1,0:T(8,128)(2,1)} %bitcast.22, s32[2,128]{1,0:T(2,128)} %bitcast.31, f32[2,128]{1,0:T(2,128)} %bitcast.32), custom_call_target="tpu_custom_call" | custom-call | tf_op jit(solution)/shard_map/pick/pallas_call | solution.py:51
  3.4 5.7 %collective-permute-start = (bf16[32,3584]{1,0:T(8,128)(2,1)}, bf16[32,3584]{1,0:T(8,128)(2,1)S(1)}, u32[]{:S(2)}, u32[]{:S(2)}) collective-permute-start(bf16[32,3584]{1,0:T(8,128)(2,1)} %get-tuple-element.21), channel_id=1, source_target_pairs={{0,16},{1,17},{2,18},{3,19},{4,20},{5,21},{6,22},{7,23},{8,24},{9,... | collective-permute-start | bytes 688136 | tf_op jit(solution)/shard_map/far/ppermute | solution.py:108
  9.2 3.6 %collective-permute-start.5 = (bf16[32,3584]{1,0:T(8,128)(2,1)}, bf16[32,3584]{1,0:T(8,128)(2,1)}, u32[]{:S(2)}, u32[]{:S(2)}) collective-permute-start(bf16[32,3584]{1,0:T(8,128)(2,1)} %get-tuple-element.20), channel_id=1, source_target_pairs={{0,8},{1,9},{2,10},{3,11},{4,12},{5,13},{6,14},{7,15},{8,0},{9,1},... | collective-permute-start | bytes 688136 | tf_op jit(solution)/shard_map/beside/ppermute | solution.py:108
  12.7 3.4 %collective-permute-start.2 = (bf16[3584,128]{1,0:T(8,128)(2,1)S(1)}, bf16[3584,128]{1,0:T(8,128)(2,1)}, u32[]{:S(2)}, u32[]{:S(2)}) collective-permute-start(bf16[3584,128]{1,0:T(8,128)(2,1)S(1)} %copy-done), channel_id=1, source_target_pairs={{0,1},{1,0},{2,3},{3,2},{4,5},{5,4},{6,7},{7,6},{8,9},{9,8},{10,11... | collective-permute-start | bytes 2752520 | tf_op jit(solution)/shard_map/weight_up/ppermute | solution.py:108
  16.1 1.9 %collective-permute-start.3 = (bf16[128,3584]{1,0:T(8,128)(2,1)}, bf16[128,3584]{1,0:T(8,128)(2,1)}, u32[]{:S(2)}, u32[]{:S(2)}) collective-permute-start(bf16[128,3584]{1,0:T(8,128)(2,1)} %down_mine.3), channel_id=1, source_target_pairs={{0,1},{1,0},{2,3},{3,2},{4,5},{5,4},{6,7},{7,6},{8,9},{9,8},{10,11... | collective-permute-start | bytes 2752520 | tf_op jit(solution)/shard_map/weight_down/ppermute | solution.py:108
  18.0 1.0 fusion.41
  19.1 1.4 %broadcast_in_dim.31 = bf16[4,64,3584]{2,1,0:T(8,128)(2,1)} broadcast(bf16[64,3584]{1,0:T(8,128)(2,1)S(1)} %pad_maximum_fusion), dimensions={1,2} | broadcast | bytes 2293760 | tf_op jit(solution)/shard_map/near_ring/broadcast_in_dim | solution.py:132
  20.5 4.6 %all-to-all-start = ((bf16[4,64,3584]{2,1,0:T(8,128)(2,1)}), bf16[4,64,3584]{2,1,0:T(8,128)(2,1)S(1)}, u32[]{:S(2)}, u32[]{:S(2)}) async-start(bf16[4,64,3584]{2,1,0:T(8,128)(2,1)} %broadcast_in_dim.31), calls=%async_computation | async-start | bytes 3670016 | tf_op jit(solution)/shard_map/near_ring/all_to_all | solution.py:133
  25.1 3.2 %collective-permute-start.1 = (bf16[32,3584]{1,0:T(8,128)(2,1)}, bf16[32,3584]{1,0:T(8,128)(2,1)S(1)}, u32[]{:S(2)}, u32[]{:S(2)}) collective-permute-start(bf16[32,3584]{1,0:T(8,128)(2,1)} %copy-done.2), channel_id=1, source_target_pairs={{0,8},{1,9},{2,10},{3,11},{4,12},{5,13},{6,14},{7,15},{8,0},{9,1},... | collective-permute-start | bytes 688136 | tf_op jit(solution)/shard_map/far_beside/ppermute | solution.py:108
  28.3 1.0 fusion.39
  30.0 2.8 %collective-permute-done.1 = bf16[32,3584]{1,0:T(8,128)(2,1)S(1)} collective-permute-done((bf16[32,3584]{1,0:T(8,128)(2,1)}, bf16[32,3584]{1,0:T(8,128)(2,1)S(1)}, u32[]{:S(2)}, u32[]{:S(2)}) %collective-permute-start.1) | collective-permute-done | bytes 229408 | tf_op jit(solution)/shard_map/far_beside/ppermute | solution.py:108
  32.8 15.3 %collective-permute-start.4 = (bf16[64,1792]{1,0:T(8,128)(2,1)}, bf16[64,1792]{1,0:T(8,128)(2,1)}, u32[]{:S(2)}, u32[]{:S(2)}) collective-permute-start(bf16[64,1792]{1,0:T(8,128)(2,1)} %constant_dynamic-slice_fusion.4), channel_id=1, source_target_pairs={{0,256},{32,288},{64,320},{96,352},{128,384},{160,416},{192,448},{... | collective-permute-start | bytes 688136 | tf_op jit(solution)/shard_map/rows_mirror/ppermute | solution.py:112
  48.2 1.4 %broadcast_in_dim.32 = bf16[4,64,3584]{2,1,0:T(8,128)(2,1)} broadcast(bf16[64,3584]{1,0:T(8,128)(2,1)S(1)} %pad_maximum_fusion.1), dimensions={1,2} | broadcast | bytes 2293760 | tf_op jit(solution)/shard_map/pair_ring/broadcast_in_dim | solution.py:132
  49.5 4.4 %all-to-all-start.1 = ((bf16[4,64,3584]{2,1,0:T(8,128)(2,1)}), bf16[4,64,3584]{2,1,0:T(8,128)(2,1)}, u32[]{:S(2)}, u32[]{:S(2)}) async-start(bf16[4,64,3584]{2,1,0:T(8,128)(2,1)} %broadcast_in_dim.32), calls=%async_computation.1 | async-start | bytes 3670016 | tf_op jit(solution)/shard_map/pair_ring/all_to_all | solution.py:133
  53.9 2.7 %near_units.1 = bf16[256,256]{1,0:T(8,128)(2,1)S(1)} custom-call(bf16[4,64,3584]{2,1,0:T(8,128)(2,1)S(1)} %all-to-all-done.rows, bf16[3584,128]{1,0:T(8,128)(2,1)S(1)} %copy-done, bf16[3584,128]{1,0:T(8,128)(2,1)} %collective-permute-done.2.up_other, bf16[128,3584]{1,0:T(8,128)(2,1)} %down_mine.3, bf16[128,3584]{1,0:T(8,128)(2,1)} %collective-permute-done.3.down_other), custom_call_target="tpu_custom_call" | custom-call | tf_op jit(solution)/shard_map/near_units/pallas_call | solution.py:87
  56.7 14.3 %collective-permute-start.6 = (bf16[256,256]{1,0:T(8,128)(2,1)S(1)}, bf16[256,256]{1,0:T(8,128)(2,1)S(1)}, u32[]{:S(2)}, u32[]{:S(2)}) collective-permute-start(bf16[256,256]{1,0:T(8,128)(2,1)S(1)} %near_units.1), channel_id=1, source_target_pairs={{0,256},{32,288},{64,320},{96,352},{128,384},{160,416},{192,448},{... | collective-permute-start | bytes 393224 | tf_op jit(solution)/shard_map/units_near/ppermute | solution.py:112
  71.0 1.9 %collective-permute-start.8 = (bf16[64,1792]{1,0:T(8,128)(2,1)}, bf16[64,1792]{1,0:T(8,128)(2,1)S(1)}, u32[]{:S(2)}, u32[]{:S(2)}) collective-permute-start(bf16[64,1792]{1,0:T(8,128)(2,1)} %collective-permute-done.4), channel_id=1, source_target_pairs={{0,8},{1,9},{2,10},{3,11},{4,12},{5,13},{6,14},{7,15},{8,0},{9,1},... | collective-permute-start | bytes 688136 | tf_op jit(solution)/shard_map/pair_m/ppermute | solution.py:108
  73.9 14.0 %collective-permute-done.8 = bf16[64,1792]{1,0:T(8,128)(2,1)S(1)} collective-permute-done((bf16[64,1792]{1,0:T(8,128)(2,1)}, bf16[64,1792]{1,0:T(8,128)(2,1)S(1)}, u32[]{:S(2)}, u32[]{:S(2)}) %collective-permute-start.8) | collective-permute-done | bytes 229408 | tf_op jit(solution)/shard_map/pair_m/ppermute | solution.py:108
  87.9 1.0 pad_maximum_fusion.2
  88.9 1.3 %broadcast_in_dim.33 = bf16[4,128,1792]{2,1,0:T(8,128)(2,1)} broadcast(bf16[128,1792]{1,0:T(8,128)(2,1)S(1)} %pad_maximum_fusion.2), dimensions={1,2} | broadcast | bytes 2293760 | tf_op jit(solution)/shard_map/mirror_ring/broadcast_in_dim | solution.py:132
  90.2 3.6 %all-to-all-start.2 = ((bf16[4,128,1792]{2,1,0:T(8,128)(2,1)}), bf16[4,128,1792]{2,1,0:T(8,128)(2,1)S(1)}, u32[]{:S(2)}, u32[]{:S(2)}) async-start(bf16[4,128,1792]{2,1,0:T(8,128)(2,1)} %broadcast_in_dim.33), calls=%async_computation.2 | async-start | bytes 3670016 | tf_op jit(solution)/shard_map/mirror_ring/all_to_all | solution.py:133
  93.8 3.3 %pair_units.1 = bf16[256,256]{1,0:T(8,128)(2,1)S(1)} custom-call(bf16[4,64,3584]{2,1,0:T(8,128)(2,1)} %all-to-all-done.1.rows, bf16[3584,128]{1,0:T(8,128)(2,1)S(1)} %copy-done, bf16[3584,128]{1,0:T(8,128)(2,1)} %collective-permute-done.2.up_other, bf16[128,3584]{1,0:T(8,128)(2,1)} %down_mine.3, bf16[128,3584]{1,0:T(8,128)(2,1)} %collective-permute-done.3.down_other), custom_call_target="tpu_custom_call" | custom-call | tf_op jit(solution)/shard_map/pair_units/pallas_call | solution.py:87
  97.1 3.6 %collective-permute-start.7 = (bf16[256,256]{1,0:T(8,128)(2,1)S(1)}, bf16[256,256]{1,0:T(8,128)(2,1)}, u32[]{:S(2)}, u32[]{:S(2)}) collective-permute-start(bf16[256,256]{1,0:T(8,128)(2,1)S(1)} %pair_units.1), channel_id=1, source_target_pairs={{0,256},{32,288},{64,320},{96,352},{128,384},{160,416},{192,448},{... | collective-permute-start | bytes 393224 | tf_op jit(solution)/shard_map/units_pair/ppermute | solution.py:112
  100.7 1.6 %fusion.37 = (bf16[4,32,3584]{2,1,0:T(8,128)(2,1)S(1)}, bf16[4,32,3584]{2,1,0:T(8,128)(2,1)S(1)}) fusion(bf16[4,64,3584]{2,1,0:T(8,128)(2,1)} %all-to-all-done.1.rows), kind=kLoop, calls=%fused_computation.49 | loop fusion | bytes 3670016 | tf_op jit(solution)/shard_map/slice | solution.py:171
  102.3 1.0 constant_dynamic-slice_fusion
  103.9 10.7 %collective-permute-done.7 = bf16[256,256]{1,0:T(8,128)(2,1)} collective-permute-done((bf16[256,256]{1,0:T(8,128)(2,1)S(1)}, bf16[256,256]{1,0:T(8,128)(2,1)}, u32[]{:S(2)}, u32[]{:S(2)}) %collective-permute-start.7) | collective-permute-done | bytes 131104 | tf_op jit(solution)/shard_map/units_pair/ppermute | solution.py:112
  114.6 1.4 %all-to-all-done.2 = bf16[4,128,1792]{2,1,0:T(8,128)(2,1)S(1)} async-done(((bf16[4,128,1792]{2,1,0:T(8,128)(2,1)}), bf16[4,128,1792]{2,1,0:T(8,128)(2,1)S(1)}, u32[]{:S(2)}, u32[]{:S(2)}) %all-to-all-start.2) | async-done | bytes 1835040 | tf_op jit(solution)/shard_map/mirror_ring/all_to_all | solution.py:133
  116.1 0.9 fusion.43
  117.0 1.9 %fusion = f32[1792,256]{1,0:T(8,128)S(1)} fusion(bf16[128,1792]{1,0:T(8,128)(2,1)S(1)} %bitcast.25, bf16[128,1792]{1,0:T(8,128)(2,1)S(1)} %bitcast.26, bf16[128,1792]{1,0:T(8,128)(2,1)} %bitcast.30, bf16[128,1792]{1,0:T(8,128)(2,1)} %bitcast.28, bf16[128,256]{1,0:T(8,128)(2,1)S(1)} %get-tuple-element.68, bf16[128,256]{1,0:T(8,128)(2,1)S(1)} %copy-done.5, ...), kind=kOutput, calls=%fused_computation | convolution fusion | flops 478150656 | bytes 3932160 | tf_op jit(solution)/shard_map/dot_general | solution.py:182
  119.0 7.7 %collective-permute-start.9 = (bf16[1792,128]{1,0:T(8,128)(2,1)S(1)}, bf16[1792,128]{1,0:T(8,128)(2,1)S(1)}, u32[]{:S(2)}, u32[]{:S(2)}) collective-permute-start(bf16[1792,128]{1,0:T(8,128)(2,1)S(1)} %slice.135), channel_id=1, source_target_pairs={{0,1},{1,0},{2,3},{3,2},{4,5},{5,4},{6,7},{7,6},{8,9},{9,8},{10,11... | collective-permute-start | bytes 1376264 | tf_op jit(solution)/shard_map/up_swap/ppermute | solution.py:108
  127.5 1.9 %collective-permute-start.10 = (bf16[128,1792]{1,0:T(8,128)(2,1)S(1)}, bf16[128,1792]{1,0:T(8,128)(2,1)S(1)}, u32[]{:S(2)}, u32[]{:S(2)}) collective-permute-start(bf16[128,1792]{1,0:T(8,128)(2,1)S(1)} %slice.134), channel_id=1, source_target_pairs={{0,1},{1,0},{2,3},{3,2},{4,5},{5,4},{6,7},{7,6},{8,9},{9,8},{10,11... | collective-permute-start | bytes 1376264 | tf_op jit(solution)/shard_map/down_swap/ppermute | solution.py:108
  130.3 0.9 collective-permute-done.10
  (35 shorter events, 5.2 us)
Async XLA Ops:
  0.6 12.1 %copy-start = (bf16[3584,128]{1,0:T(8,128)(2,1)S(1)}, bf16[3584,128]{1,0:T(8,128)(2,1)}, u32[]{:S(2)}) copy-start(bf16[3584,128]{1,0:T(8,128)(2,1)} %up_mine.3) | copy-start | bytes 2752516
  3.4 15.6 %collective-permute-start = (bf16[32,3584]{1,0:T(8,128)(2,1)}, bf16[32,3584]{1,0:T(8,128)(2,1)S(1)}, u32[]{:S(2)}, u32[]{:S(2)}) collective-permute-start(bf16[32,3584]{1,0:T(8,128)(2,1)} %get-tuple-element.21), channel_id=1, source_target_pairs={{0,16},{1,17},{2,18},{3,19},{4,20},{5,21},{6,22},{7,23},{8,24},{9,... | collective-permute-start | bytes 688136 | tf_op jit(solution)/shard_map/far/ppermute | solution.py:108
  9.2 19.1 %collective-permute-start.5 = (bf16[32,3584]{1,0:T(8,128)(2,1)}, bf16[32,3584]{1,0:T(8,128)(2,1)}, u32[]{:S(2)}, u32[]{:S(2)}) collective-permute-start(bf16[32,3584]{1,0:T(8,128)(2,1)} %get-tuple-element.20), channel_id=1, source_target_pairs={{0,8},{1,9},{2,10},{3,11},{4,12},{5,13},{6,14},{7,15},{8,0},{9,1},... | collective-permute-start | bytes 688136 | tf_op jit(solution)/shard_map/beside/ppermute | solution.py:108
  12.7 20.0 %collective-permute-start.2 = (bf16[3584,128]{1,0:T(8,128)(2,1)S(1)}, bf16[3584,128]{1,0:T(8,128)(2,1)}, u32[]{:S(2)}, u32[]{:S(2)}) collective-permute-start(bf16[3584,128]{1,0:T(8,128)(2,1)S(1)} %copy-done), channel_id=1, source_target_pairs={{0,1},{1,0},{2,3},{3,2},{4,5},{5,4},{6,7},{7,6},{8,9},{9,8},{10,11... | collective-permute-start | bytes 2752520 | tf_op jit(solution)/shard_map/weight_up/ppermute | solution.py:108
  16.1 16.7 %collective-permute-start.3 = (bf16[128,3584]{1,0:T(8,128)(2,1)}, bf16[128,3584]{1,0:T(8,128)(2,1)}, u32[]{:S(2)}, u32[]{:S(2)}) collective-permute-start(bf16[128,3584]{1,0:T(8,128)(2,1)} %down_mine.3), channel_id=1, source_target_pairs={{0,1},{1,0},{2,3},{3,2},{4,5},{5,4},{6,7},{7,6},{8,9},{9,8},{10,11... | collective-permute-start | bytes 2752520 | tf_op jit(solution)/shard_map/weight_down/ppermute | solution.py:108
  19.0 1.5 %copy-start.2 = (bf16[32,3584]{1,0:T(8,128)(2,1)}, bf16[32,3584]{1,0:T(8,128)(2,1)S(1)}, u32[]{:S(2)}) copy-start(bf16[32,3584]{1,0:T(8,128)(2,1)S(1)} %collective-permute-done) | copy-start | bytes 688132
  20.5 27.7 %all-to-all-start = ((bf16[4,64,3584]{2,1,0:T(8,128)(2,1)}), bf16[4,64,3584]{2,1,0:T(8,128)(2,1)S(1)}, u32[]{:S(2)}, u32[]{:S(2)}) async-start(bf16[4,64,3584]{2,1,0:T(8,128)(2,1)} %broadcast_in_dim.31), calls=%async_computation | async-start | bytes 3670016 | tf_op jit(solution)/shard_map/near_ring/all_to_all | solution.py:133
  25.1 7.6 %collective-permute-start.1 = (bf16[32,3584]{1,0:T(8,128)(2,1)}, bf16[32,3584]{1,0:T(8,128)(2,1)S(1)}, u32[]{:S(2)}, u32[]{:S(2)}) collective-permute-start(bf16[32,3584]{1,0:T(8,128)(2,1)} %copy-done.2), channel_id=1, source_target_pairs={{0,8},{1,9},{2,10},{3,11},{4,12},{5,13},{6,14},{7,15},{8,0},{9,1},... | collective-permute-start | bytes 688136 | tf_op jit(solution)/shard_map/far_beside/ppermute | solution.py:108
  32.8 38.2 %collective-permute-start.4 = (bf16[64,1792]{1,0:T(8,128)(2,1)}, bf16[64,1792]{1,0:T(8,128)(2,1)}, u32[]{:S(2)}, u32[]{:S(2)}) collective-permute-start(bf16[64,1792]{1,0:T(8,128)(2,1)} %constant_dynamic-slice_fusion.4), channel_id=1, source_target_pairs={{0,256},{32,288},{64,320},{96,352},{128,384},{160,416},{192,448},{... | collective-permute-start | bytes 688136 | tf_op jit(solution)/shard_map/rows_mirror/ppermute | solution.py:112
  49.5 39.3 %all-to-all-start.1 = ((bf16[4,64,3584]{2,1,0:T(8,128)(2,1)}), bf16[4,64,3584]{2,1,0:T(8,128)(2,1)}, u32[]{:S(2)}, u32[]{:S(2)}) async-start(bf16[4,64,3584]{2,1,0:T(8,128)(2,1)} %broadcast_in_dim.32), calls=%async_computation.1 | async-start | bytes 3670016 | tf_op jit(solution)/shard_map/pair_ring/all_to_all | solution.py:133
  56.7 44.0 %collective-permute-start.6 = (bf16[256,256]{1,0:T(8,128)(2,1)S(1)}, bf16[256,256]{1,0:T(8,128)(2,1)S(1)}, u32[]{:S(2)}, u32[]{:S(2)}) collective-permute-start(bf16[256,256]{1,0:T(8,128)(2,1)S(1)} %near_units.1), channel_id=1, source_target_pairs={{0,256},{32,288},{64,320},{96,352},{128,384},{160,416},{192,448},{... | collective-permute-start | bytes 393224 | tf_op jit(solution)/shard_map/units_near/ppermute | solution.py:112
  71.0 16.9 %collective-permute-start.8 = (bf16[64,1792]{1,0:T(8,128)(2,1)}, bf16[64,1792]{1,0:T(8,128)(2,1)S(1)}, u32[]{:S(2)}, u32[]{:S(2)}) collective-permute-start(bf16[64,1792]{1,0:T(8,128)(2,1)} %collective-permute-done.4), channel_id=1, source_target_pairs={{0,8},{1,9},{2,10},{3,11},{4,12},{5,13},{6,14},{7,15},{8,0},{9,1},... | collective-permute-start | bytes 688136 | tf_op jit(solution)/shard_map/pair_m/ppermute | solution.py:108
  90.2 25.7 %all-to-all-start.2 = ((bf16[4,128,1792]{2,1,0:T(8,128)(2,1)}), bf16[4,128,1792]{2,1,0:T(8,128)(2,1)S(1)}, u32[]{:S(2)}, u32[]{:S(2)}) async-start(bf16[4,128,1792]{2,1,0:T(8,128)(2,1)} %broadcast_in_dim.33), calls=%async_computation.2 | async-start | bytes 3670016 | tf_op jit(solution)/shard_map/mirror_ring/all_to_all | solution.py:133
  97.1 17.5 %collective-permute-start.7 = (bf16[256,256]{1,0:T(8,128)(2,1)S(1)}, bf16[256,256]{1,0:T(8,128)(2,1)}, u32[]{:S(2)}, u32[]{:S(2)}) collective-permute-start(bf16[256,256]{1,0:T(8,128)(2,1)S(1)} %pair_units.1), channel_id=1, source_target_pairs={{0,256},{32,288},{64,320},{96,352},{128,384},{160,416},{192,448},{... | collective-permute-start | bytes 393224 | tf_op jit(solution)/shard_map/units_pair/ppermute | solution.py:112
  103.9 13.1 %copy-start.4 = (bf16[128,256]{1,0:T(8,128)(2,1)S(1)}, bf16[128,256]{1,0:T(8,128)(2,1)}, u32[]{:S(2)}) copy-start(bf16[128,256]{1,0:T(8,128)(2,1)} %get-tuple-element.57) | copy-start | bytes 196612
  116.0 1.0 copy-start.5
  117.0 9.7 %copy-start.1 = (bf16[4,32,1792]{2,1,0:T(8,128)(2,1)S(1)}, bf16[4,32,1792]{2,1,0:T(8,128)(2,1)}, u32[]{:S(2)}) copy-start(bf16[4,32,1792]{2,1,0:T(8,128)(2,1)} %get-tuple-element.64) | copy-start | bytes 1376260
  117.0 9.7 %copy-start.3 = (bf16[128,256]{1,0:T(8,128)(2,1)S(1)}, bf16[128,256]{1,0:T(8,128)(2,1)}, u32[]{:S(2)}) copy-start(bf16[128,256]{1,0:T(8,128)(2,1)} %get-tuple-element.63) | copy-start | bytes 196612
  119.0 10.4 %collective-permute-start.9 = (bf16[1792,128]{1,0:T(8,128)(2,1)S(1)}, bf16[1792,128]{1,0:T(8,128)(2,1)S(1)}, u32[]{:S(2)}, u32[]{:S(2)}) collective-permute-start(bf16[1792,128]{1,0:T(8,128)(2,1)S(1)} %slice.135), channel_id=1, source_target_pairs={{0,1},{1,0},{2,3},{3,2},{4,5},{5,4},{6,7},{7,6},{8,9},{9,8},{10,11... | collective-permute-start | bytes 1376264 | tf_op jit(solution)/shard_map/up_swap/ppermute | solution.py:108
  127.5 3.7 %collective-permute-start.10 = (bf16[128,1792]{1,0:T(8,128)(2,1)S(1)}, bf16[128,1792]{1,0:T(8,128)(2,1)S(1)}, u32[]{:S(2)}, u32[]{:S(2)}) collective-permute-start(bf16[128,1792]{1,0:T(8,128)(2,1)S(1)} %slice.134), channel_id=1, source_target_pairs={{0,1},{1,0},{2,3},{3,2},{4,5},{5,4},{6,7},{7,6},{8,9},{9,8},{10,11... | collective-permute-start | bytes 1376264 | tf_op jit(solution)/shard_map/down_swap/ppermute | solution.py:108

commit v4 on v3

--- a/solution.py
+++ b/solution.py
@@ -127,10 +127,15 @@
 
     circles = [[z + 2 * x for x in range(4)] for z in [8 * (k // 2) + k % 2 for k in range(members // 4)]]
 
+    def repeated(block):
+        return jnp.broadcast_to(block[None], (4, *block.shape))
+
+    def around(tag, copies):
+        with jax.named_scope(tag):
+            return lax.all_to_all(copies, "expert", 0, 0, axis_index_groups=circles, tiled=True)
+
     def ring(tag, block):
-        with jax.named_scope(tag):
-            copies = jnp.broadcast_to(block[None], (4, *block.shape))
-            return lax.all_to_all(copies, "expert", 0, 0, axis_index_groups=circles, tiled=True)
+        return around(tag, repeated(block))
 
     other_up = across("weight_up", up_weight, core_mask=1)
     other_down = across("weight_down", down_weight, core_mask=1)
@@ -157,18 +162,25 @@
     near_sent = mirrored("units_near", near_units)
     other_down, near_units = after(other_down, near_units)
     pair_units = through("pair_units", pair_ring, up_weight, other_up, down_weight, other_down)
-    pair_sent = mirrored("units_pair", pair_units)
 
     mirror_near = mirrored("rows_mirror", sent)
     mirror_near, near_units = after(mirror_near, near_units)
     mirror_pair = across("pair_m", mirror_near, z_mask=1)
-    mirror_ring = ring("mirror_ring", jnp.concatenate([mirror_near, mirror_pair], axis=0))
+    mirror_pair, pair_units = after(mirror_pair, pair_units)
+    mirror_copies, pair_units, pair_ring = lax.optimization_barrier(
+        (repeated(jnp.concatenate([mirror_near, mirror_pair], axis=0)), pair_units, pair_ring)
+    )
+    mirror_ring = around("mirror_ring", mirror_copies)
+    pair_cols, pair_units = after(lax.dynamic_slice_in_dim(pair_ring[:, n:], own_start, half, 2), pair_units)
+    pair_sent = mirrored("units_pair", pair_units)
     near_ring, near_units = after(near_ring, near_units)
-    pair_ring, near_sent, pair_units = lax.optimization_barrier((pair_ring, near_sent, pair_units))
-    pair_sent, mirror_ring = after(pair_sent, mirror_ring)
+    near_sent, pair_sent, mirror_ring = lax.optimization_barrier((near_sent, pair_sent, mirror_ring))
+
+    def own_columns(part, at):
+        return lax.dynamic_slice_in_dim(part[:, at : at + n], own_start, half, 2)
 
     def gathered(at):
-        own = [lax.dynamic_slice_in_dim(part[:, at : at + n], own_start, half, 2) for part in (near_ring, pair_ring)]
+        own = [own_columns(near_ring, at), own_columns(pair_ring, at) if at == 0 else pair_cols]
         sent = [mirror_ring[:, at + k : at + k + n] for k in (0, 2 * n)]
         return jnp.concatenate([part.reshape(slots, half) for part in own + sent], axis=0)
 

time: 133 us -> 132 us (level)
  starting transfers between devices: 75.1 us -> 72 us
  waiting for transfers between devices: 29.7 us -> 31.7 us
    ppermute x3, waiting for transfers between devices: 10.7 us -> 18.3 us  [mirrored(): lax.ppermute(value, 'pipe', [(q, q ^ sections // 2) for q in range(sectio...]
    ppermute x8, starting transfers between devices: 29.3 us -> 24.4 us  [across(): lax.ppermute(value, 'expert', [(s, s ^ flip) for s in range(members)])]
    ppermute x8, waiting for transfers between devices: 17.7 us -> 13.2 us  [across(): lax.ppermute(value, 'expert', [(s, s ^ flip) for s in range(members)])]
    ppermute x3, starting transfers between devices: 33.2 us -> 35 us  [mirrored(): lax.ppermute(value, 'pipe', [(q, q ^ sections // 2) for q in range(sectio...]
  transfers between devices with their start and end apart: 14 -> 14, of which waited for: 5 -> 5; matrix products, arithmetic and copies ran while one was open for 10% -> 11% of each run, Pallas kernels for 5% -> 5%
where the time goes in v4:
time: 132 us; the launch traced here: 131 us
  starting transfers between devices  72 us (55%)
  waiting for transfers between devices  31.7 us (24%)
  local copies, waits for them, and re-layouts  12.6 us (10%)
  Pallas kernels  8.76 us (7%)
  other arithmetic  2.85 us (2%)
  matrix products  2.45 us (2%)
    ppermute x3, starting transfers between devices, mirrored(): lax.ppermute(value, 'pipe', [(q, q ^ sections // 2) for q in range(sectio...  35 us
    ppermute x8, starting transfers between devices, across(): lax.ppermute(value, 'expert', [(s, s ^ flip) for s in range(members)])  24.4 us
    ppermute x3, waiting for transfers between devices, mirrored(): lax.ppermute(value, 'pipe', [(q, q ^ sections // 2) for q in range(sectio...  18.3 us
    ppermute x8, waiting for transfers between devices, across(): lax.ppermute(value, 'expert', [(s, s ^ flip) for s in range(members)])  13.2 us
    all_to_all x3, starting transfers between devices, around(): lax.all_to_all(copies, 'expert', 0, 0, axis_index_groups=circles, tiled=T...  12.6 us
    pallas_call x2, Pallas kernels, in_vmem(): pl.pallas_call(kernel, in_specs=[vmem] * len(operands), out_specs=vmem, o...  5.96 us
    broadcast_in_dim x3, local copies, waits for them, and re-layouts, repeated(): return jnp.broadcast_to(block[None], (4, *block.shape))  4.1 us
    pallas_call x1, Pallas kernels, picked(): pl.pallas_call(pick_rows, in_specs=[pl.BlockSpec(memory_space=pltpu.SMEM)...  2.8 us
  transfers between devices with their start and end apart: 14, of which 5 were waited for; matrix products, arithmetic and copies ran while one was open for 11% of the time, Pallas kernels for 5%

profile of v4, /device:TPU:1, one launch (start us, length us, event | category | flops | bytes accessed | tf_op | source)
XLA Modules:
  0.0 131.2 jit_solution(17143726549508432257)
XLA Ops:
  0.6 2.8 %pick.1 = (bf16[32,3584]{1,0:T(8,128)(2,1)}, bf16[32,3584]{1,0:T(8,128)(2,1)}) custom-call(s32[1]{0:T(128)} %bitcast.side_ref, bf16[128,3584]{1,0:T(8,128)(2,1)} %bitcast.21, bf16[128,3584]{1,0:T(8,128)(2,1)} %bitcast.22, s32[2,128]{1,0:T(2,128)} %bitcast.31, f32[2,128]{1,0:T(2,128)} %bitcast.32), custom_call_target="tpu_custom_call" | custom-call | tf_op jit(solution)/shard_map/pick/pallas_call | solution.py:51
  3.4 5.7 %collective-permute-start = (bf16[32,3584]{1,0:T(8,128)(2,1)}, bf16[32,3584]{1,0:T(8,128)(2,1)S(1)}, u32[]{:S(2)}, u32[]{:S(2)}) collective-permute-start(bf16[32,3584]{1,0:T(8,128)(2,1)} %get-tuple-element.26), channel_id=1, source_target_pairs={{0,16},{1,17},{2,18},{3,19},{4,20},{5,21},{6,22},{7,23},{8,24},{9,... | collective-permute-start | bytes 688136 | tf_op jit(solution)/shard_map/far/ppermute | solution.py:108
  9.2 5.0 %collective-permute-start.2 = (bf16[3584,128]{1,0:T(8,128)(2,1)S(1)}, bf16[3584,128]{1,0:T(8,128)(2,1)}, u32[]{:S(2)}, u32[]{:S(2)}) collective-permute-start(bf16[3584,128]{1,0:T(8,128)(2,1)S(1)} %copy-done), channel_id=1, source_target_pairs={{0,1},{1,0},{2,3},{3,2},{4,5},{5,4},{6,7},{7,6},{8,9},{9,8},{10,11... | collective-permute-start | bytes 2752520 | tf_op jit(solution)/shard_map/weight_up/ppermute | solution.py:108
  14.2 1.9 %collective-permute-start.3 = (bf16[128,3584]{1,0:T(8,128)(2,1)}, bf16[128,3584]{1,0:T(8,128)(2,1)}, u32[]{:S(2)}, u32[]{:S(2)}) collective-permute-start(bf16[128,3584]{1,0:T(8,128)(2,1)} %down_mine.3), channel_id=1, source_target_pairs={{0,1},{1,0},{2,3},{3,2},{4,5},{5,4},{6,7},{7,6},{8,9},{9,8},{10,11... | collective-permute-start | bytes 2752520 | tf_op jit(solution)/shard_map/weight_down/ppermute | solution.py:108
  16.1 1.9 %collective-permute-start.6 = (bf16[32,3584]{1,0:T(8,128)(2,1)}, bf16[32,3584]{1,0:T(8,128)(2,1)}, u32[]{:S(2)}, u32[]{:S(2)}) collective-permute-start(bf16[32,3584]{1,0:T(8,128)(2,1)} %get-tuple-element.25), channel_id=1, source_target_pairs={{0,8},{1,9},{2,10},{3,11},{4,12},{5,13},{6,14},{7,15},{8,0},{9,1},... | collective-permute-start | bytes 688136 | tf_op jit(solution)/shard_map/beside/ppermute | solution.py:108
  18.0 1.0 fusion.41
  19.1 1.4 %broadcast_in_dim.31 = bf16[4,64,3584]{2,1,0:T(8,128)(2,1)} broadcast(bf16[64,3584]{1,0:T(8,128)(2,1)S(1)} %pad_maximum_fusion), dimensions={1,2} | broadcast | bytes 2293760 | tf_op jit(solution)/shard_map/broadcast_in_dim | solution.py:131
  20.5 4.6 %all-to-all-start = ((bf16[4,64,3584]{2,1,0:T(8,128)(2,1)}), bf16[4,64,3584]{2,1,0:T(8,128)(2,1)S(1)}, u32[]{:S(2)}, u32[]{:S(2)}) async-start(bf16[4,64,3584]{2,1,0:T(8,128)(2,1)} %broadcast_in_dim.31), calls=%async_computation | async-start | bytes 3670016 | tf_op jit(solution)/shard_map/near_ring/all_to_all | solution.py:135
  25.1 3.2 %collective-permute-start.1 = (bf16[32,3584]{1,0:T(8,128)(2,1)S(1)}, bf16[32,3584]{1,0:T(8,128)(2,1)S(1)}, u32[]{:S(2)}, u32[]{:S(2)}) collective-permute-start(bf16[32,3584]{1,0:T(8,128)(2,1)S(1)} %collective-permute-done), channel_id=1, source_target_pairs={{0,8},{1,9},{2,10},{3,11},{4,12},{5,13},{6,14},{7,15},{8,0},{9,1},... | collective-permute-start | bytes 688136 | tf_op jit(solution)/shard_map/far_beside/ppermute | solution.py:108
  28.3 1.0 fusion.39
  30.0 2.4 %collective-permute-done.1 = bf16[32,3584]{1,0:T(8,128)(2,1)S(1)} collective-permute-done((bf16[32,3584]{1,0:T(8,128)(2,1)S(1)}, bf16[32,3584]{1,0:T(8,128)(2,1)S(1)}, u32[]{:S(2)}, u32[]{:S(2)}) %collective-permute-start.1) | collective-permute-done | bytes 229408 | tf_op jit(solution)/shard_map/far_beside/ppermute | solution.py:108
  32.5 15.4 %collective-permute-start.4 = (bf16[64,1792]{1,0:T(8,128)(2,1)}, bf16[64,1792]{1,0:T(8,128)(2,1)}, u32[]{:S(2)}, u32[]{:S(2)}) collective-permute-start(bf16[64,1792]{1,0:T(8,128)(2,1)} %constant_dynamic-slice_fusion.4), channel_id=1, source_target_pairs={{0,256},{32,288},{64,320},{96,352},{128,384},{160,416},{192,448},{... | collective-permute-start | bytes 688136 | tf_op jit(solution)/shard_map/rows_mirror/ppermute | solution.py:112
  47.9 1.4 %broadcast_in_dim.32 = bf16[4,64,3584]{2,1,0:T(8,128)(2,1)} broadcast(bf16[64,3584]{1,0:T(8,128)(2,1)S(1)} %pad_maximum_fusion.1), dimensions={1,2} | broadcast | bytes 2293760 | tf_op jit(solution)/shard_map/broadcast_in_dim | solution.py:131
  49.3 4.4 %all-to-all-start.1 = ((bf16[4,64,3584]{2,1,0:T(8,128)(2,1)}), bf16[4,64,3584]{2,1,0:T(8,128)(2,1)}, u32[]{:S(2)}, u32[]{:S(2)}) async-start(bf16[4,64,3584]{2,1,0:T(8,128)(2,1)} %broadcast_in_dim.32), calls=%async_computation.1 | async-start | bytes 3670016 | tf_op jit(solution)/shard_map/pair_ring/all_to_all | solution.py:135
  53.7 2.7 %near_units.1 = bf16[256,256]{1,0:T(8,128)(2,1)S(1)} custom-call(bf16[4,64,3584]{2,1,0:T(8,128)(2,1)S(1)} %all-to-all-done.rows, bf16[3584,128]{1,0:T(8,128)(2,1)S(1)} %copy-done, bf16[3584,128]{1,0:T(8,128)(2,1)} %collective-permute-done.2.up_other, bf16[128,3584]{1,0:T(8,128)(2,1)} %down_mine.3, bf16[128,3584]{1,0:T(8,128)(2,1)} %collective-permute-done.3.down_other), custom_call_target="tpu_custom_call" | custom-call | tf_op jit(solution)/shard_map/near_units/pallas_call | solution.py:87
  56.4 14.5 %collective-permute-start.7 = (bf16[256,256]{1,0:T(8,128)(2,1)S(1)}, bf16[256,256]{1,0:T(8,128)(2,1)S(1)}, u32[]{:S(2)}, u32[]{:S(2)}) collective-permute-start(bf16[256,256]{1,0:T(8,128)(2,1)S(1)} %near_units.1), channel_id=1, source_target_pairs={{0,256},{32,288},{64,320},{96,352},{128,384},{160,416},{192,448},{... | collective-permute-start | bytes 393224 | tf_op jit(solution)/shard_map/units_near/ppermute | solution.py:112
  70.9 1.9 %collective-permute-start.5 = (bf16[64,1792]{1,0:T(8,128)(2,1)}, bf16[64,1792]{1,0:T(8,128)(2,1)}, u32[]{:S(2)}, u32[]{:S(2)}) collective-permute-start(bf16[64,1792]{1,0:T(8,128)(2,1)} %collective-permute-done.4), channel_id=1, source_target_pairs={{0,8},{1,9},{2,10},{3,11},{4,12},{5,13},{6,14},{7,15},{8,0},{9,1},... | collective-permute-start | bytes 688136 | tf_op jit(solution)/shard_map/pair_m/ppermute | solution.py:108
  73.0 0.9 constant_dynamic-slice_fusion
  74.7 3.3 %pair_units.1 = bf16[256,256]{1,0:T(8,128)(2,1)S(1)} custom-call(bf16[4,64,3584]{2,1,0:T(8,128)(2,1)} %all-to-all-done.1.rows, bf16[3584,128]{1,0:T(8,128)(2,1)S(1)} %copy-done, bf16[3584,128]{1,0:T(8,128)(2,1)} %collective-permute-done.2.up_other, bf16[128,3584]{1,0:T(8,128)(2,1)} %down_mine.3, bf16[128,3584]{1,0:T(8,128)(2,1)} %collective-permute-done.3.down_other), custom_call_target="tpu_custom_call" | custom-call | tf_op jit(solution)/shard_map/pair_units/pallas_call | solution.py:87
  77.9 9.8 %collective-permute-done.5 = bf16[64,1792]{1,0:T(8,128)(2,1)} collective-permute-done((bf16[64,1792]{1,0:T(8,128)(2,1)}, bf16[64,1792]{1,0:T(8,128)(2,1)}, u32[]{:S(2)}, u32[]{:S(2)}) %collective-permute-start.5) | collective-permute-done | bytes 229408 | tf_op jit(solution)/shard_map/pair_m/ppermute | solution.py:108
  87.8 1.1 pad_maximum_fusion.2
  88.8 1.3 %broadcast_in_dim.33 = bf16[4,128,1792]{2,1,0:T(8,128)(2,1)} broadcast(bf16[128,1792]{1,0:T(8,128)(2,1)S(1)} %pad_maximum_fusion.2), dimensions={1,2} | broadcast | bytes 2293760 | tf_op jit(solution)/shard_map/broadcast_in_dim | solution.py:131
  90.2 3.6 %all-to-all-start.2 = ((bf16[4,128,1792]{2,1,0:T(8,128)(2,1)}), bf16[4,128,1792]{2,1,0:T(8,128)(2,1)S(1)}, u32[]{:S(2)}, u32[]{:S(2)}) async-start(bf16[4,128,1792]{2,1,0:T(8,128)(2,1)} %broadcast_in_dim.33), calls=%async_computation.2 | async-start | bytes 3670016 | tf_op jit(solution)/shard_map/mirror_ring/all_to_all | solution.py:135
  93.8 1.6 %fusion.38 = (bf16[4,32,3584]{2,1,0:T(8,128)(2,1)S(1)}, bf16[4,32,3584]{2,1,0:T(8,128)(2,1)S(1)}) fusion(bf16[4,64,3584]{2,1,0:T(8,128)(2,1)} %all-to-all-done.1.rows), kind=kLoop, calls=%fused_computation.50 | loop fusion | bytes 3670016 | tf_op jit(solution)/shard_map/slice | solution.py:180
  95.4 1.0 constant_dynamic-slice_fusion.1
  96.4 5.1 %collective-permute-start.8 = (bf16[256,256]{1,0:T(8,128)(2,1)S(1)}, bf16[256,256]{1,0:T(8,128)(2,1)S(1)}, u32[]{:S(2)}, u32[]{:S(2)}) collective-permute-start(bf16[256,256]{1,0:T(8,128)(2,1)S(1)} %pair_units.1), channel_id=1, source_target_pairs={{0,256},{32,288},{64,320},{96,352},{128,384},{160,416},{192,448},{... | collective-permute-start | bytes 393224 | tf_op jit(solution)/shard_map/units_pair/ppermute | solution.py:112
  102.1 18.3 %collective-permute-done.8 = bf16[256,256]{1,0:T(8,128)(2,1)S(1)} collective-permute-done((bf16[256,256]{1,0:T(8,128)(2,1)S(1)}, bf16[256,256]{1,0:T(8,128)(2,1)S(1)}, u32[]{:S(2)}, u32[]{:S(2)}) %collective-permute-start.8) | collective-permute-done | bytes 131104 | tf_op jit(solution)/shard_map/units_pair/ppermute | solution.py:112
  121.3 1.8 %fusion.8 = f32[256,1792]{1,0:T(8,128)S(1)} fusion(bf16[128,1792]{1,0:T(8,128)(2,1)S(1)} %bitcast.26, bf16[128,1792]{1,0:T(8,128)(2,1)S(1)} %bitcast.25, bf16[128,1792]{1,0:T(8,128)(2,1)} %bitcast.30, bf16[128,1792]{1,0:T(8,128)(2,1)S(1)} %bitcast.28, bf16[128,256]{1,0:T(8,128)(2,1)S(1)} %get-tuple-element.70, bf16[128,256]{1,0:T(8,128)(2,1)S(1)} %get-tuple-element.68, ...), kind=kOutput, calls=%fused_computation.8 | convolution fusion | flops 478150656 | bytes 3932160 | tf_op jit(solution)/shard_map/dot_general | solution.py:192
  123.1 2.8 %collective-permute-start.10 = (bf16[128,1792]{1,0:T(8,128)(2,1)S(1)}, bf16[128,1792]{1,0:T(8,128)(2,1)S(1)}, u32[]{:S(2)}, u32[]{:S(2)}) collective-permute-start(bf16[128,1792]{1,0:T(8,128)(2,1)S(1)} %slice.134), channel_id=1, source_target_pairs={{0,1},{1,0},{2,3},{3,2},{4,5},{5,4},{6,7},{7,6},{8,9},{9,8},{10,11... | collective-permute-start | bytes 1376264 | tf_op jit(solution)/shard_map/down_swap/ppermute | solution.py:108
  126.7 1.9 %collective-permute-start.9 = (bf16[1792,128]{1,0:T(8,128)(2,1)S(1)}, bf16[1792,128]{1,0:T(8,128)(2,1)S(1)}, u32[]{:S(2)}, u32[]{:S(2)}) collective-permute-start(bf16[1792,128]{1,0:T(8,128)(2,1)S(1)} %slice.135), channel_id=1, source_target_pairs={{0,1},{1,0},{2,3},{3,2},{4,5},{5,4},{6,7},{7,6},{8,9},{9,8},{10,11... | collective-permute-start | bytes 1376264 | tf_op jit(solution)/shard_map/up_swap/ppermute | solution.py:108
  129.5 0.9 collective-permute-done.9
  130.4 0.9 fusion.18
  (35 shorter events, 4.9 us)
Async XLA Ops:
  0.6 8.5 %copy-start = (bf16[3584,128]{1,0:T(8,128)(2,1)S(1)}, bf16[3584,128]{1,0:T(8,128)(2,1)}, u32[]{:S(2)}) copy-start(bf16[3584,128]{1,0:T(8,128)(2,1)} %up_mine.3) | copy-start | bytes 2752516
  3.4 15.6 %collective-permute-start = (bf16[32,3584]{1,0:T(8,128)(2,1)}, bf16[32,3584]{1,0:T(8,128)(2,1)S(1)}, u32[]{:S(2)}, u32[]{:S(2)}) collective-permute-start(bf16[32,3584]{1,0:T(8,128)(2,1)} %get-tuple-element.26), channel_id=1, source_target_pairs={{0,16},{1,17},{2,18},{3,19},{4,20},{5,21},{6,22},{7,23},{8,24},{9,... | collective-permute-start | bytes 688136 | tf_op jit(solution)/shard_map/far/ppermute | solution.py:108
  9.2 23.3 %collective-permute-start.2 = (bf16[3584,128]{1,0:T(8,128)(2,1)S(1)}, bf16[3584,128]{1,0:T(8,128)(2,1)}, u32[]{:S(2)}, u32[]{:S(2)}) collective-permute-start(bf16[3584,128]{1,0:T(8,128)(2,1)S(1)} %copy-done), channel_id=1, source_target_pairs={{0,1},{1,0},{2,3},{3,2},{4,5},{5,4},{6,7},{7,6},{8,9},{9,8},{10,11... | collective-permute-start | bytes 2752520 | tf_op jit(solution)/shard_map/weight_up/ppermute | solution.py:108
  14.2 18.3 %collective-permute-start.3 = (bf16[128,3584]{1,0:T(8,128)(2,1)}, bf16[128,3584]{1,0:T(8,128)(2,1)}, u32[]{:S(2)}, u32[]{:S(2)}) collective-permute-start(bf16[128,3584]{1,0:T(8,128)(2,1)} %down_mine.3), channel_id=1, source_target_pairs={{0,1},{1,0},{2,3},{3,2},{4,5},{5,4},{6,7},{7,6},{8,9},{9,8},{10,11... | collective-permute-start | bytes 2752520 | tf_op jit(solution)/shard_map/weight_down/ppermute | solution.py:108
  16.1 12.2 %collective-permute-start.6 = (bf16[32,3584]{1,0:T(8,128)(2,1)}, bf16[32,3584]{1,0:T(8,128)(2,1)}, u32[]{:S(2)}, u32[]{:S(2)}) collective-permute-start(bf16[32,3584]{1,0:T(8,128)(2,1)} %get-tuple-element.25), channel_id=1, source_target_pairs={{0,8},{1,9},{2,10},{3,11},{4,12},{5,13},{6,14},{7,15},{8,0},{9,1},... | collective-permute-start | bytes 688136 | tf_op jit(solution)/shard_map/beside/ppermute | solution.py:108
  20.5 27.5 %all-to-all-start = ((bf16[4,64,3584]{2,1,0:T(8,128)(2,1)}), bf16[4,64,3584]{2,1,0:T(8,128)(2,1)S(1)}, u32[]{:S(2)}, u32[]{:S(2)}) async-start(bf16[4,64,3584]{2,1,0:T(8,128)(2,1)} %broadcast_in_dim.31), calls=%async_computation | async-start | bytes 3670016 | tf_op jit(solution)/shard_map/near_ring/all_to_all | solution.py:135
  25.1 7.4 %collective-permute-start.1 = (bf16[32,3584]{1,0:T(8,128)(2,1)S(1)}, bf16[32,3584]{1,0:T(8,128)(2,1)S(1)}, u32[]{:S(2)}, u32[]{:S(2)}) collective-permute-start(bf16[32,3584]{1,0:T(8,128)(2,1)S(1)} %collective-permute-done), channel_id=1, source_target_pairs={{0,8},{1,9},{2,10},{3,11},{4,12},{5,13},{6,14},{7,15},{8,0},{9,1},... | collective-permute-start | bytes 688136 | tf_op jit(solution)/shard_map/far_beside/ppermute | solution.py:108
  32.5 38.5 %collective-permute-start.4 = (bf16[64,1792]{1,0:T(8,128)(2,1)}, bf16[64,1792]{1,0:T(8,128)(2,1)}, u32[]{:S(2)}, u32[]{:S(2)}) collective-permute-start(bf16[64,1792]{1,0:T(8,128)(2,1)} %constant_dynamic-slice_fusion.4), channel_id=1, source_target_pairs={{0,256},{32,288},{64,320},{96,352},{128,384},{160,416},{192,448},{... | collective-permute-start | bytes 688136 | tf_op jit(solution)/shard_map/rows_mirror/ppermute | solution.py:112
  49.3 25.4 %all-to-all-start.1 = ((bf16[4,64,3584]{2,1,0:T(8,128)(2,1)}), bf16[4,64,3584]{2,1,0:T(8,128)(2,1)}, u32[]{:S(2)}, u32[]{:S(2)}) async-start(bf16[4,64,3584]{2,1,0:T(8,128)(2,1)} %broadcast_in_dim.32), calls=%async_computation.1 | async-start | bytes 3670016 | tf_op jit(solution)/shard_map/pair_ring/all_to_all | solution.py:135
  56.4 45.7 %collective-permute-start.7 = (bf16[256,256]{1,0:T(8,128)(2,1)S(1)}, bf16[256,256]{1,0:T(8,128)(2,1)S(1)}, u32[]{:S(2)}, u32[]{:S(2)}) collective-permute-start(bf16[256,256]{1,0:T(8,128)(2,1)S(1)} %near_units.1), channel_id=1, source_target_pairs={{0,256},{32,288},{64,320},{96,352},{128,384},{160,416},{192,448},{... | collective-permute-start | bytes 393224 | tf_op jit(solution)/shard_map/units_near/ppermute | solution.py:112
  70.9 16.8 %collective-permute-start.5 = (bf16[64,1792]{1,0:T(8,128)(2,1)}, bf16[64,1792]{1,0:T(8,128)(2,1)}, u32[]{:S(2)}, u32[]{:S(2)}) collective-permute-start(bf16[64,1792]{1,0:T(8,128)(2,1)} %collective-permute-done.4), channel_id=1, source_target_pairs={{0,8},{1,9},{2,10},{3,11},{4,12},{5,13},{6,14},{7,15},{8,0},{9,1},... | collective-permute-start | bytes 688136 | tf_op jit(solution)/shard_map/pair_m/ppermute | solution.py:108
  90.2 30.3 %all-to-all-start.2 = ((bf16[4,128,1792]{2,1,0:T(8,128)(2,1)}), bf16[4,128,1792]{2,1,0:T(8,128)(2,1)S(1)}, u32[]{:S(2)}, u32[]{:S(2)}) async-start(bf16[4,128,1792]{2,1,0:T(8,128)(2,1)} %broadcast_in_dim.33), calls=%async_computation.2 | async-start | bytes 3670016 | tf_op jit(solution)/shard_map/mirror_ring/all_to_all | solution.py:135
  96.4 24.1 %collective-permute-start.8 = (bf16[256,256]{1,0:T(8,128)(2,1)S(1)}, bf16[256,256]{1,0:T(8,128)(2,1)S(1)}, u32[]{:S(2)}, u32[]{:S(2)}) collective-permute-start(bf16[256,256]{1,0:T(8,128)(2,1)S(1)} %pair_units.1), channel_id=1, source_target_pairs={{0,256},{32,288},{64,320},{96,352},{128,384},{160,416},{192,448},{... | collective-permute-start | bytes 393224 | tf_op jit(solution)/shard_map/units_pair/ppermute | solution.py:112
  102.1 18.5 %copy-start.1 = (bf16[4,32,1792]{2,1,0:T(8,128)(2,1)S(1)}, bf16[4,32,1792]{2,1,0:T(8,128)(2,1)}, u32[]{:S(2)}) copy-start(bf16[4,32,1792]{2,1,0:T(8,128)(2,1)} %get-tuple-element.74) | copy-start | bytes 1376260
  120.4 0.8 copy-start.4
  121.3 4.6 %copy-start.2 = (bf16[4,32,1792]{2,1,0:T(8,128)(2,1)S(1)}, bf16[4,32,1792]{2,1,0:T(8,128)(2,1)}, u32[]{:S(2)}) copy-start(bf16[4,32,1792]{2,1,0:T(8,128)(2,1)} %get-tuple-element.73) | copy-start | bytes 1376260
  121.3 4.6 %copy-start.3 = (bf16[128,256]{1,0:T(8,128)(2,1)S(1)}, bf16[128,256]{1,0:T(8,128)(2,1)}, u32[]{:S(2)}) copy-start(bf16[128,256]{1,0:T(8,128)(2,1)} %get-tuple-element.67) | copy-start | bytes 196612
  123.1 5.5 %collective-permute-start.10 = (bf16[128,1792]{1,0:T(8,128)(2,1)S(1)}, bf16[128,1792]{1,0:T(8,128)(2,1)S(1)}, u32[]{:S(2)}, u32[]{:S(2)}) collective-permute-start(bf16[128,1792]{1,0:T(8,128)(2,1)S(1)} %slice.134), channel_id=1, source_target_pairs={{0,1},{1,0},{2,3},{3,2},{4,5},{5,4},{6,7},{7,6},{8,9},{9,8},{10,11... | collective-permute-start | bytes 1376264 | tf_op jit(solution)/shard_map/down_swap/ppermute | solution.py:108
  126.7 3.7 %collective-permute-start.9 = (bf16[1792,128]{1,0:T(8,128)(2,1)S(1)}, bf16[1792,128]{1,0:T(8,128)(2,1)S(1)}, u32[]{:S(2)}, u32[]{:S(2)}) collective-permute-start(bf16[1792,128]{1,0:T(8,128)(2,1)S(1)} %slice.135), channel_id=1, source_target_pairs={{0,1},{1,0},{2,3},{3,2},{4,5},{5,4},{6,7},{7,6},{8,9},{9,8},{10,11... | collective-permute-start | bytes 1376264 | tf_op jit(solution)/shard_map/up_swap/ppermute | solution.py:108

commit v5 on v4

--- a/solution.py
+++ b/solution.py
@@ -171,18 +171,19 @@
         (repeated(jnp.concatenate([mirror_near, mirror_pair], axis=0)), pair_units, pair_ring)
     )
     mirror_ring = around("mirror_ring", mirror_copies)
-    pair_cols, pair_units = after(lax.dynamic_slice_in_dim(pair_ring[:, n:], own_start, half, 2), pair_units)
+    pair_cols, pair_units = after(lax.dynamic_slice(pair_ring, (0, n, own_start), (1, n, half)), pair_units)
     pair_sent = mirrored("units_pair", pair_units)
     near_ring, near_units = after(near_ring, near_units)
     near_sent, pair_sent, mirror_ring = lax.optimization_barrier((near_sent, pair_sent, mirror_ring))
 
     def own_columns(part, at):
-        return lax.dynamic_slice_in_dim(part[:, at : at + n], own_start, half, 2)
+        return lax.dynamic_slice(part, (0, at, own_start), (4, n, half))
 
     def gathered(at):
-        own = [own_columns(near_ring, at), own_columns(pair_ring, at) if at == 0 else pair_cols]
+        own = [own_columns(near_ring, at)]
+        own += [own_columns(pair_ring, at)] if at == 0 else [pair_cols, lax.dynamic_slice(pair_ring, (1, n, own_start), (3, n, half))]
         sent = [mirror_ring[:, at + k : at + k + n] for k in (0, 2 * n)]
-        return jnp.concatenate([part.reshape(slots, half) for part in own + sent], axis=0)
+        return jnp.concatenate([part.reshape(-1, half) for part in own + sent], axis=0)
 
     all_t = gathered(0)
     all_g = gathered(n)

time: 132 us -> 144 us (1.091)
  waiting for transfers between devices: 31.7 us -> 53.5 us
  starting transfers between devices: 72 us -> 61.7 us
  local copies, waits for them, and re-layouts: 12.6 us -> 15.9 us
    all_to_all x3, waiting for transfers between devices: 0.18 us -> 20.5 us  [around(): lax.all_to_all(copies, 'expert', 0, 0, axis_index_groups=circles, tiled=T...]
    ppermute x3, starting transfers between devices: 35 us -> 21.7 us  [mirrored(): lax.ppermute(value, 'pipe', [(q, q ^ sections // 2) for q in range(sectio...]
    ppermute x8, waiting for transfers between devices: 13.2 us -> 24.3 us  [across(): lax.ppermute(value, 'expert', [(s, s ^ flip) for s in range(members)])]
    ppermute x3, waiting for transfers between devices: 18.3 us -> 8.74 us  [mirrored(): lax.ppermute(value, 'pipe', [(q, q ^ sections // 2) for q in range(sectio...]
    unnamed x10 -> x22, local copies, waits for them, and re-layouts: 0.66 us -> 4.79 us
    ppermute x8, starting transfers between devices: 24.4 us -> 27.4 us  [across(): lax.ppermute(value, 'expert', [(s, s ^ flip) for s in range(members)])]
    slice x2 -> x0, local copies, waits for them, and re-layouts: 1.71 us -> none  [own_columns(): return lax.dynamic_slice_in_dim(part[:, at:at + n], own_start, half, 2)]
    slice x1, local copies, waits for them, and re-layouts: 0.13 us -> 1.61 us  [gathered(): sent = [mirror_ring[:, at + k:at + k + n] for k in (0, 2 * n)]]
  transfers between devices with their start and end apart: 14 -> 14, of which waited for: 5 -> 6; matrix products, arithmetic and copies ran while one was open for 11% -> 8% of each run, Pallas kernels for 5% -> 4%
where the time goes in v5:
time: 144 us
  starting transfers between devices  61.7 us (43%)
  waiting for transfers between devices  53.5 us (37%)
  local copies, waits for them, and re-layouts  15.9 us (11%)
  Pallas kernels  8.2 us (6%)
  other arithmetic  1.82 us (1%)
    ppermute x8, starting transfers between devices, across(): lax.ppermute(value, 'expert', [(s, s ^ flip) for s in range(members)])  27.4 us
    ppermute x8, waiting for transfers between devices, across(): lax.ppermute(value, 'expert', [(s, s ^ flip) for s in range(members)])  24.3 us
    ppermute x3, starting transfers between devices, mirrored(): lax.ppermute(value, 'pipe', [(q, q ^ sections // 2) for q in range(sectio...  21.7 us
    all_to_all x3, waiting for transfers between devices, around(): lax.all_to_all(copies, 'expert', 0, 0, axis_index_groups=circles, tiled=T...  20.5 us
    all_to_all x3, starting transfers between devices, around(): lax.all_to_all(copies, 'expert', 0, 0, axis_index_groups=circles, tiled=T...  12.7 us
    ppermute x3, waiting for transfers between devices, mirrored(): lax.ppermute(value, 'pipe', [(q, q ^ sections // 2) for q in range(sectio...  8.74 us
    pallas_call x2, Pallas kernels, in_vmem(): pl.pallas_call(kernel, in_specs=[vmem] * len(operands), out_specs=vmem, o...  5.4 us
    unnamed x22, local copies, waits for them, and re-layouts  4.79 us
  transfers between devices with their start and end apart: 14, of which 6 were waited for; matrix products, arithmetic and copies ran while one was open for 8% of the time, Pallas kernels for 4%

profile of v5, /device:TPU:1, one launch (start us, length us, event | category | flops | bytes accessed | tf_op | source)
XLA Modules:
  0.0 143.6 jit_solution(4265356133087390439)
XLA Ops:
  0.6 2.8 %pick.1 = (bf16[32,3584]{1,0:T(8,128)(2,1)}, bf16[32,3584]{1,0:T(8,128)(2,1)}) custom-call(s32[1]{0:T(128)} %bitcast.side_ref, bf16[128,3584]{1,0:T(8,128)(2,1)} %bitcast.28, bf16[128,3584]{1,0:T(8,128)(2,1)} %bitcast.29, s32[2,128]{1,0:T(2,128)} %bitcast.34, f32[2,128]{1,0:T(2,128)} %bitcast.35), custom_call_target="tpu_custom_call" | custom-call | tf_op jit(solution)/shard_map/pick/pallas_call | solution.py:51
  3.4 5.7 %collective-permute-start = (bf16[32,3584]{1,0:T(8,128)(2,1)}, bf16[32,3584]{1,0:T(8,128)(2,1)S(1)}, u32[]{:S(2)}, u32[]{:S(2)}) collective-permute-start(bf16[32,3584]{1,0:T(8,128)(2,1)} %get-tuple-element.26), channel_id=1, source_target_pairs={{0,16},{1,17},{2,18},{3,19},{4,20},{5,21},{6,22},{7,23},{8,24},{9,... | collective-permute-start | bytes 688136 | tf_op jit(solution)/shard_map/far/ppermute | solution.py:108
  9.2 3.6 %collective-permute-start.6 = (bf16[32,3584]{1,0:T(8,128)(2,1)}, bf16[32,3584]{1,0:T(8,128)(2,1)}, u32[]{:S(2)}, u32[]{:S(2)}) collective-permute-start(bf16[32,3584]{1,0:T(8,128)(2,1)} %get-tuple-element.25), channel_id=1, source_target_pairs={{0,8},{1,9},{2,10},{3,11},{4,12},{5,13},{6,14},{7,15},{8,0},{9,1},... | collective-permute-start | bytes 688136 | tf_op jit(solution)/shard_map/beside/ppermute | solution.py:108
  12.7 3.4 %collective-permute-start.2 = (bf16[3584,128]{1,0:T(8,128)(2,1)S(1)}, bf16[3584,128]{1,0:T(8,128)(2,1)}, u32[]{:S(2)}, u32[]{:S(2)}) collective-permute-start(bf16[3584,128]{1,0:T(8,128)(2,1)S(1)} %copy-done.2), channel_id=1, source_target_pairs={{0,1},{1,0},{2,3},{3,2},{4,5},{5,4},{6,7},{7,6},{8,9},{9,8},{10,11... | collective-permute-start | bytes 2752520 | tf_op jit(solution)/shard_map/weight_up/ppermute | solution.py:108
  16.1 1.9 %collective-permute-start.3 = (bf16[128,3584]{1,0:T(8,128)(2,1)}, bf16[128,3584]{1,0:T(8,128)(2,1)}, u32[]{:S(2)}, u32[]{:S(2)}) collective-permute-start(bf16[128,3584]{1,0:T(8,128)(2,1)} %down_mine.3), channel_id=1, source_target_pairs={{0,1},{1,0},{2,3},{3,2},{4,5},{5,4},{6,7},{7,6},{8,9},{9,8},{10,11... | collective-permute-start | bytes 2752520 | tf_op jit(solution)/shard_map/weight_down/ppermute | solution.py:108
  18.0 1.0 fusion.32
  19.1 1.4 broadcast_in_dim.31
  20.5 4.6 %all-to-all-start = ((bf16[4,64,3584]{2,1,0:T(8,128)(2,1)}), bf16[4,64,3584]{2,1,0:T(8,128)(2,1)S(1)}, u32[]{:S(2)}, u32[]{:S(2)}) async-start(bf16[4,64,3584]{2,1,0:T(8,128)(2,1)} %broadcast_in_dim.31), calls=%async_computation | async-start | bytes 3670016 | tf_op jit(solution)/shard_map/near_ring/all_to_all | solution.py:135
  25.1 3.2 %collective-permute-start.1 = (bf16[32,3584]{1,0:T(8,128)(2,1)S(1)}, bf16[32,3584]{1,0:T(8,128)(2,1)S(1)}, u32[]{:S(2)}, u32[]{:S(2)}) collective-permute-start(bf16[32,3584]{1,0:T(8,128)(2,1)S(1)} %collective-permute-done), channel_id=1, source_target_pairs={{0,8},{1,9},{2,10},{3,11},{4,12},{5,13},{6,14},{7,15},{8,0},{9,1},... | collective-permute-start | bytes 688136 | tf_op jit(solution)/shard_map/far_beside/ppermute | solution.py:108
  28.3 1.0 fusion.30
  30.0 2.5 %collective-permute-done.1 = bf16[32,3584]{1,0:T(8,128)(2,1)S(1)} collective-permute-done((bf16[32,3584]{1,0:T(8,128)(2,1)S(1)}, bf16[32,3584]{1,0:T(8,128)(2,1)S(1)}, u32[]{:S(2)}, u32[]{:S(2)}) %collective-permute-start.1) | collective-permute-done | bytes 229408 | tf_op jit(solution)/shard_map/far_beside/ppermute | solution.py:108
  32.6 14.5 %all-to-all-done.rows = bf16[4,64,3584]{2,1,0:T(8,128)(2,1)S(1)} async-done(((bf16[4,64,3584]{2,1,0:T(8,128)(2,1)}), bf16[4,64,3584]{2,1,0:T(8,128)(2,1)S(1)}, u32[]{:S(2)}, u32[]{:S(2)}) %all-to-all-start) | async-done | bytes 1835040 | tf_op jit(solution)/shard_map/near_ring/all_to_all | solution.py:135
  47.1 1.5 %broadcast_in_dim.32 = bf16[4,64,3584]{2,1,0:T(8,128)(2,1)} broadcast(bf16[64,3584]{1,0:T(8,128)(2,1)S(1)} %pad_maximum_fusion.1), dimensions={1,2} | broadcast | bytes 2293760 | tf_op jit(solution)/shard_map/broadcast_in_dim | solution.py:131
  48.9 3.6 %all-to-all-start.1 = ((bf16[4,64,3584]{2,1,0:T(8,128)(2,1)}), bf16[4,64,3584]{2,1,0:T(8,128)(2,1)S(1)}, u32[]{:S(2)}, u32[]{:S(2)}) async-start(bf16[4,64,3584]{2,1,0:T(8,128)(2,1)} %broadcast_in_dim.32), calls=%async_computation.1 | async-start | bytes 3670016 | tf_op jit(solution)/shard_map/pair_ring/all_to_all | solution.py:135
  52.5 15.3 %collective-permute-start.4 = (bf16[64,1792]{1,0:T(8,128)(2,1)S(1)}, bf16[64,1792]{1,0:T(8,128)(2,1)S(1)}, u32[]{:S(2)}, u32[]{:S(2)}) collective-permute-start(bf16[64,1792]{1,0:T(8,128)(2,1)S(1)} %copy-done.5), channel_id=1, source_target_pairs={{0,256},{32,288},{64,320},{96,352},{128,384},{160,416},{192,448},{... | collective-permute-start | bytes 688136 | tf_op jit(solution)/shard_map/rows_mirror/ppermute | solution.py:112
  67.9 1.5 %copy-done.1 = bf16[4,64,3584]{2,1,0:T(8,128)(2,1)S(1)} copy-done((bf16[4,64,3584]{2,1,0:T(8,128)(2,1)S(1)}, bf16[4,64,3584]{2,1,0:T(8,128)(2,1)}, u32[]{:S(2)}) %copy-start.1) | copy-done | bytes 1835032
  69.4 2.7 %near_units.1 = bf16[256,256]{1,0:T(8,128)(2,1)S(1)} custom-call(bf16[4,64,3584]{2,1,0:T(8,128)(2,1)S(1)} %copy-done.1, bf16[3584,128]{1,0:T(8,128)(2,1)S(1)} %copy-done.2, bf16[3584,128]{1,0:T(8,128)(2,1)} %collective-permute-done.2.up_other, bf16[128,3584]{1,0:T(8,128)(2,1)} %down_mine.3, bf16[128,3584]{1,0:T(8,128)(2,1)} %collective-permute-done.3.down_other), custom_call_target="tpu_custom_call" | custom-call | tf_op jit(solution)/shard_map/near_units/pallas_call | solution.py:87
  72.1 1.9 %collective-permute-start.7 = (bf16[256,256]{1,0:T(8,128)(2,1)S(1)}, bf16[256,256]{1,0:T(8,128)(2,1)}, u32[]{:S(2)}, u32[]{:S(2)}) collective-permute-start(bf16[256,256]{1,0:T(8,128)(2,1)S(1)} %near_units.1), channel_id=1, source_target_pairs={{0,256},{32,288},{64,320},{96,352},{128,384},{160,416},{192,448},{... | collective-permute-start | bytes 393224 | tf_op jit(solution)/shard_map/units_near/ppermute | solution.py:112
  74.0 1.9 %collective-permute-start.5 = (bf16[64,1792]{1,0:T(8,128)(2,1)S(1)}, bf16[64,1792]{1,0:T(8,128)(2,1)S(1)}, u32[]{:S(2)}, u32[]{:S(2)}) collective-permute-start(bf16[64,1792]{1,0:T(8,128)(2,1)S(1)} %collective-permute-done.4), channel_id=1, source_target_pairs={{0,8},{1,9},{2,10},{3,11},{4,12},{5,13},{6,14},{7,15},{8,0},{9,1},... | collective-permute-start | bytes 688136 | tf_op jit(solution)/shard_map/pair_m/ppermute | solution.py:108
  78.2 2.7 %pair_units.1 = bf16[256,256]{1,0:T(8,128)(2,1)S(1)} custom-call(bf16[4,64,3584]{2,1,0:T(8,128)(2,1)S(1)} %all-to-all-done.1.rows, bf16[3584,128]{1,0:T(8,128)(2,1)S(1)} %copy-done.2, bf16[3584,128]{1,0:T(8,128)(2,1)} %collective-permute-done.2.up_other, bf16[128,3584]{1,0:T(8,128)(2,1)} %down_mine.3, bf16[128,3584]{1,0:T(8,128)(2,1)} %collective-permute-done.3.down_other), custom_call_target="tpu_custom_call" | custom-call | tf_op jit(solution)/shard_map/pair_units/pallas_call | solution.py:87
  81.0 20.9 %collective-permute-done.5 = bf16[64,1792]{1,0:T(8,128)(2,1)S(1)} collective-permute-done((bf16[64,1792]{1,0:T(8,128)(2,1)S(1)}, bf16[64,1792]{1,0:T(8,128)(2,1)S(1)}, u32[]{:S(2)}, u32[]{:S(2)}) %collective-permute-start.5) | collective-permute-done | bytes 229408 | tf_op jit(solution)/shard_map/pair_m/ppermute | solution.py:108
  101.9 1.4 broadcast_in_dim.33
  103.3 4.5 %all-to-all-start.2 = ((bf16[4,128,1792]{2,1,0:T(8,128)(2,1)}), bf16[4,128,1792]{2,1,0:T(8,128)(2,1)}, u32[]{:S(2)}, u32[]{:S(2)}) async-start(bf16[4,128,1792]{2,1,0:T(8,128)(2,1)} %broadcast_in_dim.33), calls=%async_computation.2 | async-start | bytes 3670016 | tf_op jit(solution)/shard_map/mirror_ring/all_to_all | solution.py:135
  107.7 4.4 %collective-permute-start.8 = (bf16[256,256]{1,0:T(8,128)(2,1)S(1)}, bf16[256,256]{1,0:T(8,128)(2,1)S(1)}, u32[]{:S(2)}, u32[]{:S(2)}) collective-permute-start(bf16[256,256]{1,0:T(8,128)(2,1)S(1)} %pair_units.1), channel_id=1, source_target_pairs={{0,256},{32,288},{64,320},{96,352},{128,384},{160,416},{192,448},{... | collective-permute-start | bytes 393224 | tf_op jit(solution)/shard_map/units_pair/ppermute | solution.py:112
  113.7 8.7 %collective-permute-done.8 = bf16[256,256]{1,0:T(8,128)(2,1)S(1)} collective-permute-done((bf16[256,256]{1,0:T(8,128)(2,1)S(1)}, bf16[256,256]{1,0:T(8,128)(2,1)S(1)}, u32[]{:S(2)}, u32[]{:S(2)}) %collective-permute-start.8) | collective-permute-done | bytes 131104 | tf_op jit(solution)/shard_map/units_pair/ppermute | solution.py:112
  123.1 5.9 %all-to-all-done.2 = bf16[4,128,1792]{2,1,0:T(8,128)(2,1)} async-done(((bf16[4,128,1792]{2,1,0:T(8,128)(2,1)}), bf16[4,128,1792]{2,1,0:T(8,128)(2,1)}, u32[]{:S(2)}, u32[]{:S(2)}) %all-to-all-start.2) | async-done | bytes 1835040 | tf_op jit(solution)/shard_map/mirror_ring/all_to_all | solution.py:135
  129.1 1.6 %fusion.29 = (bf16[4,32,1792]{2,1,0:T(8,128)(2,1)S(1)}, bf16[4,32,1792]{2,1,0:T(8,128)(2,1)S(1)}, bf16[4,32,1792]{2,1,0:T(8,128)(2,1)S(1)}, bf16[4,32,1792]{2,1,0:T(8,128)(2,1)S(1)}) fusion(bf16[4,128,1792]{2,1,0:T(8,128)(2,1)} %all-to-all-done.2), kind=kLoop, calls=%fused_computation.47 | loop fusion | bytes 3670016 | tf_op jit(solution)/shard_map/slice | solution.py:185
  130.7 0.9 fusion.36
  132.4 5.8 %collective-permute-start.9 = (bf16[1792,128]{1,0:T(8,128)(2,1)S(1)}, bf16[1792,128]{1,0:T(8,128)(2,1)S(1)}, u32[]{:S(2)}, u32[]{:S(2)}) collective-permute-start(bf16[1792,128]{1,0:T(8,128)(2,1)S(1)} %slice.119), channel_id=1, source_target_pairs={{0,1},{1,0},{2,3},{3,2},{4,5},{5,4},{6,7},{7,6},{8,9},{9,8},{10,11... | collective-permute-start | bytes 1376264 | tf_op jit(solution)/shard_map/up_swap/ppermute | solution.py:108
  139.0 1.9 %collective-permute-start.10 = (bf16[128,1792]{1,0:T(8,128)(2,1)S(1)}, bf16[128,1792]{1,0:T(8,128)(2,1)S(1)}, u32[]{:S(2)}, u32[]{:S(2)}) collective-permute-start(bf16[128,1792]{1,0:T(8,128)(2,1)S(1)} %slice.118), channel_id=1, source_target_pairs={{0,1},{1,0},{2,3},{3,2},{4,5},{5,4},{6,7},{7,6},{8,9},{9,8},{10,11... | collective-permute-start | bytes 1376264 | tf_op jit(solution)/shard_map/down_swap/ppermute | solution.py:108
  140.9 0.9 fusion.10
  141.8 0.9 collective-permute-done.10
  (47 shorter events, 8.1 us)
Async XLA Ops:
  0.6 12.1 %copy-start.2 = (bf16[3584,128]{1,0:T(8,128)(2,1)S(1)}, bf16[3584,128]{1,0:T(8,128)(2,1)}, u32[]{:S(2)}) copy-start(bf16[3584,128]{1,0:T(8,128)(2,1)} %up_mine.3) | copy-start | bytes 2752516
  3.4 15.6 %collective-permute-start = (bf16[32,3584]{1,0:T(8,128)(2,1)}, bf16[32,3584]{1,0:T(8,128)(2,1)S(1)}, u32[]{:S(2)}, u32[]{:S(2)}) collective-permute-start(bf16[32,3584]{1,0:T(8,128)(2,1)} %get-tuple-element.26), channel_id=1, source_target_pairs={{0,16},{1,17},{2,18},{3,19},{4,20},{5,21},{6,22},{7,23},{8,24},{9,... | collective-permute-start | bytes 688136 | tf_op jit(solution)/shard_map/far/ppermute | solution.py:108
  9.2 19.1 %collective-permute-start.6 = (bf16[32,3584]{1,0:T(8,128)(2,1)}, bf16[32,3584]{1,0:T(8,128)(2,1)}, u32[]{:S(2)}, u32[]{:S(2)}) collective-permute-start(bf16[32,3584]{1,0:T(8,128)(2,1)} %get-tuple-element.25), channel_id=1, source_target_pairs={{0,8},{1,9},{2,10},{3,11},{4,12},{5,13},{6,14},{7,15},{8,0},{9,1},... | collective-permute-start | bytes 688136 | tf_op jit(solution)/shard_map/beside/ppermute | solution.py:108
  12.7 19.8 %collective-permute-start.2 = (bf16[3584,128]{1,0:T(8,128)(2,1)S(1)}, bf16[3584,128]{1,0:T(8,128)(2,1)}, u32[]{:S(2)}, u32[]{:S(2)}) collective-permute-start(bf16[3584,128]{1,0:T(8,128)(2,1)S(1)} %copy-done.2), channel_id=1, source_target_pairs={{0,1},{1,0},{2,3},{3,2},{4,5},{5,4},{6,7},{7,6},{8,9},{9,8},{10,11... | collective-permute-start | bytes 2752520 | tf_op jit(solution)/shard_map/weight_up/ppermute | solution.py:108
  16.1 16.4 %collective-permute-start.3 = (bf16[128,3584]{1,0:T(8,128)(2,1)}, bf16[128,3584]{1,0:T(8,128)(2,1)}, u32[]{:S(2)}, u32[]{:S(2)}) collective-permute-start(bf16[128,3584]{1,0:T(8,128)(2,1)} %down_mine.3), channel_id=1, source_target_pairs={{0,1},{1,0},{2,3},{3,2},{4,5},{5,4},{6,7},{7,6},{8,9},{9,8},{10,11... | collective-permute-start | bytes 2752520 | tf_op jit(solution)/shard_map/weight_down/ppermute | solution.py:108
  20.5 26.6 %all-to-all-start = ((bf16[4,64,3584]{2,1,0:T(8,128)(2,1)}), bf16[4,64,3584]{2,1,0:T(8,128)(2,1)S(1)}, u32[]{:S(2)}, u32[]{:S(2)}) async-start(bf16[4,64,3584]{2,1,0:T(8,128)(2,1)} %broadcast_in_dim.31), calls=%async_computation | async-start | bytes 3670016 | tf_op jit(solution)/shard_map/near_ring/all_to_all | solution.py:135
  25.1 7.4 %collective-permute-start.1 = (bf16[32,3584]{1,0:T(8,128)(2,1)S(1)}, bf16[32,3584]{1,0:T(8,128)(2,1)S(1)}, u32[]{:S(2)}, u32[]{:S(2)}) collective-permute-start(bf16[32,3584]{1,0:T(8,128)(2,1)S(1)} %collective-permute-done), channel_id=1, source_target_pairs={{0,8},{1,9},{2,10},{3,11},{4,12},{5,13},{6,14},{7,15},{8,0},{9,1},... | collective-permute-start | bytes 688136 | tf_op jit(solution)/shard_map/far_beside/ppermute | solution.py:108
  47.1 1.8 %copy-start = (bf16[4,64,3584]{2,1,0:T(8,128)(2,1)}, bf16[4,64,3584]{2,1,0:T(8,128)(2,1)S(1)}, u32[]{:S(2)}) copy-start(bf16[4,64,3584]{2,1,0:T(8,128)(2,1)S(1)} %all-to-all-done.rows) | copy-start | bytes 5505028
  48.6 4.0 %copy-start.5 = (bf16[64,1792]{1,0:T(8,128)(2,1)S(1)}, bf16[64,1792]{1,0:T(8,128)(2,1)}, u32[]{:S(2)}) copy-start(bf16[64,1792]{1,0:T(8,128)(2,1)} %constant_dynamic-slice_fusion.4) | copy-start | bytes 688132
  48.9 29.3 %all-to-all-start.1 = ((bf16[4,64,3584]{2,1,0:T(8,128)(2,1)}), bf16[4,64,3584]{2,1,0:T(8,128)(2,1)S(1)}, u32[]{:S(2)}, u32[]{:S(2)}) async-start(bf16[4,64,3584]{2,1,0:T(8,128)(2,1)} %broadcast_in_dim.32), calls=%async_computation.1 | async-start | bytes 3670016 | tf_op jit(solution)/shard_map/pair_ring/all_to_all | solution.py:135
  52.5 21.5 %collective-permute-start.4 = (bf16[64,1792]{1,0:T(8,128)(2,1)S(1)}, bf16[64,1792]{1,0:T(8,128)(2,1)S(1)}, u32[]{:S(2)}, u32[]{:S(2)}) collective-permute-start(bf16[64,1792]{1,0:T(8,128)(2,1)S(1)} %copy-done.5), channel_id=1, source_target_pairs={{0,256},{32,288},{64,320},{96,352},{128,384},{160,416},{192,448},{... | collective-permute-start | bytes 688136 | tf_op jit(solution)/shard_map/rows_mirror/ppermute | solution.py:112
  67.9 1.5 %copy-start.1 = (bf16[4,64,3584]{2,1,0:T(8,128)(2,1)S(1)}, bf16[4,64,3584]{2,1,0:T(8,128)(2,1)}, u32[]{:S(2)}) copy-start(bf16[4,64,3584]{2,1,0:T(8,128)(2,1)} %copy-done) | copy-start | bytes 5505028
  72.1 41.6 %collective-permute-start.7 = (bf16[256,256]{1,0:T(8,128)(2,1)S(1)}, bf16[256,256]{1,0:T(8,128)(2,1)}, u32[]{:S(2)}, u32[]{:S(2)}) collective-permute-start(bf16[256,256]{1,0:T(8,128)(2,1)S(1)} %near_units.1), channel_id=1, source_target_pairs={{0,256},{32,288},{64,320},{96,352},{128,384},{160,416},{192,448},{... | collective-permute-start | bytes 393224 | tf_op jit(solution)/shard_map/units_near/ppermute | solution.py:112
  74.0 27.8 %collective-permute-start.5 = (bf16[64,1792]{1,0:T(8,128)(2,1)S(1)}, bf16[64,1792]{1,0:T(8,128)(2,1)S(1)}, u32[]{:S(2)}, u32[]{:S(2)}) collective-permute-start(bf16[64,1792]{1,0:T(8,128)(2,1)S(1)} %collective-permute-done.4), channel_id=1, source_target_pairs={{0,8},{1,9},{2,10},{3,11},{4,12},{5,13},{6,14},{7,15},{8,0},{9,1},... | collective-permute-start | bytes 688136 | tf_op jit(solution)/shard_map/pair_m/ppermute | solution.py:108
  103.3 25.8 %all-to-all-start.2 = ((bf16[4,128,1792]{2,1,0:T(8,128)(2,1)}), bf16[4,128,1792]{2,1,0:T(8,128)(2,1)}, u32[]{:S(2)}, u32[]{:S(2)}) async-start(bf16[4,128,1792]{2,1,0:T(8,128)(2,1)} %broadcast_in_dim.33), calls=%async_computation.2 | async-start | bytes 3670016 | tf_op jit(solution)/shard_map/mirror_ring/all_to_all | solution.py:135
  107.7 14.7 %collective-permute-start.8 = (bf16[256,256]{1,0:T(8,128)(2,1)S(1)}, bf16[256,256]{1,0:T(8,128)(2,1)S(1)}, u32[]{:S(2)}, u32[]{:S(2)}) collective-permute-start(bf16[256,256]{1,0:T(8,128)(2,1)S(1)} %pair_units.1), channel_id=1, source_target_pairs={{0,256},{32,288},{64,320},{96,352},{128,384},{160,416},{192,448},{... | collective-permute-start | bytes 393224 | tf_op jit(solution)/shard_map/units_pair/ppermute | solution.py:112
  113.7 17.9 %copy-start.4 = (bf16[4,32,1792]{2,1,0:T(8,128)(2,1)S(1)}, bf16[4,32,1792]{2,1,0:T(8,128)(2,1)}, u32[]{:S(2)}) copy-start(bf16[4,32,1792]{2,1,0:T(8,128)(2,1)} %get-tuple-element.53) | copy-start | bytes 1376260
  113.7 17.9 %copy-start.8 = (bf16[128,256]{1,0:T(8,128)(2,1)S(1)}, bf16[128,256]{1,0:T(8,128)(2,1)}, u32[]{:S(2)}) copy-start(bf16[128,256]{1,0:T(8,128)(2,1)} %get-tuple-element.63) | copy-start | bytes 196612
  122.5 0.7 copy-start.6
  129.1 1.6 %copy-start.7 = (bf16[256,256]{1,0:T(8,128)(2,1)S(1)}, bf16[256,256]{1,0:T(8,128)(2,1)}, u32[]{:S(2)}) copy-start(bf16[256,256]{1,0:T(8,128)(2,1)} %copy-done.6) | copy-start | bytes 393220
  131.6 6.6 %copy-start.3 = (bf16[512,1792]{1,0:T(8,128)(2,1)S(1)}, bf16[512,1792]{1,0:T(8,128)(2,1)}, u32[]{:S(2)}) copy-start(bf16[512,1792]{1,0:T(8,128)(2,1)} %constant_dynamic-update-slice_fusion.2) | copy-start | bytes 5505028
  132.4 8.6 %collective-permute-start.9 = (bf16[1792,128]{1,0:T(8,128)(2,1)S(1)}, bf16[1792,128]{1,0:T(8,128)(2,1)S(1)}, u32[]{:S(2)}, u32[]{:S(2)}) collective-permute-start(bf16[1792,128]{1,0:T(8,128)(2,1)S(1)} %slice.119), channel_id=1, source_target_pairs={{0,1},{1,0},{2,3},{3,2},{4,5},{5,4},{6,7},{7,6},{8,9},{9,8},{10,11... | collective-permute-start | bytes 1376264 | tf_op jit(solution)/shard_map/up_swap/ppermute | solution.py:108
  139.0 3.7 %collective-permute-start.10 = (bf16[128,1792]{1,0:T(8,128)(2,1)S(1)}, bf16[128,1792]{1,0:T(8,128)(2,1)S(1)}, u32[]{:S(2)}, u32[]{:S(2)}) collective-permute-start(bf16[128,1792]{1,0:T(8,128)(2,1)S(1)} %slice.118), channel_id=1, source_target_pairs={{0,1},{1,0},{2,3},{3,2},{4,5},{5,4},{6,7},{7,6},{8,9},{9,8},{10,11... | collective-permute-start | bytes 1376264 | tf_op jit(solution)/shard_map/down_swap/ppermute | solution.py:108

commit v6 on v5

--- a/solution.py
+++ b/solution.py
@@ -177,7 +177,7 @@
     near_sent, pair_sent, mirror_ring = lax.optimization_barrier((near_sent, pair_sent, mirror_ring))
 
     def own_columns(part, at):
-        return lax.dynamic_slice(part, (0, at, own_start), (4, n, half))
+        return lax.dynamic_slice_in_dim(part[:, at : at + n], own_start, half, 2)
 
     def gathered(at):
         own = [own_columns(near_ring, at)]

time: 144 us -> 134 us (0.931)
  waiting for transfers between devices: 53.5 us -> 29.1 us
  starting transfers between devices: 61.7 us -> 71.4 us
  local copies, waits for them, and re-layouts: 15.9 us -> 17.7 us
    all_to_all x3, waiting for transfers between devices: 20.5 us -> 0.28 us  [around(): lax.all_to_all(copies, 'expert', 0, 0, axis_index_groups=circles, tiled=T...]
    ppermute x3, starting transfers between devices: 21.7 us -> 34.6 us  [mirrored(): lax.ppermute(value, 'pipe', [(q, q ^ sections // 2) for q in range(sectio...]
    ppermute x8, waiting for transfers between devices: 24.3 us -> 13.5 us  [across(): lax.ppermute(value, 'expert', [(s, s ^ flip) for s in range(members)])]
    ppermute x3, waiting for transfers between devices: 8.74 us -> 15.3 us  [mirrored(): lax.ppermute(value, 'pipe', [(q, q ^ sections // 2) for q in range(sectio...]
    unnamed x22, local copies, waits for them, and re-layouts: 4.79 us -> 0.7 us
    ppermute x8, starting transfers between devices: 27.4 us -> 24.1 us  [across(): lax.ppermute(value, 'expert', [(s, s ^ flip) for s in range(members)])]
    slice x0 -> x2, local copies, waits for them, and re-layouts: none -> 3.24 us  [own_columns(): return lax.dynamic_slice_in_dim(part[:, at:at + n], own_start, half, 2)]
    dynamic_slice x1, local copies, waits for them, and re-layouts: 0.01 us -> 1.55 us  [shards(): lax.dynamic_slice(pair_ring, (0, n, own_start), (1, n, half))]
  transfers between devices with their start and end apart: 14 -> 14, of which waited for: 6 -> 5; matrix products, arithmetic and copies ran while one was open for 8% -> 14% of each run, Pallas kernels for 4% -> 4%
where the time goes in v6:
time: 134 us; the launch traced here: 133 us
  starting transfers between devices  71.4 us (53%)
  waiting for transfers between devices  29.1 us (22%)
  local copies, waits for them, and re-layouts  17.7 us (13%)
  Pallas kernels  8.74 us (7%)
  other arithmetic  2.86 us (2%)
  matrix products  2.5 us (2%)
    ppermute x3, starting transfers between devices, mirrored(): lax.ppermute(value, 'pipe', [(q, q ^ sections // 2) for q in range(sectio...  34.6 us
    ppermute x8, starting transfers between devices, across(): lax.ppermute(value, 'expert', [(s, s ^ flip) for s in range(members)])  24.1 us
    ppermute x3, waiting for transfers between devices, mirrored(): lax.ppermute(value, 'pipe', [(q, q ^ sections // 2) for q in range(sectio...  15.3 us
    ppermute x8, waiting for transfers between devices, across(): lax.ppermute(value, 'expert', [(s, s ^ flip) for s in range(members)])  13.5 us
    all_to_all x3, starting transfers between devices, around(): lax.all_to_all(copies, 'expert', 0, 0, axis_index_groups=circles, tiled=T...  12.7 us
    pallas_call x2, Pallas kernels, in_vmem(): pl.pallas_call(kernel, in_specs=[vmem] * len(operands), out_specs=vmem, o...  5.95 us
    broadcast_in_dim x3, local copies, waits for them, and re-layouts, repeated(): return jnp.broadcast_to(block[None], (4, *block.shape))  4.08 us
    slice x2, local copies, waits for them, and re-layouts, own_columns(): return lax.dynamic_slice_in_dim(part[:, at:at + n], own_start, half, 2)  3.24 us
  transfers between devices with their start and end apart: 14, of which 5 were waited for; matrix products, arithmetic and copies ran while one was open for 14% of the time, Pallas kernels for 4%

profile of v6, /device:TPU:1, one launch (start us, length us, event | category | flops | bytes accessed | tf_op | source)
XLA Modules:
  0.0 133.4 jit_solution(8085039721217503709)
XLA Ops:
  0.6 2.8 %pick.1 = (bf16[32,3584]{1,0:T(8,128)(2,1)}, bf16[32,3584]{1,0:T(8,128)(2,1)}) custom-call(s32[1]{0:T(128)} %bitcast.side_ref, bf16[128,3584]{1,0:T(8,128)(2,1)} %bitcast.28, bf16[128,3584]{1,0:T(8,128)(2,1)} %bitcast.29, s32[2,128]{1,0:T(2,128)} %bitcast.34, f32[2,128]{1,0:T(2,128)} %bitcast.35), custom_call_target="tpu_custom_call" | custom-call | tf_op jit(solution)/shard_map/pick/pallas_call | solution.py:51
  3.4 5.7 %collective-permute-start = (bf16[32,3584]{1,0:T(8,128)(2,1)}, bf16[32,3584]{1,0:T(8,128)(2,1)S(1)}, u32[]{:S(2)}, u32[]{:S(2)}) collective-permute-start(bf16[32,3584]{1,0:T(8,128)(2,1)} %get-tuple-element.26), channel_id=1, source_target_pairs={{0,16},{1,17},{2,18},{3,19},{4,20},{5,21},{6,22},{7,23},{8,24},{9,... | collective-permute-start | bytes 688136 | tf_op jit(solution)/shard_map/far/ppermute | solution.py:108
  9.2 3.6 %collective-permute-start.6 = (bf16[32,3584]{1,0:T(8,128)(2,1)}, bf16[32,3584]{1,0:T(8,128)(2,1)}, u32[]{:S(2)}, u32[]{:S(2)}) collective-permute-start(bf16[32,3584]{1,0:T(8,128)(2,1)} %get-tuple-element.25), channel_id=1, source_target_pairs={{0,8},{1,9},{2,10},{3,11},{4,12},{5,13},{6,14},{7,15},{8,0},{9,1},... | collective-permute-start | bytes 688136 | tf_op jit(solution)/shard_map/beside/ppermute | solution.py:108
  12.7 3.4 %collective-permute-start.2 = (bf16[3584,128]{1,0:T(8,128)(2,1)S(1)}, bf16[3584,128]{1,0:T(8,128)(2,1)}, u32[]{:S(2)}, u32[]{:S(2)}) collective-permute-start(bf16[3584,128]{1,0:T(8,128)(2,1)S(1)} %copy-done), channel_id=1, source_target_pairs={{0,1},{1,0},{2,3},{3,2},{4,5},{5,4},{6,7},{7,6},{8,9},{9,8},{10,11... | collective-permute-start | bytes 2752520 | tf_op jit(solution)/shard_map/weight_up/ppermute | solution.py:108
  16.1 1.9 %collective-permute-start.3 = (bf16[128,3584]{1,0:T(8,128)(2,1)}, bf16[128,3584]{1,0:T(8,128)(2,1)}, u32[]{:S(2)}, u32[]{:S(2)}) collective-permute-start(bf16[128,3584]{1,0:T(8,128)(2,1)} %down_mine.3), channel_id=1, source_target_pairs={{0,1},{1,0},{2,3},{3,2},{4,5},{5,4},{6,7},{7,6},{8,9},{9,8},{10,11... | collective-permute-start | bytes 2752520 | tf_op jit(solution)/shard_map/weight_down/ppermute | solution.py:108
  18.0 1.0 fusion.33
  19.1 1.4 %broadcast_in_dim.31 = bf16[4,64,3584]{2,1,0:T(8,128)(2,1)} broadcast(bf16[64,3584]{1,0:T(8,128)(2,1)S(1)} %pad_maximum_fusion), dimensions={1,2} | broadcast | bytes 2293760 | tf_op jit(solution)/shard_map/broadcast_in_dim | solution.py:131
  20.5 4.6 %all-to-all-start = ((bf16[4,64,3584]{2,1,0:T(8,128)(2,1)}), bf16[4,64,3584]{2,1,0:T(8,128)(2,1)S(1)}, u32[]{:S(2)}, u32[]{:S(2)}) async-start(bf16[4,64,3584]{2,1,0:T(8,128)(2,1)} %broadcast_in_dim.31), calls=%async_computation | async-start | bytes 3670016 | tf_op jit(solution)/shard_map/near_ring/all_to_all | solution.py:135
  25.1 3.2 %collective-permute-start.1 = (bf16[32,3584]{1,0:T(8,128)(2,1)}, bf16[32,3584]{1,0:T(8,128)(2,1)S(1)}, u32[]{:S(2)}, u32[]{:S(2)}) collective-permute-start(bf16[32,3584]{1,0:T(8,128)(2,1)} %copy-done.6), channel_id=1, source_target_pairs={{0,8},{1,9},{2,10},{3,11},{4,12},{5,13},{6,14},{7,15},{8,0},{9,1},... | collective-permute-start | bytes 688136 | tf_op jit(solution)/shard_map/far_beside/ppermute | solution.py:108
  28.3 1.0 fusion.31
  30.0 2.8 %collective-permute-done.1 = bf16[32,3584]{1,0:T(8,128)(2,1)S(1)} collective-permute-done((bf16[32,3584]{1,0:T(8,128)(2,1)}, bf16[32,3584]{1,0:T(8,128)(2,1)S(1)}, u32[]{:S(2)}, u32[]{:S(2)}) %collective-permute-start.1) | collective-permute-done | bytes 229408 | tf_op jit(solution)/shard_map/far_beside/ppermute | solution.py:108
  32.8 15.3 %collective-permute-start.4 = (bf16[64,1792]{1,0:T(8,128)(2,1)}, bf16[64,1792]{1,0:T(8,128)(2,1)}, u32[]{:S(2)}, u32[]{:S(2)}) collective-permute-start(bf16[64,1792]{1,0:T(8,128)(2,1)} %constant_dynamic-slice_fusion.4), channel_id=1, source_target_pairs={{0,256},{32,288},{64,320},{96,352},{128,384},{160,416},{192,448},{... | collective-permute-start | bytes 688136 | tf_op jit(solution)/shard_map/rows_mirror/ppermute | solution.py:112
  48.2 1.4 %broadcast_in_dim.32 = bf16[4,64,3584]{2,1,0:T(8,128)(2,1)} broadcast(bf16[64,3584]{1,0:T(8,128)(2,1)S(1)} %pad_maximum_fusion.1), dimensions={1,2} | broadcast | bytes 2293760 | tf_op jit(solution)/shard_map/broadcast_in_dim | solution.py:131
  49.5 4.4 %all-to-all-start.1 = ((bf16[4,64,3584]{2,1,0:T(8,128)(2,1)}), bf16[4,64,3584]{2,1,0:T(8,128)(2,1)}, u32[]{:S(2)}, u32[]{:S(2)}) async-start(bf16[4,64,3584]{2,1,0:T(8,128)(2,1)} %broadcast_in_dim.32), calls=%async_computation.1 | async-start | bytes 3670016 | tf_op jit(solution)/shard_map/pair_ring/all_to_all | solution.py:135
  53.9 2.7 %near_units.1 = bf16[256,256]{1,0:T(8,128)(2,1)S(1)} custom-call(bf16[4,64,3584]{2,1,0:T(8,128)(2,1)S(1)} %all-to-all-done.rows, bf16[3584,128]{1,0:T(8,128)(2,1)S(1)} %copy-done, bf16[3584,128]{1,0:T(8,128)(2,1)} %collective-permute-done.2.up_other, bf16[128,3584]{1,0:T(8,128)(2,1)} %down_mine.3, bf16[128,3584]{1,0:T(8,128)(2,1)} %collective-permute-done.3.down_other), custom_call_target="tpu_custom_call" | custom-call | tf_op jit(solution)/shard_map/near_units/pallas_call | solution.py:87
  56.6 14.3 %collective-permute-start.7 = (bf16[256,256]{1,0:T(8,128)(2,1)S(1)}, bf16[256,256]{1,0:T(8,128)(2,1)}, u32[]{:S(2)}, u32[]{:S(2)}) collective-permute-start(bf16[256,256]{1,0:T(8,128)(2,1)S(1)} %near_units.1), channel_id=1, source_target_pairs={{0,256},{32,288},{64,320},{96,352},{128,384},{160,416},{192,448},{... | collective-permute-start | bytes 393224 | tf_op jit(solution)/shard_map/units_near/ppermute | solution.py:112
  70.9 1.9 %collective-permute-start.5 = (bf16[64,1792]{1,0:T(8,128)(2,1)}, bf16[64,1792]{1,0:T(8,128)(2,1)}, u32[]{:S(2)}, u32[]{:S(2)}) collective-permute-start(bf16[64,1792]{1,0:T(8,128)(2,1)} %collective-permute-done.4), channel_id=1, source_target_pairs={{0,8},{1,9},{2,10},{3,11},{4,12},{5,13},{6,14},{7,15},{8,0},{9,1},... | collective-permute-start | bytes 688136 | tf_op jit(solution)/shard_map/pair_m/ppermute | solution.py:108
  72.9 1.1 fusion.30
  74.9 3.2 %pair_units.1 = bf16[256,256]{1,0:T(8,128)(2,1)S(1)} custom-call(bf16[4,64,3584]{2,1,0:T(8,128)(2,1)} %all-to-all-done.1.rows, bf16[3584,128]{1,0:T(8,128)(2,1)S(1)} %copy-done, bf16[3584,128]{1,0:T(8,128)(2,1)} %collective-permute-done.2.up_other, bf16[128,3584]{1,0:T(8,128)(2,1)} %down_mine.3, bf16[128,3584]{1,0:T(8,128)(2,1)} %collective-permute-done.3.down_other), custom_call_target="tpu_custom_call" | custom-call | tf_op jit(solution)/shard_map/pair_units/pallas_call | solution.py:87
  78.1 9.9 %collective-permute-done.5 = bf16[64,1792]{1,0:T(8,128)(2,1)} collective-permute-done((bf16[64,1792]{1,0:T(8,128)(2,1)}, bf16[64,1792]{1,0:T(8,128)(2,1)}, u32[]{:S(2)}, u32[]{:S(2)}) %collective-permute-start.5) | collective-permute-done | bytes 229408 | tf_op jit(solution)/shard_map/pair_m/ppermute | solution.py:108
  88.0 1.1 pad_maximum_fusion.2
  89.1 1.3 %broadcast_in_dim.33 = bf16[4,128,1792]{2,1,0:T(8,128)(2,1)} broadcast(bf16[128,1792]{1,0:T(8,128)(2,1)S(1)} %pad_maximum_fusion.2), dimensions={1,2} | broadcast | bytes 2293760 | tf_op jit(solution)/shard_map/broadcast_in_dim | solution.py:131
  90.4 1.6 %constant_dynamic-slice_fusion.1 = bf16[1,32,1792]{2,1,0:T(8,128)(2,1)} fusion(bf16[4,64,3584]{2,1,0:T(8,128)(2,1)} %all-to-all-done.1.rows, s32[]{:T(128)S(6)} %mul.7), kind=kLoop, calls=%fused_computation.40 | loop fusion | bytes 229380 | tf_op jit(solution)/shard_map/dynamic_slice | solution.py:174
  91.9 2.2 %slice.92 = bf16[4,32,3584]{2,1,0:T(8,128)(2,1)} slice(bf16[4,64,3584]{2,1,0:T(8,128)(2,1)} %all-to-all-done.1.rows), slice={[0:4], [0:32], [0:3584]} | slice | bytes 1835008 | tf_op jit(solution)/shard_map/slice | solution.py:180
  94.1 3.7 %all-to-all-start.2 = ((bf16[4,128,1792]{2,1,0:T(8,128)(2,1)}), bf16[4,128,1792]{2,1,0:T(8,128)(2,1)S(1)}, u32[]{:S(2)}, u32[]{:S(2)}) async-start(bf16[4,128,1792]{2,1,0:T(8,128)(2,1)} %broadcast_in_dim.33), calls=%async_computation.2 | async-start | bytes 3670016 | tf_op jit(solution)/shard_map/mirror_ring/all_to_all | solution.py:135
  97.9 5.0 %collective-permute-start.8 = (bf16[256,256]{1,0:T(8,128)(2,1)S(1)}, bf16[256,256]{1,0:T(8,128)(2,1)}, u32[]{:S(2)}, u32[]{:S(2)}) collective-permute-start(bf16[256,256]{1,0:T(8,128)(2,1)S(1)} %pair_units.1), channel_id=1, source_target_pairs={{0,256},{32,288},{64,320},{96,352},{128,384},{160,416},{192,448},{... | collective-permute-start | bytes 393224 | tf_op jit(solution)/shard_map/units_pair/ppermute | solution.py:112
  102.9 1.9 %constant_dynamic-slice_fusion = (bf16[4,32,1792]{2,1,0:T(8,128)(2,1)S(1)}, bf16[4,32,1792]{2,1,0:T(8,128)(2,1)}) fusion(bf16[4,32,3584]{2,1,0:T(8,128)(2,1)S(1)} %copy-done.3, s32[]{:T(128)S(6)} %mul.7, bf16[4,32,3584]{2,1,0:T(8,128)(2,1)} %slice.92), kind=kLoop, calls=%fused_computation.39 | loop fusion | bytes 1835012 | tf_op jit(solution)/shard_map/dynamic_slice | solution.py:180
  104.7 1.0 constant_dynamic-slice_fusion.5
  107.1 15.3 %collective-permute-done.8 = bf16[256,256]{1,0:T(8,128)(2,1)} collective-permute-done((bf16[256,256]{1,0:T(8,128)(2,1)S(1)}, bf16[256,256]{1,0:T(8,128)(2,1)}, u32[]{:S(2)}, u32[]{:S(2)}) %collective-permute-start.8) | collective-permute-done | bytes 131104 | tf_op jit(solution)/shard_map/units_pair/ppermute | solution.py:112
  123.6 1.8 %fusion = f32[1792,256]{1,0:T(8,128)S(1)} fusion(bf16[128,1792]{1,0:T(8,128)(2,1)S(1)} %bitcast.30, bf16[128,1792]{1,0:T(8,128)(2,1)S(1)} %bitcast.31, bf16[128,1792]{1,0:T(8,128)(2,1)} %bitcast.33, bf16[128,1792]{1,0:T(8,128)(2,1)S(1)} %bitcast.32, bf16[128,256]{1,0:T(8,128)(2,1)S(1)} %get-tuple-element.72, bf16[128,256]{1,0:T(8,128)(2,1)S(1)} %get-tuple-element.67, ...), kind=kOutput, calls=%fused_computation | convolution fusion | flops 478150656 | bytes 3932160 | tf_op jit(solution)/shard_map/dot_general | solution.py:195
  125.5 2.5 %collective-permute-start.9 = (bf16[1792,128]{1,0:T(8,128)(2,1)S(1)}, bf16[1792,128]{1,0:T(8,128)(2,1)S(1)}, u32[]{:S(2)}, u32[]{:S(2)}) collective-permute-start(bf16[1792,128]{1,0:T(8,128)(2,1)S(1)} %slice.131), channel_id=1, source_target_pairs={{0,1},{1,0},{2,3},{3,2},{4,5},{5,4},{6,7},{7,6},{8,9},{9,8},{10,11... | collective-permute-start | bytes 1376264 | tf_op jit(solution)/shard_map/up_swap/ppermute | solution.py:108
  128.8 1.9 %collective-permute-start.10 = (bf16[128,1792]{1,0:T(8,128)(2,1)S(1)}, bf16[128,1792]{1,0:T(8,128)(2,1)S(1)}, u32[]{:S(2)}, u32[]{:S(2)}) collective-permute-start(bf16[128,1792]{1,0:T(8,128)(2,1)S(1)} %slice.130), channel_id=1, source_target_pairs={{0,1},{1,0},{2,3},{3,2},{4,5},{5,4},{6,7},{7,6},{8,9},{9,8},{10,11... | collective-permute-start | bytes 1376264 | tf_op jit(solution)/shard_map/down_swap/ppermute | solution.py:108
  (49 shorter events, 7.7 us)
Async XLA Ops:
  0.6 12.1 %copy-start = (bf16[3584,128]{1,0:T(8,128)(2,1)S(1)}, bf16[3584,128]{1,0:T(8,128)(2,1)}, u32[]{:S(2)}) copy-start(bf16[3584,128]{1,0:T(8,128)(2,1)} %up_mine.3) | copy-start | bytes 2752516
  3.4 15.6 %collective-permute-start = (bf16[32,3584]{1,0:T(8,128)(2,1)}, bf16[32,3584]{1,0:T(8,128)(2,1)S(1)}, u32[]{:S(2)}, u32[]{:S(2)}) collective-permute-start(bf16[32,3584]{1,0:T(8,128)(2,1)} %get-tuple-element.26), channel_id=1, source_target_pairs={{0,16},{1,17},{2,18},{3,19},{4,20},{5,21},{6,22},{7,23},{8,24},{9,... | collective-permute-start | bytes 688136 | tf_op jit(solution)/shard_map/far/ppermute | solution.py:108
  9.2 19.1 %collective-permute-start.6 = (bf16[32,3584]{1,0:T(8,128)(2,1)}, bf16[32,3584]{1,0:T(8,128)(2,1)}, u32[]{:S(2)}, u32[]{:S(2)}) collective-permute-start(bf16[32,3584]{1,0:T(8,128)(2,1)} %get-tuple-element.25), channel_id=1, source_target_pairs={{0,8},{1,9},{2,10},{3,11},{4,12},{5,13},{6,14},{7,15},{8,0},{9,1},... | collective-permute-start | bytes 688136 | tf_op jit(solution)/shard_map/beside/ppermute | solution.py:108
  12.7 20.0 %collective-permute-start.2 = (bf16[3584,128]{1,0:T(8,128)(2,1)S(1)}, bf16[3584,128]{1,0:T(8,128)(2,1)}, u32[]{:S(2)}, u32[]{:S(2)}) collective-permute-start(bf16[3584,128]{1,0:T(8,128)(2,1)S(1)} %copy-done), channel_id=1, source_target_pairs={{0,1},{1,0},{2,3},{3,2},{4,5},{5,4},{6,7},{7,6},{8,9},{9,8},{10,11... | collective-permute-start | bytes 2752520 | tf_op jit(solution)/shard_map/weight_up/ppermute | solution.py:108
  16.1 16.7 %collective-permute-start.3 = (bf16[128,3584]{1,0:T(8,128)(2,1)}, bf16[128,3584]{1,0:T(8,128)(2,1)}, u32[]{:S(2)}, u32[]{:S(2)}) collective-permute-start(bf16[128,3584]{1,0:T(8,128)(2,1)} %down_mine.3), channel_id=1, source_target_pairs={{0,1},{1,0},{2,3},{3,2},{4,5},{5,4},{6,7},{7,6},{8,9},{9,8},{10,11... | collective-permute-start | bytes 2752520 | tf_op jit(solution)/shard_map/weight_down/ppermute | solution.py:108
  19.0 1.5 %copy-start.6 = (bf16[32,3584]{1,0:T(8,128)(2,1)}, bf16[32,3584]{1,0:T(8,128)(2,1)S(1)}, u32[]{:S(2)}) copy-start(bf16[32,3584]{1,0:T(8,128)(2,1)S(1)} %collective-permute-done) | copy-start | bytes 688132
  20.5 27.7 %all-to-all-start = ((bf16[4,64,3584]{2,1,0:T(8,128)(2,1)}), bf16[4,64,3584]{2,1,0:T(8,128)(2,1)S(1)}, u32[]{:S(2)}, u32[]{:S(2)}) async-start(bf16[4,64,3584]{2,1,0:T(8,128)(2,1)} %broadcast_in_dim.31), calls=%async_computation | async-start | bytes 3670016 | tf_op jit(solution)/shard_map/near_ring/all_to_all | solution.py:135
  25.1 7.6 %collective-permute-start.1 = (bf16[32,3584]{1,0:T(8,128)(2,1)}, bf16[32,3584]{1,0:T(8,128)(2,1)S(1)}, u32[]{:S(2)}, u32[]{:S(2)}) collective-permute-start(bf16[32,3584]{1,0:T(8,128)(2,1)} %copy-done.6), channel_id=1, source_target_pairs={{0,8},{1,9},{2,10},{3,11},{4,12},{5,13},{6,14},{7,15},{8,0},{9,1},... | collective-permute-start | bytes 688136 | tf_op jit(solution)/shard_map/far_beside/ppermute | solution.py:108
  32.8 38.2 %collective-permute-start.4 = (bf16[64,1792]{1,0:T(8,128)(2,1)}, bf16[64,1792]{1,0:T(8,128)(2,1)}, u32[]{:S(2)}, u32[]{:S(2)}) collective-permute-start(bf16[64,1792]{1,0:T(8,128)(2,1)} %constant_dynamic-slice_fusion.4), channel_id=1, source_target_pairs={{0,256},{32,288},{64,320},{96,352},{128,384},{160,416},{192,448},{... | collective-permute-start | bytes 688136 | tf_op jit(solution)/shard_map/rows_mirror/ppermute | solution.py:112
  49.5 25.3 %all-to-all-start.1 = ((bf16[4,64,3584]{2,1,0:T(8,128)(2,1)}), bf16[4,64,3584]{2,1,0:T(8,128)(2,1)}, u32[]{:S(2)}, u32[]{:S(2)}) async-start(bf16[4,64,3584]{2,1,0:T(8,128)(2,1)} %broadcast_in_dim.32), calls=%async_computation.1 | async-start | bytes 3670016 | tf_op jit(solution)/shard_map/pair_ring/all_to_all | solution.py:135
  56.6 50.0 %collective-permute-start.7 = (bf16[256,256]{1,0:T(8,128)(2,1)S(1)}, bf16[256,256]{1,0:T(8,128)(2,1)}, u32[]{:S(2)}, u32[]{:S(2)}) collective-permute-start(bf16[256,256]{1,0:T(8,128)(2,1)S(1)} %near_units.1), channel_id=1, source_target_pairs={{0,256},{32,288},{64,320},{96,352},{128,384},{160,416},{192,448},{... | collective-permute-start | bytes 393224 | tf_op jit(solution)/shard_map/units_near/ppermute | solution.py:112
  70.9 17.0 %collective-permute-start.5 = (bf16[64,1792]{1,0:T(8,128)(2,1)}, bf16[64,1792]{1,0:T(8,128)(2,1)}, u32[]{:S(2)}, u32[]{:S(2)}) collective-permute-start(bf16[64,1792]{1,0:T(8,128)(2,1)} %collective-permute-done.4), channel_id=1, source_target_pairs={{0,8},{1,9},{2,10},{3,11},{4,12},{5,13},{6,14},{7,15},{8,0},{9,1},... | collective-permute-start | bytes 688136 | tf_op jit(solution)/shard_map/pair_m/ppermute | solution.py:108
  94.1 8.8 %copy-start.3 = (bf16[4,32,3584]{2,1,0:T(8,128)(2,1)S(1)}, bf16[4,32,3584]{2,1,0:T(8,128)(2,1)}, u32[]{:S(2)}) copy-start(bf16[4,32,3584]{2,1,0:T(8,128)(2,1)} %get-tuple-element.52) | copy-start | bytes 2752516
  94.1 28.3 %all-to-all-start.2 = ((bf16[4,128,1792]{2,1,0:T(8,128)(2,1)}), bf16[4,128,1792]{2,1,0:T(8,128)(2,1)S(1)}, u32[]{:S(2)}, u32[]{:S(2)}) async-start(bf16[4,128,1792]{2,1,0:T(8,128)(2,1)} %broadcast_in_dim.33), calls=%async_computation.2 | async-start | bytes 3670016 | tf_op jit(solution)/shard_map/mirror_ring/all_to_all | solution.py:135
  97.8 7.9 %copy-start.4 = (bf16[1,32,1792]{2,1,0:T(8,128)(2,1)S(1)}, bf16[1,32,1792]{2,1,0:T(8,128)(2,1)}, u32[]{:S(2)}) copy-start(bf16[1,32,1792]{2,1,0:T(8,128)(2,1)} %constant_dynamic-slice_fusion.1) | copy-start | bytes 344068
  97.9 24.6 %collective-permute-start.8 = (bf16[256,256]{1,0:T(8,128)(2,1)S(1)}, bf16[256,256]{1,0:T(8,128)(2,1)}, u32[]{:S(2)}, u32[]{:S(2)}) collective-permute-start(bf16[256,256]{1,0:T(8,128)(2,1)S(1)} %pair_units.1), channel_id=1, source_target_pairs={{0,256},{32,288},{64,320},{96,352},{128,384},{160,416},{192,448},{... | collective-permute-start | bytes 393224 | tf_op jit(solution)/shard_map/units_pair/ppermute | solution.py:112
  105.8 1.3 copy-start.1
  107.1 16.4 %copy-start.7 = (bf16[128,256]{1,0:T(8,128)(2,1)S(1)}, bf16[128,256]{1,0:T(8,128)(2,1)}, u32[]{:S(2)}) copy-start(bf16[128,256]{1,0:T(8,128)(2,1)} %get-tuple-element.63) | copy-start | bytes 196612
  107.1 16.4 %copy-start.8 = (bf16[128,256]{1,0:T(8,128)(2,1)S(1)}, bf16[128,256]{1,0:T(8,128)(2,1)}, u32[]{:S(2)}) copy-start(bf16[128,256]{1,0:T(8,128)(2,1)} %get-tuple-element.65) | copy-start | bytes 196612
  123.6 4.5 %copy-start.2 = (bf16[512,1792]{1,0:T(8,128)(2,1)S(1)}, bf16[512,1792]{1,0:T(8,128)(2,1)}, u32[]{:S(2)}) copy-start(bf16[512,1792]{1,0:T(8,128)(2,1)} %copy-done.1) | copy-start | bytes 5505028
  125.4 2.7 %copy-start.5 = (bf16[128,256]{1,0:T(8,128)(2,1)S(1)}, bf16[128,256]{1,0:T(8,128)(2,1)}, u32[]{:S(2)}) copy-start(bf16[128,256]{1,0:T(8,128)(2,1)} %get-tuple-element.64) | copy-start | bytes 196612
  125.5 5.3 %collective-permute-start.9 = (bf16[1792,128]{1,0:T(8,128)(2,1)S(1)}, bf16[1792,128]{1,0:T(8,128)(2,1)S(1)}, u32[]{:S(2)}, u32[]{:S(2)}) collective-permute-start(bf16[1792,128]{1,0:T(8,128)(2,1)S(1)} %slice.131), channel_id=1, source_target_pairs={{0,1},{1,0},{2,3},{3,2},{4,5},{5,4},{6,7},{7,6},{8,9},{9,8},{10,11... | collective-permute-start | bytes 1376264 | tf_op jit(solution)/shard_map/up_swap/ppermute | solution.py:108
  128.8 3.7 %collective-permute-start.10 = (bf16[128,1792]{1,0:T(8,128)(2,1)S(1)}, bf16[128,1792]{1,0:T(8,128)(2,1)S(1)}, u32[]{:S(2)}, u32[]{:S(2)}) collective-permute-start(bf16[128,1792]{1,0:T(8,128)(2,1)S(1)} %slice.130), channel_id=1, source_target_pairs={{0,1},{1,0},{2,3},{3,2},{4,5},{5,4},{6,7},{7,6},{8,9},{9,8},{10,11... | collective-permute-start | bytes 1376264 | tf_op jit(solution)/shard_map/down_swap/ppermute | solution.py:108

commit v7 on v4

--- a/solution.py
+++ b/solution.py
@@ -62,37 +62,53 @@
 STEP = 512
 
 
-def rows_to_units(rows, up_mine, up_other, down_mine, down_other, units):
+def rows_to_units(rows, up_mine, up_other, down_mine, down_other, units, up_sum, grad_sum):
+    parts, tall, _ = rows.shape
+    n = tall // 2
+    step = pl.program_id(0)
+    wide_up = jnp.concatenate([up_mine[...], up_other[...]], axis=1)
+    wide_down = jnp.concatenate([down_mine[...], down_other[...]], axis=0)
+    rows_t = jnp.concatenate([rows[k, :n] for k in range(parts)], axis=0)
+    rows_g = jnp.concatenate([rows[k, n:] for k in range(parts)], axis=0)
+    more_up = jnp.dot(rows_t, wide_up, preferred_element_type=FL)
+    more_grad = lax.dot_general(rows_g, wide_down, (((1,), (1,)), ((), ())), preferred_element_type=FL)
+
+    @pl.when(step == 0)
+    def _():
+        up_sum[...] = more_up
+        grad_sum[...] = more_grad
+
+    @pl.when(step > 0)
+    def _():
+        up_sum[...] += more_up
+        grad_sum[...] += more_grad
+
+    @pl.when(step == pl.num_programs(0) - 1)
+    def _():
+        up = up_sum[...]
+        sigma = 1.0 / (1.0 + jnp.exp(-up))
+        slots = up.shape[0]
+        units[:slots] = (up * sigma).astype(BF)
+        units[slots:] = (grad_sum[...] * sigma * (1.0 + up * (1.0 - sigma))).astype(BF)
+
+
+def contracted(name, shape, rows, *weights):
     parts, tall, width = rows.shape
-    n = tall // 2
-    up = grad = None
-    for at in range(0, width, STEP):
-        span = slice(at, at + STEP)
-        wide_up = jnp.concatenate([up_mine[span], up_other[span]], axis=1)
-        wide_down = jnp.concatenate([down_mine[:, span], down_other[:, span]], axis=0)
-        rows_t = jnp.concatenate([rows[k, :n, span] for k in range(parts)], axis=0)
-        rows_g = jnp.concatenate([rows[k, n:, span] for k in range(parts)], axis=0)
-        more_up = jnp.dot(rows_t, wide_up, preferred_element_type=FL)
-        more_grad = lax.dot_general(rows_g, wide_down, (((1,), (1,)), ((), ())), preferred_element_type=FL)
-        up = more_up if up is None else up + more_up
-        grad = more_grad if grad is None else grad + more_grad
-    sigma = 1.0 / (1.0 + jnp.exp(-up))
-    slots = up.shape[0]
-    units[:slots] = (up * sigma).astype(BF)
-    units[slots:] = (grad * sigma * (1.0 + up * (1.0 - sigma))).astype(BF)
-
-
-def in_vmem(kernel, name, shape, *operands):
-    vmem = pl.BlockSpec(memory_space=pltpu.VMEM)
+    hid = weights[0].shape[1]
+    tall_part = pl.BlockSpec((STEP, hid), lambda k: (k, 0))
+    wide_part = pl.BlockSpec((hid, STEP), lambda k: (0, k))
+    total = pltpu.VMEM((shape[0] // 2, shape[1]), FL)
     return pl.pallas_call(
-        kernel,
-        in_specs=[vmem] * len(operands),
-        out_specs=vmem,
+        rows_to_units,
+        grid=(width // STEP,),
+        in_specs=[pl.BlockSpec((parts, tall, STEP), lambda k: (0, 0, k)), tall_part, tall_part, wide_part, wide_part],
+        out_specs=pl.BlockSpec(shape, lambda k: (0, 0)),
         out_shape=jax.ShapeDtypeStruct(shape, BF),
+        scratch_shapes=[total, total],
         name=name,
         cost_estimate=FREE,
         compiler_params=pltpu.CompilerParams(vmem_limit_bytes=20 * 2**20),
-    )(*operands)
+    )(rows, *weights)
 
 
 def shards(tokens, cotangent, routed, gate, up_weight, down_weight):
@@ -156,7 +172,7 @@
     slots = 8 * CAP
 
     def through(name, rows, *weights):
-        return in_vmem(rows_to_units, name, (2 * slots, 2 * hid), rows, *weights)
+        return contracted(name, (2 * slots, 2 * hid), rows, *weights)
 
     near_units = through("near_units", near_ring, up_weight, other_up, down_weight, other_down)
     near_sent = mirrored("units_near", near_units)

time: 132 us -> 135 us (1.023)
  Pallas kernels: 8.76 us -> 14.2 us
  waiting for transfers between devices: 31.7 us -> 29.4 us
    pallas_call x2, Pallas kernels: 5.96 us -> 11.4 us  [contracted(): pl.pallas_call(rows_to_units, grid=(width // STEP,), in_specs=[pl.BlockSp...]
    ppermute x8, waiting for transfers between devices: 13.2 us -> 10.6 us  [across(): lax.ppermute(value, 'expert', [(s, s ^ flip) for s in range(members)])]
  transfers between devices with their start and end apart: 14 -> 14, of which waited for: 5 -> 4; matrix products, arithmetic and copies ran while one was open for 11% -> 11% of each run, Pallas kernels for 5% -> 9%
where the time goes in v7:
time: 135 us; the launch traced here: 134 us
  starting transfers between devices  71.5 us (53%)
  waiting for transfers between devices  29.4 us (22%)
  Pallas kernels  14.2 us (11%)
  local copies, waits for them, and re-layouts  12.6 us (9%)
  other arithmetic  2.85 us (2%)
  matrix products  2.45 us (2%)
    ppermute x3, starting transfers between devices, mirrored(): lax.ppermute(value, 'pipe', [(q, q ^ sections // 2) for q in range(sectio...  34.6 us
    ppermute x8, starting transfers between devices, across(): lax.ppermute(value, 'expert', [(s, s ^ flip) for s in range(members)])  24 us
    ppermute x3, waiting for transfers between devices, mirrored(): lax.ppermute(value, 'pipe', [(q, q ^ sections // 2) for q in range(sectio...  18.8 us
    all_to_all x3, starting transfers between devices, around(): lax.all_to_all(copies, 'expert', 0, 0, axis_index_groups=circles, tiled=T...  12.9 us
    pallas_call x2, Pallas kernels, contracted(): pl.pallas_call(rows_to_units, grid=(width // STEP,), in_specs=[pl.BlockSp...  11.4 us
    ppermute x8, waiting for transfers between devices, across(): lax.ppermute(value, 'expert', [(s, s ^ flip) for s in range(members)])  10.6 us
    broadcast_in_dim x3, local copies, waits for them, and re-layouts, repeated(): return jnp.broadcast_to(block[None], (4, *block.shape))  4.1 us
    pallas_call x1, Pallas kernels, picked(): pl.pallas_call(pick_rows, in_specs=[pl.BlockSpec(memory_space=pltpu.SMEM)...  2.8 us
  transfers between devices with their start and end apart: 14, of which 4 were waited for; matrix products, arithmetic and copies ran while one was open for 11% of the time, Pallas kernels for 9%

profile of v7, /device:TPU:1, one launch (start us, length us, event | category | flops | bytes accessed | tf_op | source)
XLA Modules:
  0.0 133.9 jit_solution(6062740108117301780)
XLA Ops:
  0.6 2.8 %pick.1 = (bf16[32,3584]{1,0:T(8,128)(2,1)}, bf16[32,3584]{1,0:T(8,128)(2,1)}) custom-call(s32[1]{0:T(128)} %bitcast.side_ref, bf16[128,3584]{1,0:T(8,128)(2,1)} %bitcast.21, bf16[128,3584]{1,0:T(8,128)(2,1)} %bitcast.22, s32[2,128]{1,0:T(2,128)} %bitcast.31, f32[2,128]{1,0:T(2,128)} %bitcast.32), custom_call_target="tpu_custom_call" | custom-call | tf_op jit(solution)/shard_map/pick/pallas_call | solution.py:51
  3.4 5.7 %collective-permute-start = (bf16[32,3584]{1,0:T(8,128)(2,1)}, bf16[32,3584]{1,0:T(8,128)(2,1)S(1)}, u32[]{:S(2)}, u32[]{:S(2)}) collective-permute-start(bf16[32,3584]{1,0:T(8,128)(2,1)} %get-tuple-element.26), channel_id=1, source_target_pairs={{0,16},{1,17},{2,18},{3,19},{4,20},{5,21},{6,22},{7,23},{8,24},{9,... | collective-permute-start | bytes 688136 | tf_op jit(solution)/shard_map/far/ppermute | solution.py:124
  9.2 5.0 %collective-permute-start.2 = (bf16[3584,128]{1,0:T(8,128)(2,1)S(1)}, bf16[3584,128]{1,0:T(8,128)(2,1)}, u32[]{:S(2)}, u32[]{:S(2)}) collective-permute-start(bf16[3584,128]{1,0:T(8,128)(2,1)S(1)} %copy-done), channel_id=1, source_target_pairs={{0,1},{1,0},{2,3},{3,2},{4,5},{5,4},{6,7},{7,6},{8,9},{9,8},{10,11... | collective-permute-start | bytes 2752520 | tf_op jit(solution)/shard_map/weight_up/ppermute | solution.py:124
  14.2 1.9 %collective-permute-start.3 = (bf16[128,3584]{1,0:T(8,128)(2,1)}, bf16[128,3584]{1,0:T(8,128)(2,1)}, u32[]{:S(2)}, u32[]{:S(2)}) collective-permute-start(bf16[128,3584]{1,0:T(8,128)(2,1)} %down_mine.3), channel_id=1, source_target_pairs={{0,1},{1,0},{2,3},{3,2},{4,5},{5,4},{6,7},{7,6},{8,9},{9,8},{10,11... | collective-permute-start | bytes 2752520 | tf_op jit(solution)/shard_map/weight_down/ppermute | solution.py:124
  16.1 1.9 %collective-permute-start.6 = (bf16[32,3584]{1,0:T(8,128)(2,1)}, bf16[32,3584]{1,0:T(8,128)(2,1)}, u32[]{:S(2)}, u32[]{:S(2)}) collective-permute-start(bf16[32,3584]{1,0:T(8,128)(2,1)} %get-tuple-element.25), channel_id=1, source_target_pairs={{0,8},{1,9},{2,10},{3,11},{4,12},{5,13},{6,14},{7,15},{8,0},{9,1},... | collective-permute-start | bytes 688136 | tf_op jit(solution)/shard_map/beside/ppermute | solution.py:124
  18.0 1.0 fusion.41
  19.1 1.4 %broadcast_in_dim.31 = bf16[4,64,3584]{2,1,0:T(8,128)(2,1)} broadcast(bf16[64,3584]{1,0:T(8,128)(2,1)S(1)} %pad_maximum_fusion), dimensions={1,2} | broadcast | bytes 2293760 | tf_op jit(solution)/shard_map/broadcast_in_dim | solution.py:147
  20.5 4.6 %all-to-all-start = ((bf16[4,64,3584]{2,1,0:T(8,128)(2,1)}), bf16[4,64,3584]{2,1,0:T(8,128)(2,1)S(1)}, u32[]{:S(2)}, u32[]{:S(2)}) async-start(bf16[4,64,3584]{2,1,0:T(8,128)(2,1)} %broadcast_in_dim.31), calls=%async_computation | async-start | bytes 3670016 | tf_op jit(solution)/shard_map/near_ring/all_to_all | solution.py:151
  25.1 3.2 %collective-permute-start.1 = (bf16[32,3584]{1,0:T(8,128)(2,1)S(1)}, bf16[32,3584]{1,0:T(8,128)(2,1)S(1)}, u32[]{:S(2)}, u32[]{:S(2)}) collective-permute-start(bf16[32,3584]{1,0:T(8,128)(2,1)S(1)} %collective-permute-done), channel_id=1, source_target_pairs={{0,8},{1,9},{2,10},{3,11},{4,12},{5,13},{6,14},{7,15},{8,0},{9,1},... | collective-permute-start | bytes 688136 | tf_op jit(solution)/shard_map/far_beside/ppermute | solution.py:124
  28.3 1.0 fusion.39
  30.0 2.4 %collective-permute-done.1 = bf16[32,3584]{1,0:T(8,128)(2,1)S(1)} collective-permute-done((bf16[32,3584]{1,0:T(8,128)(2,1)S(1)}, bf16[32,3584]{1,0:T(8,128)(2,1)S(1)}, u32[]{:S(2)}, u32[]{:S(2)}) %collective-permute-start.1) | collective-permute-done | bytes 229408 | tf_op jit(solution)/shard_map/far_beside/ppermute | solution.py:124
  32.5 15.4 %collective-permute-start.4 = (bf16[64,1792]{1,0:T(8,128)(2,1)}, bf16[64,1792]{1,0:T(8,128)(2,1)}, u32[]{:S(2)}, u32[]{:S(2)}) collective-permute-start(bf16[64,1792]{1,0:T(8,128)(2,1)} %constant_dynamic-slice_fusion.4), channel_id=1, source_target_pairs={{0,256},{32,288},{64,320},{96,352},{128,384},{160,416},{192,448},{... | collective-permute-start | bytes 688136 | tf_op jit(solution)/shard_map/rows_mirror/ppermute | solution.py:128
  47.9 1.4 %broadcast_in_dim.32 = bf16[4,64,3584]{2,1,0:T(8,128)(2,1)} broadcast(bf16[64,3584]{1,0:T(8,128)(2,1)S(1)} %pad_maximum_fusion.1), dimensions={1,2} | broadcast | bytes 2293760 | tf_op jit(solution)/shard_map/broadcast_in_dim | solution.py:147
  49.3 4.4 %all-to-all-start.1 = ((bf16[4,64,3584]{2,1,0:T(8,128)(2,1)}), bf16[4,64,3584]{2,1,0:T(8,128)(2,1)}, u32[]{:S(2)}, u32[]{:S(2)}) async-start(bf16[4,64,3584]{2,1,0:T(8,128)(2,1)} %broadcast_in_dim.32), calls=%async_computation.1 | async-start | bytes 3670016 | tf_op jit(solution)/shard_map/pair_ring/all_to_all | solution.py:151
  53.7 5.6 %near_units.1 = bf16[256,256]{1,0:T(8,128)(2,1)S(1)} custom-call(bf16[4,64,3584]{2,1,0:T(8,128)(2,1)S(1)} %all-to-all-done.rows, bf16[3584,128]{1,0:T(8,128)(2,1)S(1)} %copy-done, bf16[3584,128]{1,0:T(8,128)(2,1)} %collective-permute-done.2.up_other, bf16[128,3584]{1,0:T(8,128)(2,1)} %down_mine.3, bf16[128,3584]{1,0:T(8,128)(2,1)} %collective-permute-done.3.down_other), custom_call_target="tpu_custom_call" | custom-call | tf_op jit(solution)/shard_map/near_units/pallas_call | solution.py:101
  59.3 14.5 %collective-permute-start.7 = (bf16[256,256]{1,0:T(8,128)(2,1)S(1)}, bf16[256,256]{1,0:T(8,128)(2,1)S(1)}, u32[]{:S(2)}, u32[]{:S(2)}) collective-permute-start(bf16[256,256]{1,0:T(8,128)(2,1)S(1)} %near_units.1), channel_id=1, source_target_pairs={{0,256},{32,288},{64,320},{96,352},{128,384},{160,416},{192,448},{... | collective-permute-start | bytes 393224 | tf_op jit(solution)/shard_map/units_near/ppermute | solution.py:128
  73.8 1.9 %collective-permute-start.5 = (bf16[64,1792]{1,0:T(8,128)(2,1)}, bf16[64,1792]{1,0:T(8,128)(2,1)}, u32[]{:S(2)}, u32[]{:S(2)}) collective-permute-start(bf16[64,1792]{1,0:T(8,128)(2,1)} %collective-permute-done.4), channel_id=1, source_target_pairs={{0,8},{1,9},{2,10},{3,11},{4,12},{5,13},{6,14},{7,15},{8,0},{9,1},... | collective-permute-start | bytes 688136 | tf_op jit(solution)/shard_map/pair_m/ppermute | solution.py:124
  75.9 0.9 constant_dynamic-slice_fusion
  77.4 5.8 %pair_units.1 = bf16[256,256]{1,0:T(8,128)(2,1)S(1)} custom-call(bf16[4,64,3584]{2,1,0:T(8,128)(2,1)} %all-to-all-done.1.rows, bf16[3584,128]{1,0:T(8,128)(2,1)S(1)} %copy-done, bf16[3584,128]{1,0:T(8,128)(2,1)} %collective-permute-done.2.up_other, bf16[128,3584]{1,0:T(8,128)(2,1)} %down_mine.3, bf16[128,3584]{1,0:T(8,128)(2,1)} %collective-permute-done.3.down_other), custom_call_target="tpu_custom_call" | custom-call | tf_op jit(solution)/shard_map/pair_units/pallas_call | solution.py:101
  83.2 7.2 %collective-permute-done.5 = bf16[64,1792]{1,0:T(8,128)(2,1)} collective-permute-done((bf16[64,1792]{1,0:T(8,128)(2,1)}, bf16[64,1792]{1,0:T(8,128)(2,1)}, u32[]{:S(2)}, u32[]{:S(2)}) %collective-permute-start.5) | collective-permute-done | bytes 229408 | tf_op jit(solution)/shard_map/pair_m/ppermute | solution.py:124
  90.4 1.1 pad_maximum_fusion.2
  91.5 1.3 %broadcast_in_dim.33 = bf16[4,128,1792]{2,1,0:T(8,128)(2,1)} broadcast(bf16[128,1792]{1,0:T(8,128)(2,1)S(1)} %pad_maximum_fusion.2), dimensions={1,2} | broadcast | bytes 2293760 | tf_op jit(solution)/shard_map/broadcast_in_dim | solution.py:147
  92.8 3.9 %all-to-all-start.2 = ((bf16[4,128,1792]{2,1,0:T(8,128)(2,1)}), bf16[4,128,1792]{2,1,0:T(8,128)(2,1)S(1)}, u32[]{:S(2)}, u32[]{:S(2)}) async-start(bf16[4,128,1792]{2,1,0:T(8,128)(2,1)} %broadcast_in_dim.33), calls=%async_computation.2 | async-start | bytes 3670016 | tf_op jit(solution)/shard_map/mirror_ring/all_to_all | solution.py:151
  96.7 1.6 %fusion.38 = (bf16[4,32,3584]{2,1,0:T(8,128)(2,1)S(1)}, bf16[4,32,3584]{2,1,0:T(8,128)(2,1)S(1)}) fusion(bf16[4,64,3584]{2,1,0:T(8,128)(2,1)} %all-to-all-done.1.rows), kind=kLoop, calls=%fused_computation.50 | loop fusion | bytes 3670016 | tf_op jit(solution)/shard_map/slice | solution.py:196
  98.3 1.0 constant_dynamic-slice_fusion.1
  99.3 4.7 %collective-permute-start.8 = (bf16[256,256]{1,0:T(8,128)(2,1)S(1)}, bf16[256,256]{1,0:T(8,128)(2,1)S(1)}, u32[]{:S(2)}, u32[]{:S(2)}) collective-permute-start(bf16[256,256]{1,0:T(8,128)(2,1)S(1)} %pair_units.1), channel_id=1, source_target_pairs={{0,256},{32,288},{64,320},{96,352},{128,384},{160,416},{192,448},{... | collective-permute-start | bytes 393224 | tf_op jit(solution)/shard_map/units_pair/ppermute | solution.py:128
  104.7 18.8 %collective-permute-done.8 = bf16[256,256]{1,0:T(8,128)(2,1)S(1)} collective-permute-done((bf16[256,256]{1,0:T(8,128)(2,1)S(1)}, bf16[256,256]{1,0:T(8,128)(2,1)S(1)}, u32[]{:S(2)}, u32[]{:S(2)}) %collective-permute-start.8) | collective-permute-done | bytes 131104 | tf_op jit(solution)/shard_map/units_pair/ppermute | solution.py:128
  124.3 1.8 %fusion.8 = f32[256,1792]{1,0:T(8,128)S(1)} fusion(bf16[128,1792]{1,0:T(8,128)(2,1)S(1)} %bitcast.26, bf16[128,1792]{1,0:T(8,128)(2,1)S(1)} %bitcast.25, bf16[128,1792]{1,0:T(8,128)(2,1)} %bitcast.30, bf16[128,1792]{1,0:T(8,128)(2,1)S(1)} %bitcast.28, bf16[128,256]{1,0:T(8,128)(2,1)S(1)} %get-tuple-element.70, bf16[128,256]{1,0:T(8,128)(2,1)S(1)} %get-tuple-element.68, ...), kind=kOutput, calls=%fused_computation.8 | convolution fusion | flops 478150656 | bytes 3932160 | tf_op jit(solution)/shard_map/dot_general | solution.py:208
  126.2 2.4 %collective-permute-start.10 = (bf16[128,1792]{1,0:T(8,128)(2,1)S(1)}, bf16[128,1792]{1,0:T(8,128)(2,1)S(1)}, u32[]{:S(2)}, u32[]{:S(2)}) collective-permute-start(bf16[128,1792]{1,0:T(8,128)(2,1)S(1)} %slice.134), channel_id=1, source_target_pairs={{0,1},{1,0},{2,3},{3,2},{4,5},{5,4},{6,7},{7,6},{8,9},{9,8},{10,11... | collective-permute-start | bytes 1376264 | tf_op jit(solution)/shard_map/down_swap/ppermute | solution.py:124
  129.4 1.9 %collective-permute-start.9 = (bf16[1792,128]{1,0:T(8,128)(2,1)S(1)}, bf16[1792,128]{1,0:T(8,128)(2,1)S(1)}, u32[]{:S(2)}, u32[]{:S(2)}) collective-permute-start(bf16[1792,128]{1,0:T(8,128)(2,1)S(1)} %slice.135), channel_id=1, source_target_pairs={{0,1},{1,0},{2,3},{3,2},{4,5},{5,4},{6,7},{7,6},{8,9},{9,8},{10,11... | collective-permute-start | bytes 1376264 | tf_op jit(solution)/shard_map/up_swap/ppermute | solution.py:124
  132.1 0.9 collective-permute-done.9
  133.1 0.9 fusion.18
  (35 shorter events, 4.7 us)
Async XLA Ops:
  0.6 8.5 %copy-start = (bf16[3584,128]{1,0:T(8,128)(2,1)S(1)}, bf16[3584,128]{1,0:T(8,128)(2,1)}, u32[]{:S(2)}) copy-start(bf16[3584,128]{1,0:T(8,128)(2,1)} %up_mine.3) | copy-start | bytes 2752516
  3.4 15.6 %collective-permute-start = (bf16[32,3584]{1,0:T(8,128)(2,1)}, bf16[32,3584]{1,0:T(8,128)(2,1)S(1)}, u32[]{:S(2)}, u32[]{:S(2)}) collective-permute-start(bf16[32,3584]{1,0:T(8,128)(2,1)} %get-tuple-element.26), channel_id=1, source_target_pairs={{0,16},{1,17},{2,18},{3,19},{4,20},{5,21},{6,22},{7,23},{8,24},{9,... | collective-permute-start | bytes 688136 | tf_op jit(solution)/shard_map/far/ppermute | solution.py:124
  9.2 23.3 %collective-permute-start.2 = (bf16[3584,128]{1,0:T(8,128)(2,1)S(1)}, bf16[3584,128]{1,0:T(8,128)(2,1)}, u32[]{:S(2)}, u32[]{:S(2)}) collective-permute-start(bf16[3584,128]{1,0:T(8,128)(2,1)S(1)} %copy-done), channel_id=1, source_target_pairs={{0,1},{1,0},{2,3},{3,2},{4,5},{5,4},{6,7},{7,6},{8,9},{9,8},{10,11... | collective-permute-start | bytes 2752520 | tf_op jit(solution)/shard_map/weight_up/ppermute | solution.py:124
  14.2 18.3 %collective-permute-start.3 = (bf16[128,3584]{1,0:T(8,128)(2,1)}, bf16[128,3584]{1,0:T(8,128)(2,1)}, u32[]{:S(2)}, u32[]{:S(2)}) collective-permute-start(bf16[128,3584]{1,0:T(8,128)(2,1)} %down_mine.3), channel_id=1, source_target_pairs={{0,1},{1,0},{2,3},{3,2},{4,5},{5,4},{6,7},{7,6},{8,9},{9,8},{10,11... | collective-permute-start | bytes 2752520 | tf_op jit(solution)/shard_map/weight_down/ppermute | solution.py:124
  16.1 12.2 %collective-permute-start.6 = (bf16[32,3584]{1,0:T(8,128)(2,1)}, bf16[32,3584]{1,0:T(8,128)(2,1)}, u32[]{:S(2)}, u32[]{:S(2)}) collective-permute-start(bf16[32,3584]{1,0:T(8,128)(2,1)} %get-tuple-element.25), channel_id=1, source_target_pairs={{0,8},{1,9},{2,10},{3,11},{4,12},{5,13},{6,14},{7,15},{8,0},{9,1},... | collective-permute-start | bytes 688136 | tf_op jit(solution)/shard_map/beside/ppermute | solution.py:124
  20.5 27.5 %all-to-all-start = ((bf16[4,64,3584]{2,1,0:T(8,128)(2,1)}), bf16[4,64,3584]{2,1,0:T(8,128)(2,1)S(1)}, u32[]{:S(2)}, u32[]{:S(2)}) async-start(bf16[4,64,3584]{2,1,0:T(8,128)(2,1)} %broadcast_in_dim.31), calls=%async_computation | async-start | bytes 3670016 | tf_op jit(solution)/shard_map/near_ring/all_to_all | solution.py:151
  25.1 7.4 %collective-permute-start.1 = (bf16[32,3584]{1,0:T(8,128)(2,1)S(1)}, bf16[32,3584]{1,0:T(8,128)(2,1)S(1)}, u32[]{:S(2)}, u32[]{:S(2)}) collective-permute-start(bf16[32,3584]{1,0:T(8,128)(2,1)S(1)} %collective-permute-done), channel_id=1, source_target_pairs={{0,8},{1,9},{2,10},{3,11},{4,12},{5,13},{6,14},{7,15},{8,0},{9,1},... | collective-permute-start | bytes 688136 | tf_op jit(solution)/shard_map/far_beside/ppermute | solution.py:124
  32.5 41.4 %collective-permute-start.4 = (bf16[64,1792]{1,0:T(8,128)(2,1)}, bf16[64,1792]{1,0:T(8,128)(2,1)}, u32[]{:S(2)}, u32[]{:S(2)}) collective-permute-start(bf16[64,1792]{1,0:T(8,128)(2,1)} %constant_dynamic-slice_fusion.4), channel_id=1, source_target_pairs={{0,256},{32,288},{64,320},{96,352},{128,384},{160,416},{192,448},{... | collective-permute-start | bytes 688136 | tf_op jit(solution)/shard_map/rows_mirror/ppermute | solution.py:128
  49.3 28.1 %all-to-all-start.1 = ((bf16[4,64,3584]{2,1,0:T(8,128)(2,1)}), bf16[4,64,3584]{2,1,0:T(8,128)(2,1)}, u32[]{:S(2)}, u32[]{:S(2)}) async-start(bf16[4,64,3584]{2,1,0:T(8,128)(2,1)} %broadcast_in_dim.32), calls=%async_computation.1 | async-start | bytes 3670016 | tf_op jit(solution)/shard_map/pair_ring/all_to_all | solution.py:151
  59.3 45.4 %collective-permute-start.7 = (bf16[256,256]{1,0:T(8,128)(2,1)S(1)}, bf16[256,256]{1,0:T(8,128)(2,1)S(1)}, u32[]{:S(2)}, u32[]{:S(2)}) collective-permute-start(bf16[256,256]{1,0:T(8,128)(2,1)S(1)} %near_units.1), channel_id=1, source_target_pairs={{0,256},{32,288},{64,320},{96,352},{128,384},{160,416},{192,448},{... | collective-permute-start | bytes 393224 | tf_op jit(solution)/shard_map/units_near/ppermute | solution.py:128
  73.8 16.6 %collective-permute-start.5 = (bf16[64,1792]{1,0:T(8,128)(2,1)}, bf16[64,1792]{1,0:T(8,128)(2,1)}, u32[]{:S(2)}, u32[]{:S(2)}) collective-permute-start(bf16[64,1792]{1,0:T(8,128)(2,1)} %collective-permute-done.4), channel_id=1, source_target_pairs={{0,8},{1,9},{2,10},{3,11},{4,12},{5,13},{6,14},{7,15},{8,0},{9,1},... | collective-permute-start | bytes 688136 | tf_op jit(solution)/shard_map/pair_m/ppermute | solution.py:124
  92.8 30.7 %all-to-all-start.2 = ((bf16[4,128,1792]{2,1,0:T(8,128)(2,1)}), bf16[4,128,1792]{2,1,0:T(8,128)(2,1)S(1)}, u32[]{:S(2)}, u32[]{:S(2)}) async-start(bf16[4,128,1792]{2,1,0:T(8,128)(2,1)} %broadcast_in_dim.33), calls=%async_computation.2 | async-start | bytes 3670016 | tf_op jit(solution)/shard_map/mirror_ring/all_to_all | solution.py:151
  99.3 24.2 %collective-permute-start.8 = (bf16[256,256]{1,0:T(8,128)(2,1)S(1)}, bf16[256,256]{1,0:T(8,128)(2,1)S(1)}, u32[]{:S(2)}, u32[]{:S(2)}) collective-permute-start(bf16[256,256]{1,0:T(8,128)(2,1)S(1)} %pair_units.1), channel_id=1, source_target_pairs={{0,256},{32,288},{64,320},{96,352},{128,384},{160,416},{192,448},{... | collective-permute-start | bytes 393224 | tf_op jit(solution)/shard_map/units_pair/ppermute | solution.py:128
  104.7 19.0 %copy-start.1 = (bf16[4,32,1792]{2,1,0:T(8,128)(2,1)S(1)}, bf16[4,32,1792]{2,1,0:T(8,128)(2,1)}, u32[]{:S(2)}) copy-start(bf16[4,32,1792]{2,1,0:T(8,128)(2,1)} %get-tuple-element.74) | copy-start | bytes 1376260
  123.5 0.8 copy-start.4
  124.3 4.2 %copy-start.2 = (bf16[4,32,1792]{2,1,0:T(8,128)(2,1)S(1)}, bf16[4,32,1792]{2,1,0:T(8,128)(2,1)}, u32[]{:S(2)}) copy-start(bf16[4,32,1792]{2,1,0:T(8,128)(2,1)} %get-tuple-element.73) | copy-start | bytes 1376260
  124.3 4.3 %copy-start.3 = (bf16[128,256]{1,0:T(8,128)(2,1)S(1)}, bf16[128,256]{1,0:T(8,128)(2,1)}, u32[]{:S(2)}) copy-start(bf16[128,256]{1,0:T(8,128)(2,1)} %get-tuple-element.67) | copy-start | bytes 196612
  126.2 5.1 %collective-permute-start.10 = (bf16[128,1792]{1,0:T(8,128)(2,1)S(1)}, bf16[128,1792]{1,0:T(8,128)(2,1)S(1)}, u32[]{:S(2)}, u32[]{:S(2)}) collective-permute-start(bf16[128,1792]{1,0:T(8,128)(2,1)S(1)} %slice.134), channel_id=1, source_target_pairs={{0,1},{1,0},{2,3},{3,2},{4,5},{5,4},{6,7},{7,6},{8,9},{9,8},{10,11... | collective-permute-start | bytes 1376264 | tf_op jit(solution)/shard_map/down_swap/ppermute | solution.py:124
  129.4 3.7 %collective-permute-start.9 = (bf16[1792,128]{1,0:T(8,128)(2,1)S(1)}, bf16[1792,128]{1,0:T(8,128)(2,1)S(1)}, u32[]{:S(2)}, u32[]{:S(2)}) collective-permute-start(bf16[1792,128]{1,0:T(8,128)(2,1)S(1)} %slice.135), channel_id=1, source_target_pairs={{0,1},{1,0},{2,3},{3,2},{4,5},{5,4},{6,7},{7,6},{8,9},{9,8},{10,11... | collective-permute-start | bytes 1376264 | tf_op jit(solution)/shard_map/up_swap/ppermute | solution.py:124

commit v8 on v4

--- a/solution.py
+++ b/solution.py
@@ -59,7 +59,7 @@
 
 
 FREE = pl.CostEstimate(flops=0, transcendentals=0, bytes_accessed=0)
-STEP = 512
+STEP = 1792
 
 
 def rows_to_units(rows, up_mine, up_other, down_mine, down_other, units):

time: 132 us -> 132 us (level)
  transfers between devices with their start and end apart: 14 -> 14, of which waited for: 5 -> 5; matrix products, arithmetic and copies ran while one was open for 11% -> 11% of each run, Pallas kernels for 5% -> 4%
where the time goes in v8:
time: 132 us; the launch traced here: 131 us
  starting transfers between devices  71.9 us (54%)
  waiting for transfers between devices  31.9 us (24%)
  local copies, waits for them, and re-layouts  12.6 us (10%)
  Pallas kernels  8.63 us (7%)
  other arithmetic  2.85 us (2%)
  matrix products  2.45 us (2%)
    ppermute x3, starting transfers between devices, mirrored(): lax.ppermute(value, 'pipe', [(q, q ^ sections // 2) for q in range(sectio...  34.9 us
    ppermute x8, starting transfers between devices, across(): lax.ppermute(value, 'expert', [(s, s ^ flip) for s in range(members)])  24.3 us
    ppermute x3, waiting for transfers between devices, mirrored(): lax.ppermute(value, 'pipe', [(q, q ^ sections // 2) for q in range(sectio...  18.4 us
    ppermute x8, waiting for transfers between devices, across(): lax.ppermute(value, 'expert', [(s, s ^ flip) for s in range(members)])  13.3 us
    all_to_all x3, starting transfers between devices, around(): lax.all_to_all(copies, 'expert', 0, 0, axis_index_groups=circles, tiled=T...  12.6 us
    pallas_call x2, Pallas kernels, in_vmem(): pl.pallas_call(kernel, in_specs=[vmem] * len(operands), out_specs=vmem, o...  5.83 us
    broadcast_in_dim x3, local copies, waits for them, and re-layouts, repeated(): return jnp.broadcast_to(block[None], (4, *block.shape))  4.1 us
    pallas_call x1, Pallas kernels, picked(): pl.pallas_call(pick_rows, in_specs=[pl.BlockSpec(memory_space=pltpu.SMEM)...  2.8 us
  transfers between devices with their start and end apart: 14, of which 5 were waited for; matrix products, arithmetic and copies ran while one was open for 11% of the time, Pallas kernels for 4%

profile of v8, /device:TPU:1, one launch (start us, length us, event | category | flops | bytes accessed | tf_op | source)
XLA Modules:
  0.0 131.2 jit_solution(4386407034374396422)
XLA Ops:
  0.6 2.8 %pick.1 = (bf16[32,3584]{1,0:T(8,128)(2,1)}, bf16[32,3584]{1,0:T(8,128)(2,1)}) custom-call(s32[1]{0:T(128)} %bitcast.side_ref, bf16[128,3584]{1,0:T(8,128)(2,1)} %bitcast.21, bf16[128,3584]{1,0:T(8,128)(2,1)} %bitcast.22, s32[2,128]{1,0:T(2,128)} %bitcast.31, f32[2,128]{1,0:T(2,128)} %bitcast.32), custom_call_target="tpu_custom_call" | custom-call | tf_op jit(solution)/shard_map/pick/pallas_call | solution.py:51
  3.4 5.7 %collective-permute-start = (bf16[32,3584]{1,0:T(8,128)(2,1)}, bf16[32,3584]{1,0:T(8,128)(2,1)S(1)}, u32[]{:S(2)}, u32[]{:S(2)}) collective-permute-start(bf16[32,3584]{1,0:T(8,128)(2,1)} %get-tuple-element.26), channel_id=1, source_target_pairs={{0,16},{1,17},{2,18},{3,19},{4,20},{5,21},{6,22},{7,23},{8,24},{9,... | collective-permute-start | bytes 688136 | tf_op jit(solution)/shard_map/far/ppermute | solution.py:108
  9.2 5.0 %collective-permute-start.2 = (bf16[3584,128]{1,0:T(8,128)(2,1)S(1)}, bf16[3584,128]{1,0:T(8,128)(2,1)}, u32[]{:S(2)}, u32[]{:S(2)}) collective-permute-start(bf16[3584,128]{1,0:T(8,128)(2,1)S(1)} %copy-done), channel_id=1, source_target_pairs={{0,1},{1,0},{2,3},{3,2},{4,5},{5,4},{6,7},{7,6},{8,9},{9,8},{10,11... | collective-permute-start | bytes 2752520 | tf_op jit(solution)/shard_map/weight_up/ppermute | solution.py:108
  14.2 1.9 %collective-permute-start.3 = (bf16[128,3584]{1,0:T(8,128)(2,1)}, bf16[128,3584]{1,0:T(8,128)(2,1)}, u32[]{:S(2)}, u32[]{:S(2)}) collective-permute-start(bf16[128,3584]{1,0:T(8,128)(2,1)} %down_mine.3), channel_id=1, source_target_pairs={{0,1},{1,0},{2,3},{3,2},{4,5},{5,4},{6,7},{7,6},{8,9},{9,8},{10,11... | collective-permute-start | bytes 2752520 | tf_op jit(solution)/shard_map/weight_down/ppermute | solution.py:108
  16.1 1.9 %collective-permute-start.6 = (bf16[32,3584]{1,0:T(8,128)(2,1)}, bf16[32,3584]{1,0:T(8,128)(2,1)}, u32[]{:S(2)}, u32[]{:S(2)}) collective-permute-start(bf16[32,3584]{1,0:T(8,128)(2,1)} %get-tuple-element.25), channel_id=1, source_target_pairs={{0,8},{1,9},{2,10},{3,11},{4,12},{5,13},{6,14},{7,15},{8,0},{9,1},... | collective-permute-start | bytes 688136 | tf_op jit(solution)/shard_map/beside/ppermute | solution.py:108
  18.0 1.0 fusion.41
  19.1 1.4 %broadcast_in_dim.31 = bf16[4,64,3584]{2,1,0:T(8,128)(2,1)} broadcast(bf16[64,3584]{1,0:T(8,128)(2,1)S(1)} %pad_maximum_fusion), dimensions={1,2} | broadcast | bytes 2293760 | tf_op jit(solution)/shard_map/broadcast_in_dim | solution.py:131
  20.5 4.6 %all-to-all-start = ((bf16[4,64,3584]{2,1,0:T(8,128)(2,1)}), bf16[4,64,3584]{2,1,0:T(8,128)(2,1)S(1)}, u32[]{:S(2)}, u32[]{:S(2)}) async-start(bf16[4,64,3584]{2,1,0:T(8,128)(2,1)} %broadcast_in_dim.31), calls=%async_computation | async-start | bytes 3670016 | tf_op jit(solution)/shard_map/near_ring/all_to_all | solution.py:135
  25.1 3.2 %collective-permute-start.1 = (bf16[32,3584]{1,0:T(8,128)(2,1)S(1)}, bf16[32,3584]{1,0:T(8,128)(2,1)S(1)}, u32[]{:S(2)}, u32[]{:S(2)}) collective-permute-start(bf16[32,3584]{1,0:T(8,128)(2,1)S(1)} %collective-permute-done), channel_id=1, source_target_pairs={{0,8},{1,9},{2,10},{3,11},{4,12},{5,13},{6,14},{7,15},{8,0},{9,1},... | collective-permute-start | bytes 688136 | tf_op jit(solution)/shard_map/far_beside/ppermute | solution.py:108
  28.3 1.0 fusion.39
  30.0 2.4 %collective-permute-done.1 = bf16[32,3584]{1,0:T(8,128)(2,1)S(1)} collective-permute-done((bf16[32,3584]{1,0:T(8,128)(2,1)S(1)}, bf16[32,3584]{1,0:T(8,128)(2,1)S(1)}, u32[]{:S(2)}, u32[]{:S(2)}) %collective-permute-start.1) | collective-permute-done | bytes 229408 | tf_op jit(solution)/shard_map/far_beside/ppermute | solution.py:108
  32.5 15.4 %collective-permute-start.4 = (bf16[64,1792]{1,0:T(8,128)(2,1)}, bf16[64,1792]{1,0:T(8,128)(2,1)}, u32[]{:S(2)}, u32[]{:S(2)}) collective-permute-start(bf16[64,1792]{1,0:T(8,128)(2,1)} %constant_dynamic-slice_fusion.4), channel_id=1, source_target_pairs={{0,256},{32,288},{64,320},{96,352},{128,384},{160,416},{192,448},{... | collective-permute-start | bytes 688136 | tf_op jit(solution)/shard_map/rows_mirror/ppermute | solution.py:112
  47.9 1.4 %broadcast_in_dim.32 = bf16[4,64,3584]{2,1,0:T(8,128)(2,1)} broadcast(bf16[64,3584]{1,0:T(8,128)(2,1)S(1)} %pad_maximum_fusion.1), dimensions={1,2} | broadcast | bytes 2293760 | tf_op jit(solution)/shard_map/broadcast_in_dim | solution.py:131
  49.3 4.4 %all-to-all-start.1 = ((bf16[4,64,3584]{2,1,0:T(8,128)(2,1)}), bf16[4,64,3584]{2,1,0:T(8,128)(2,1)}, u32[]{:S(2)}, u32[]{:S(2)}) async-start(bf16[4,64,3584]{2,1,0:T(8,128)(2,1)} %broadcast_in_dim.32), calls=%async_computation.1 | async-start | bytes 3670016 | tf_op jit(solution)/shard_map/pair_ring/all_to_all | solution.py:135
  53.7 2.6 %near_units.1 = bf16[256,256]{1,0:T(8,128)(2,1)S(1)} custom-call(bf16[4,64,3584]{2,1,0:T(8,128)(2,1)S(1)} %all-to-all-done.rows, bf16[3584,128]{1,0:T(8,128)(2,1)S(1)} %copy-done, bf16[3584,128]{1,0:T(8,128)(2,1)} %collective-permute-done.2.up_other, bf16[128,3584]{1,0:T(8,128)(2,1)} %down_mine.3, bf16[128,3584]{1,0:T(8,128)(2,1)} %collective-permute-done.3.down_other), custom_call_target="tpu_custom_call" | custom-call | tf_op jit(solution)/shard_map/near_units/pallas_call | solution.py:87
  56.4 14.5 %collective-permute-start.7 = (bf16[256,256]{1,0:T(8,128)(2,1)S(1)}, bf16[256,256]{1,0:T(8,128)(2,1)S(1)}, u32[]{:S(2)}, u32[]{:S(2)}) collective-permute-start(bf16[256,256]{1,0:T(8,128)(2,1)S(1)} %near_units.1), channel_id=1, source_target_pairs={{0,256},{32,288},{64,320},{96,352},{128,384},{160,416},{192,448},{... | collective-permute-start | bytes 393224 | tf_op jit(solution)/shard_map/units_near/ppermute | solution.py:112
  70.9 1.9 %collective-permute-start.5 = (bf16[64,1792]{1,0:T(8,128)(2,1)}, bf16[64,1792]{1,0:T(8,128)(2,1)}, u32[]{:S(2)}, u32[]{:S(2)}) collective-permute-start(bf16[64,1792]{1,0:T(8,128)(2,1)} %collective-permute-done.4), channel_id=1, source_target_pairs={{0,8},{1,9},{2,10},{3,11},{4,12},{5,13},{6,14},{7,15},{8,0},{9,1},... | collective-permute-start | bytes 688136 | tf_op jit(solution)/shard_map/pair_m/ppermute | solution.py:108
  72.9 0.9 constant_dynamic-slice_fusion
  74.7 3.2 %pair_units.1 = bf16[256,256]{1,0:T(8,128)(2,1)S(1)} custom-call(bf16[4,64,3584]{2,1,0:T(8,128)(2,1)} %all-to-all-done.1.rows, bf16[3584,128]{1,0:T(8,128)(2,1)S(1)} %copy-done, bf16[3584,128]{1,0:T(8,128)(2,1)} %collective-permute-done.2.up_other, bf16[128,3584]{1,0:T(8,128)(2,1)} %down_mine.3, bf16[128,3584]{1,0:T(8,128)(2,1)} %collective-permute-done.3.down_other), custom_call_target="tpu_custom_call" | custom-call | tf_op jit(solution)/shard_map/pair_units/pallas_call | solution.py:87
  77.9 9.9 %collective-permute-done.5 = bf16[64,1792]{1,0:T(8,128)(2,1)} collective-permute-done((bf16[64,1792]{1,0:T(8,128)(2,1)}, bf16[64,1792]{1,0:T(8,128)(2,1)}, u32[]{:S(2)}, u32[]{:S(2)}) %collective-permute-start.5) | collective-permute-done | bytes 229408 | tf_op jit(solution)/shard_map/pair_m/ppermute | solution.py:108
  87.8 1.1 pad_maximum_fusion.2
  88.8 1.3 %broadcast_in_dim.33 = bf16[4,128,1792]{2,1,0:T(8,128)(2,1)} broadcast(bf16[128,1792]{1,0:T(8,128)(2,1)S(1)} %pad_maximum_fusion.2), dimensions={1,2} | broadcast | bytes 2293760 | tf_op jit(solution)/shard_map/broadcast_in_dim | solution.py:131
  90.2 3.6 %all-to-all-start.2 = ((bf16[4,128,1792]{2,1,0:T(8,128)(2,1)}), bf16[4,128,1792]{2,1,0:T(8,128)(2,1)S(1)}, u32[]{:S(2)}, u32[]{:S(2)}) async-start(bf16[4,128,1792]{2,1,0:T(8,128)(2,1)} %broadcast_in_dim.33), calls=%async_computation.2 | async-start | bytes 3670016 | tf_op jit(solution)/shard_map/mirror_ring/all_to_all | solution.py:135
  93.8 1.6 %fusion.38 = (bf16[4,32,3584]{2,1,0:T(8,128)(2,1)S(1)}, bf16[4,32,3584]{2,1,0:T(8,128)(2,1)S(1)}) fusion(bf16[4,64,3584]{2,1,0:T(8,128)(2,1)} %all-to-all-done.1.rows), kind=kLoop, calls=%fused_computation.50 | loop fusion | bytes 3670016 | tf_op jit(solution)/shard_map/slice | solution.py:180
  95.4 1.0 constant_dynamic-slice_fusion.1
  96.4 5.0 %collective-permute-start.8 = (bf16[256,256]{1,0:T(8,128)(2,1)S(1)}, bf16[256,256]{1,0:T(8,128)(2,1)S(1)}, u32[]{:S(2)}, u32[]{:S(2)}) collective-permute-start(bf16[256,256]{1,0:T(8,128)(2,1)S(1)} %pair_units.1), channel_id=1, source_target_pairs={{0,256},{32,288},{64,320},{96,352},{128,384},{160,416},{192,448},{... | collective-permute-start | bytes 393224 | tf_op jit(solution)/shard_map/units_pair/ppermute | solution.py:112
  102.1 18.4 %collective-permute-done.8 = bf16[256,256]{1,0:T(8,128)(2,1)S(1)} collective-permute-done((bf16[256,256]{1,0:T(8,128)(2,1)S(1)}, bf16[256,256]{1,0:T(8,128)(2,1)S(1)}, u32[]{:S(2)}, u32[]{:S(2)}) %collective-permute-start.8) | collective-permute-done | bytes 131104 | tf_op jit(solution)/shard_map/units_pair/ppermute | solution.py:112
  121.3 1.8 %fusion.8 = f32[256,1792]{1,0:T(8,128)S(1)} fusion(bf16[128,1792]{1,0:T(8,128)(2,1)S(1)} %bitcast.26, bf16[128,1792]{1,0:T(8,128)(2,1)S(1)} %bitcast.25, bf16[128,1792]{1,0:T(8,128)(2,1)} %bitcast.30, bf16[128,1792]{1,0:T(8,128)(2,1)S(1)} %bitcast.28, bf16[128,256]{1,0:T(8,128)(2,1)S(1)} %get-tuple-element.70, bf16[128,256]{1,0:T(8,128)(2,1)S(1)} %get-tuple-element.68, ...), kind=kOutput, calls=%fused_computation.8 | convolution fusion | flops 478150656 | bytes 3932160 | tf_op jit(solution)/shard_map/dot_general | solution.py:192
  123.1 2.7 %collective-permute-start.10 = (bf16[128,1792]{1,0:T(8,128)(2,1)S(1)}, bf16[128,1792]{1,0:T(8,128)(2,1)S(1)}, u32[]{:S(2)}, u32[]{:S(2)}) collective-permute-start(bf16[128,1792]{1,0:T(8,128)(2,1)S(1)} %slice.134), channel_id=1, source_target_pairs={{0,1},{1,0},{2,3},{3,2},{4,5},{5,4},{6,7},{7,6},{8,9},{9,8},{10,11... | collective-permute-start | bytes 1376264 | tf_op jit(solution)/shard_map/down_swap/ppermute | solution.py:108
  126.7 1.9 %collective-permute-start.9 = (bf16[1792,128]{1,0:T(8,128)(2,1)S(1)}, bf16[1792,128]{1,0:T(8,128)(2,1)S(1)}, u32[]{:S(2)}, u32[]{:S(2)}) collective-permute-start(bf16[1792,128]{1,0:T(8,128)(2,1)S(1)} %slice.135), channel_id=1, source_target_pairs={{0,1},{1,0},{2,3},{3,2},{4,5},{5,4},{6,7},{7,6},{8,9},{9,8},{10,11... | collective-permute-start | bytes 1376264 | tf_op jit(solution)/shard_map/up_swap/ppermute | solution.py:108
  129.5 0.9 collective-permute-done.9
  130.4 0.9 fusion.18
  (35 shorter events, 4.9 us)
Async XLA Ops:
  0.6 8.5 %copy-start = (bf16[3584,128]{1,0:T(8,128)(2,1)S(1)}, bf16[3584,128]{1,0:T(8,128)(2,1)}, u32[]{:S(2)}) copy-start(bf16[3584,128]{1,0:T(8,128)(2,1)} %up_mine.3) | copy-start | bytes 2752516
  3.4 15.6 %collective-permute-start = (bf16[32,3584]{1,0:T(8,128)(2,1)}, bf16[32,3584]{1,0:T(8,128)(2,1)S(1)}, u32[]{:S(2)}, u32[]{:S(2)}) collective-permute-start(bf16[32,3584]{1,0:T(8,128)(2,1)} %get-tuple-element.26), channel_id=1, source_target_pairs={{0,16},{1,17},{2,18},{3,19},{4,20},{5,21},{6,22},{7,23},{8,24},{9,... | collective-permute-start | bytes 688136 | tf_op jit(solution)/shard_map/far/ppermute | solution.py:108
  9.2 23.3 %collective-permute-start.2 = (bf16[3584,128]{1,0:T(8,128)(2,1)S(1)}, bf16[3584,128]{1,0:T(8,128)(2,1)}, u32[]{:S(2)}, u32[]{:S(2)}) collective-permute-start(bf16[3584,128]{1,0:T(8,128)(2,1)S(1)} %copy-done), channel_id=1, source_target_pairs={{0,1},{1,0},{2,3},{3,2},{4,5},{5,4},{6,7},{7,6},{8,9},{9,8},{10,11... | collective-permute-start | bytes 2752520 | tf_op jit(solution)/shard_map/weight_up/ppermute | solution.py:108
  14.2 18.3 %collective-permute-start.3 = (bf16[128,3584]{1,0:T(8,128)(2,1)}, bf16[128,3584]{1,0:T(8,128)(2,1)}, u32[]{:S(2)}, u32[]{:S(2)}) collective-permute-start(bf16[128,3584]{1,0:T(8,128)(2,1)} %down_mine.3), channel_id=1, source_target_pairs={{0,1},{1,0},{2,3},{3,2},{4,5},{5,4},{6,7},{7,6},{8,9},{9,8},{10,11... | collective-permute-start | bytes 2752520 | tf_op jit(solution)/shard_map/weight_down/ppermute | solution.py:108
  16.1 12.2 %collective-permute-start.6 = (bf16[32,3584]{1,0:T(8,128)(2,1)}, bf16[32,3584]{1,0:T(8,128)(2,1)}, u32[]{:S(2)}, u32[]{:S(2)}) collective-permute-start(bf16[32,3584]{1,0:T(8,128)(2,1)} %get-tuple-element.25), channel_id=1, source_target_pairs={{0,8},{1,9},{2,10},{3,11},{4,12},{5,13},{6,14},{7,15},{8,0},{9,1},... | collective-permute-start | bytes 688136 | tf_op jit(solution)/shard_map/beside/ppermute | solution.py:108
  20.5 27.5 %all-to-all-start = ((bf16[4,64,3584]{2,1,0:T(8,128)(2,1)}), bf16[4,64,3584]{2,1,0:T(8,128)(2,1)S(1)}, u32[]{:S(2)}, u32[]{:S(2)}) async-start(bf16[4,64,3584]{2,1,0:T(8,128)(2,1)} %broadcast_in_dim.31), calls=%async_computation | async-start | bytes 3670016 | tf_op jit(solution)/shard_map/near_ring/all_to_all | solution.py:135
  25.1 7.4 %collective-permute-start.1 = (bf16[32,3584]{1,0:T(8,128)(2,1)S(1)}, bf16[32,3584]{1,0:T(8,128)(2,1)S(1)}, u32[]{:S(2)}, u32[]{:S(2)}) collective-permute-start(bf16[32,3584]{1,0:T(8,128)(2,1)S(1)} %collective-permute-done), channel_id=1, source_target_pairs={{0,8},{1,9},{2,10},{3,11},{4,12},{5,13},{6,14},{7,15},{8,0},{9,1},... | collective-permute-start | bytes 688136 | tf_op jit(solution)/shard_map/far_beside/ppermute | solution.py:108
  32.5 38.4 %collective-permute-start.4 = (bf16[64,1792]{1,0:T(8,128)(2,1)}, bf16[64,1792]{1,0:T(8,128)(2,1)}, u32[]{:S(2)}, u32[]{:S(2)}) collective-permute-start(bf16[64,1792]{1,0:T(8,128)(2,1)} %constant_dynamic-slice_fusion.4), channel_id=1, source_target_pairs={{0,256},{32,288},{64,320},{96,352},{128,384},{160,416},{192,448},{... | collective-permute-start | bytes 688136 | tf_op jit(solution)/shard_map/rows_mirror/ppermute | solution.py:112
  49.3 25.4 %all-to-all-start.1 = ((bf16[4,64,3584]{2,1,0:T(8,128)(2,1)}), bf16[4,64,3584]{2,1,0:T(8,128)(2,1)}, u32[]{:S(2)}, u32[]{:S(2)}) async-start(bf16[4,64,3584]{2,1,0:T(8,128)(2,1)} %broadcast_in_dim.32), calls=%async_computation.1 | async-start | bytes 3670016 | tf_op jit(solution)/shard_map/pair_ring/all_to_all | solution.py:135
  56.4 45.7 %collective-permute-start.7 = (bf16[256,256]{1,0:T(8,128)(2,1)S(1)}, bf16[256,256]{1,0:T(8,128)(2,1)S(1)}, u32[]{:S(2)}, u32[]{:S(2)}) collective-permute-start(bf16[256,256]{1,0:T(8,128)(2,1)S(1)} %near_units.1), channel_id=1, source_target_pairs={{0,256},{32,288},{64,320},{96,352},{128,384},{160,416},{192,448},{... | collective-permute-start | bytes 393224 | tf_op jit(solution)/shard_map/units_near/ppermute | solution.py:112
  70.9 16.9 %collective-permute-start.5 = (bf16[64,1792]{1,0:T(8,128)(2,1)}, bf16[64,1792]{1,0:T(8,128)(2,1)}, u32[]{:S(2)}, u32[]{:S(2)}) collective-permute-start(bf16[64,1792]{1,0:T(8,128)(2,1)} %collective-permute-done.4), channel_id=1, source_target_pairs={{0,8},{1,9},{2,10},{3,11},{4,12},{5,13},{6,14},{7,15},{8,0},{9,1},... | collective-permute-start | bytes 688136 | tf_op jit(solution)/shard_map/pair_m/ppermute | solution.py:108
  90.2 30.3 %all-to-all-start.2 = ((bf16[4,128,1792]{2,1,0:T(8,128)(2,1)}), bf16[4,128,1792]{2,1,0:T(8,128)(2,1)S(1)}, u32[]{:S(2)}, u32[]{:S(2)}) async-start(bf16[4,128,1792]{2,1,0:T(8,128)(2,1)} %broadcast_in_dim.33), calls=%async_computation.2 | async-start | bytes 3670016 | tf_op jit(solution)/shard_map/mirror_ring/all_to_all | solution.py:135
  96.4 24.1 %collective-permute-start.8 = (bf16[256,256]{1,0:T(8,128)(2,1)S(1)}, bf16[256,256]{1,0:T(8,128)(2,1)S(1)}, u32[]{:S(2)}, u32[]{:S(2)}) collective-permute-start(bf16[256,256]{1,0:T(8,128)(2,1)S(1)} %pair_units.1), channel_id=1, source_target_pairs={{0,256},{32,288},{64,320},{96,352},{128,384},{160,416},{192,448},{... | collective-permute-start | bytes 393224 | tf_op jit(solution)/shard_map/units_pair/ppermute | solution.py:112
  102.1 18.6 %copy-start.1 = (bf16[4,32,1792]{2,1,0:T(8,128)(2,1)S(1)}, bf16[4,32,1792]{2,1,0:T(8,128)(2,1)}, u32[]{:S(2)}) copy-start(bf16[4,32,1792]{2,1,0:T(8,128)(2,1)} %get-tuple-element.74) | copy-start | bytes 1376260
  120.5 0.8 copy-start.4
  121.3 4.6 %copy-start.2 = (bf16[4,32,1792]{2,1,0:T(8,128)(2,1)S(1)}, bf16[4,32,1792]{2,1,0:T(8,128)(2,1)}, u32[]{:S(2)}) copy-start(bf16[4,32,1792]{2,1,0:T(8,128)(2,1)} %get-tuple-element.73) | copy-start | bytes 1376260
  121.3 4.6 %copy-start.3 = (bf16[128,256]{1,0:T(8,128)(2,1)S(1)}, bf16[128,256]{1,0:T(8,128)(2,1)}, u32[]{:S(2)}) copy-start(bf16[128,256]{1,0:T(8,128)(2,1)} %get-tuple-element.67) | copy-start | bytes 196612
  123.1 5.5 %collective-permute-start.10 = (bf16[128,1792]{1,0:T(8,128)(2,1)S(1)}, bf16[128,1792]{1,0:T(8,128)(2,1)S(1)}, u32[]{:S(2)}, u32[]{:S(2)}) collective-permute-start(bf16[128,1792]{1,0:T(8,128)(2,1)S(1)} %slice.134), channel_id=1, source_target_pairs={{0,1},{1,0},{2,3},{3,2},{4,5},{5,4},{6,7},{7,6},{8,9},{9,8},{10,11... | collective-permute-start | bytes 1376264 | tf_op jit(solution)/shard_map/down_swap/ppermute | solution.py:108
  126.7 3.7 %collective-permute-start.9 = (bf16[1792,128]{1,0:T(8,128)(2,1)S(1)}, bf16[1792,128]{1,0:T(8,128)(2,1)S(1)}, u32[]{:S(2)}, u32[]{:S(2)}) collective-permute-start(bf16[1792,128]{1,0:T(8,128)(2,1)S(1)} %slice.135), channel_id=1, source_target_pairs={{0,1},{1,0},{2,3},{3,2},{4,5},{5,4},{6,7},{7,6},{8,9},{9,8},{10,11... | collective-permute-start | bytes 1376264 | tf_op jit(solution)/shard_map/up_swap/ppermute | solution.py:108
